TPU v7x, 32 devices: a whole 2x2x4 slice. The times are simulated.
32 devices in a mesh: groups: 2 (over y), pages: 4 (over z), patches: 4 (over x, core).
Axes of the slice: x: 2, y: 2, z: 4, core: 2. Of those that a mesh axis runs over, the one named last changes fastest.
Arguments:
- queries: bfloat16 [16, 32, 128], P(('groups', 'pages'), 'patches'), parts along dimension 0, may hold values from -6 to 6
- gallery: bfloat16 [640, 1024, 128], P(('groups', 'pages'), 'patches'), parts along dimension 0, may hold values from -0.5 to 0.5
- page_rows: int32 [640], P('groups'), parts along dimension 0, may hold values from 0 to 319, as said below
- candidates: int32 [16, 32], P(('groups', 'pages')), parts along dimension 0, may hold values from 0 to 319, as said below
Outputs:
- scores: float32 [16, 32], P(('groups', 'pages')), parts along dimension 0
There are 2 independent parts, one for each index of `groups`. A program takes and returns all parts, laid end to end along the dimension named above; each array names one. Nothing has to cross between parts.
Inputs may be any that keep to these rules, and one draw needn't show every extreme that they name: A permutation: page id c is stored at row page_rows[c] of gallery, which lies on pages index page_rows[c] // 80. Each query's 32 page ids are distinct. The 2 queries of one pages index have at most 48 candidates stored on one pages index, and in every draw some pages index stores exactly 48 candidates of the queries of every pages index.
All inputs are finite; a program needn't handle non-finite values.
Results may differ from a plain program's by a relative error of at most 0.0003.
Values may be sent and summed in bfloat16 or wider, within the bound.
No kernel may reach another device: no remote copies, remote signals or barrier semaphores. Data moves between devices by JAX's collectives and lax.ppermute only.
A program may use at most 64 MiB of HBM per device.

v0:
```python
import jax
import jax.numpy as jnp
from jax import lax
from jax.sharding import PartitionSpec as P

QT = 32
CAP = 48


def token_maxima(query_rows, gallery):
    page_count = gallery.shape[0]
    grouped = gallery.reshape(page_count // 8, 8, gallery.shape[1], gallery.shape[2])

    def per_block(block):
        sims = jnp.einsum("rd,bpd->brp", query_rows, block, preferred_element_type=jnp.float32)
        return jnp.max(sims, axis=2)

    result = lax.map(per_block, grouped)
    return result.reshape(page_count, query_rows.shape[0])


def slot_plan(storage, page_count, owner_count, query_count):
    flat_rows = storage.reshape(-1)
    holder = flat_rows // page_count
    local_page = flat_rows % page_count
    onehot = (holder[:, None] == jnp.arange(owner_count, dtype=jnp.int32)[None, :]).astype(
        jnp.int32
    )
    running = jnp.cumsum(onehot, axis=0) - onehot
    rank = jnp.sum(running * onehot, axis=1)
    query_ids = (
        lax.axis_index("pages") * query_count + jnp.arange(query_count, dtype=jnp.int32)[:, None]
    )
    query_ids = jnp.broadcast_to(query_ids, storage.shape).reshape(-1)
    codes = (
        jnp.full((owner_count, CAP), -1, jnp.int32)
        .at[holder, rank]
        .set(query_ids * page_count + local_page)
    )
    return (holder, rank, codes)


def body(queries, gallery, page_rows, candidates):
    query_count = queries.shape[0]
    page_count = gallery.shape[0]
    owner_count = lax.axis_size("pages")
    storage = jnp.take(page_rows, candidates, axis=0)
    local_tokens = lax.all_gather(queries, "patches", axis=1, tiled=True)
    shard_rows = lax.all_gather(local_tokens, "pages", axis=0, tiled=True)
    maxima = token_maxima(shard_rows.reshape(-1, shard_rows.shape[2]), gallery)
    part_count = lax.axis_size("patches")
    arrived = lax.all_to_all(maxima, "patches", split_axis=0, concat_axis=0, tiled=True)
    share_max = jnp.max(arrived.reshape(part_count, page_count // part_count, -1), axis=0)
    share_scores = jnp.mean(share_max.reshape(page_count // part_count, -1, QT), axis=2)
    page_scores = lax.all_gather(share_scores, "patches", axis=0, tiled=True)
    holder, rank, codes = slot_plan(storage, page_count, owner_count, query_count)
    incoming = lax.all_to_all(codes, "pages", split_axis=0, concat_axis=0, tiled=True)
    safe_codes = jnp.maximum(incoming, 0)
    picked = page_scores[safe_codes % page_count, safe_codes // page_count]
    picked = jnp.where(incoming >= 0, picked, 0.0)
    returned = lax.all_to_all(picked, "pages", split_axis=0, concat_axis=0, tiled=True)
    return returned[holder, rank].reshape(storage.shape)


def solution(mesh):
    in_specs = (
        P(("groups", "pages"), "patches", None),
        P(("groups", "pages"), "patches", None),
        P("groups"),
        P(("groups", "pages"), None),
    )
    out_specs = P(("groups", "pages"), None)
    return jax.shard_map(body, mesh=mesh, in_specs=in_specs, out_specs=out_specs, check_vma=False)
```

profile of v0, /device:TPU:0, one launch (start us, length us, event | category | flops | bytes accessed | tf_op | source)
XLA Modules:
  0.0 81.3 jit_solution(7018582230763072979)
XLA Ops:
  0.0 0.7 compare_select_fusion.3
  0.8 0.8 gather_fusion
  1.7 0.7 compare_and_fusion
  3.0 0.1 reduce_window_sum.11
  3.1 0.2 select_reduce_fusion
  3.2 0.1 and.53
  3.3 0.6 broadcast_in_dim.36
  3.9 10.2 %scatter_fusion = s32[4,48]{1,0:T(4,128)} fusion(s32[4,48]{1,0:T(4,128)} %broadcast_in_dim.36, s32[64]{0:T(128)S(1)} %get-tuple-element.42, s32[64]{0:T(128)S(1)} %get-tuple-element.45), kind=kCustom, calls=%fused_computation.3 | custom fusion | bytes 1280 | tf_op jit(solution)/shard_map/scatter | solution.py:38
  14.1 6.3 %all-to-all-start = ((s32[4,1,48]{2,1,0:T(1,128)}), s32[4,1,48]{2,1,0:T(1,128)S(1)}, u32[]{:S(2)}, u32[]{:S(2)}) async-start(s32[4,1,48]{2,1,0:T(1,128)} %bitcast.6), calls=%async_computation | async-start | bytes 4096 | tf_op jit(solution)/shard_map/all_to_all | solution.py:57
  20.5 5.4 %all_gather.9 = bf16[2,32,128]{2,1,0:T(8,128)(2,1)S(1)} all-gather(bf16[2,8,128]{2,1,0:T(8,128)(2,1)} %param.6), channel_id=1, replica_groups=mesh['groups'=2,'pages'=4,'patches'=4] {'patches'}, dimensions={1}, use_global_device_ids=true | all-gather | bytes 20480 | tf_op jit(solution)/shard_map/all_gather | solution.py:48
  25.9 13.7 %all_gather.10 = bf16[8,32,128]{2,1,0:T(8,128)(2,1)S(1)} all-gather(bf16[2,32,128]{2,1,0:T(8,128)(2,1)S(1)} %all_gather.9), channel_id=1, replica_groups=mesh['groups'=2,'pages'=4,'patches'=4] {'pages'}, dimensions={0}, use_global_device_ids=true | all-gather | bytes 81920 | tf_op jit(solution)/shard_map/all_gather | solution.py:49
  39.5 15.2 %while.10 = (s32[]{:T(128)}, f32[10,8,256]{2,1,0:T(8,128)S(1)}, bf16[10,8,256,128]{3,2,1,0:T(8,128)(2,1)}, bf16[256,128]{1,0:T(8,128)(2,1)S(1)}, s32[]{:T(128)}) while((s32[]{:T(128)}, f32[10,8,256]{2,1,0:T(8,128)S(1)}, bf16[10,8,256,128]{3,2,1,0:T(8,128)(2,1)}, bf16[256,128]{1,0:T(8,128)(2,1)S(1)}, s32[]{:T(128)}) %tuple.28), condition=%wide.region_5.6_spmd, body=%wide.region_3.5_spmd.sunk | while | flops 134739968 | bytes 614477 | solution.py:18
  39.5 1.5 %convolution_reduce_fusion.2 = f32[8,256]{1,0:T(8,128)S(1)} fusion(bf16[10,8,256,128]{3,2,1,0:T(8,128)(2,1)} %get-tuple-element.84, s32[]{:T(128)S(6)} %copy.20, bf16[256,128]{1,0:T(8,128)(2,1)S(1)} %get-tuple-element.85), kind=kOutput, calls=%fused_computation.4.clone.1 | convolution fusion | flops 134739968 | bytes 598020 | tf_op jit(solution)/shard_map/while/body/eval_jaxpr/rd,bpd->brp/dot_general | solution.py:15
  41.1 1.5 %convolution_reduce_fusion.2 = f32[8,256]{1,0:T(8,128)S(1)} fusion(bf16[10,8,256,128]{3,2,1,0:T(8,128)(2,1)} %get-tuple-element.84, s32[]{:T(128)S(6)} %copy.20, bf16[256,128]{1,0:T(8,128)(2,1)S(1)} %get-tuple-element.85), kind=kOutput, calls=%fused_computation.4.clone.1 | convolution fusion | flops 134739968 | bytes 598020 | tf_op jit(solution)/shard_map/while/body/eval_jaxpr/rd,bpd->brp/dot_general | solution.py:15
  42.6 1.5 %convolution_reduce_fusion.2 = f32[8,256]{1,0:T(8,128)S(1)} fusion(bf16[10,8,256,128]{3,2,1,0:T(8,128)(2,1)} %get-tuple-element.84, s32[]{:T(128)S(6)} %copy.20, bf16[256,128]{1,0:T(8,128)(2,1)S(1)} %get-tuple-element.85), kind=kOutput, calls=%fused_computation.4.clone.1 | convolution fusion | flops 134739968 | bytes 598020 | tf_op jit(solution)/shard_map/while/body/eval_jaxpr/rd,bpd->brp/dot_general | solution.py:15
  44.1 1.5 %convolution_reduce_fusion.2 = f32[8,256]{1,0:T(8,128)S(1)} fusion(bf16[10,8,256,128]{3,2,1,0:T(8,128)(2,1)} %get-tuple-element.84, s32[]{:T(128)S(6)} %copy.20, bf16[256,128]{1,0:T(8,128)(2,1)S(1)} %get-tuple-element.85), kind=kOutput, calls=%fused_computation.4.clone.1 | convolution fusion | flops 134739968 | bytes 598020 | tf_op jit(solution)/shard_map/while/body/eval_jaxpr/rd,bpd->brp/dot_general | solution.py:15
  45.6 1.5 %convolution_reduce_fusion.2 = f32[8,256]{1,0:T(8,128)S(1)} fusion(bf16[10,8,256,128]{3,2,1,0:T(8,128)(2,1)} %get-tuple-element.84, s32[]{:T(128)S(6)} %copy.20, bf16[256,128]{1,0:T(8,128)(2,1)S(1)} %get-tuple-element.85), kind=kOutput, calls=%fused_computation.4.clone.1 | convolution fusion | flops 134739968 | bytes 598020 | tf_op jit(solution)/shard_map/while/body/eval_jaxpr/rd,bpd->brp/dot_general | solution.py:15
  47.2 1.5 %convolution_reduce_fusion.2 = f32[8,256]{1,0:T(8,128)S(1)} fusion(bf16[10,8,256,128]{3,2,1,0:T(8,128)(2,1)} %get-tuple-element.84, s32[]{:T(128)S(6)} %copy.20, bf16[256,128]{1,0:T(8,128)(2,1)S(1)} %get-tuple-element.85), kind=kOutput, calls=%fused_computation.4.clone.1 | convolution fusion | flops 134739968 | bytes 598020 | tf_op jit(solution)/shard_map/while/body/eval_jaxpr/rd,bpd->brp/dot_general | solution.py:15
  48.7 1.5 %convolution_reduce_fusion.2 = f32[8,256]{1,0:T(8,128)S(1)} fusion(bf16[10,8,256,128]{3,2,1,0:T(8,128)(2,1)} %get-tuple-element.84, s32[]{:T(128)S(6)} %copy.20, bf16[256,128]{1,0:T(8,128)(2,1)S(1)} %get-tuple-element.85), kind=kOutput, calls=%fused_computation.4.clone.1 | convolution fusion | flops 134739968 | bytes 598020 | tf_op jit(solution)/shard_map/while/body/eval_jaxpr/rd,bpd->brp/dot_general | solution.py:15
  50.2 1.5 %convolution_reduce_fusion.2 = f32[8,256]{1,0:T(8,128)S(1)} fusion(bf16[10,8,256,128]{3,2,1,0:T(8,128)(2,1)} %get-tuple-element.84, s32[]{:T(128)S(6)} %copy.20, bf16[256,128]{1,0:T(8,128)(2,1)S(1)} %get-tuple-element.85), kind=kOutput, calls=%fused_computation.4.clone.1 | convolution fusion | flops 134739968 | bytes 598020 | tf_op jit(solution)/shard_map/while/body/eval_jaxpr/rd,bpd->brp/dot_general | solution.py:15
  51.7 1.5 %convolution_reduce_fusion.2 = f32[8,256]{1,0:T(8,128)S(1)} fusion(bf16[10,8,256,128]{3,2,1,0:T(8,128)(2,1)} %get-tuple-element.84, s32[]{:T(128)S(6)} %copy.20, bf16[256,128]{1,0:T(8,128)(2,1)S(1)} %get-tuple-element.85), kind=kOutput, calls=%fused_computation.4.clone.1 | convolution fusion | flops 134739968 | bytes 598020 | tf_op jit(solution)/shard_map/while/body/eval_jaxpr/rd,bpd->brp/dot_general | solution.py:15
  53.3 1.5 %convolution_reduce_fusion.2 = f32[8,256]{1,0:T(8,128)S(1)} fusion(bf16[10,8,256,128]{3,2,1,0:T(8,128)(2,1)} %get-tuple-element.84, s32[]{:T(128)S(6)} %copy.20, bf16[256,128]{1,0:T(8,128)(2,1)S(1)} %get-tuple-element.85), kind=kOutput, calls=%fused_computation.4.clone.1 | convolution fusion | flops 134739968 | bytes 598020 | tf_op jit(solution)/shard_map/while/body/eval_jaxpr/rd,bpd->brp/dot_general | solution.py:15
  54.8 0.6 all_to_all.20
  55.4 3.3 %all-to-all-start.1 = ((f32[4,20,256]{2,1,0:T(8,128)}), f32[4,20,256]{2,1,0:T(8,128)S(1)}, u32[]{:S(2)}, u32[]{:S(2)}) async-start(f32[4,20,256]{2,1,0:T(8,128)} %all_to_all.20), calls=%async_computation.1 | async-start | bytes 196608 | tf_op jit(solution)/shard_map/all_to_all | solution.py:52
  58.7 0.2 broadcast_maximum_fusion
  59.1 3.9 %all-to-all-done.1 = f32[4,20,256]{2,1,0:T(8,128)S(1)} async-done(((f32[4,20,256]{2,1,0:T(8,128)}), f32[4,20,256]{2,1,0:T(8,128)S(1)}, u32[]{:S(2)}, u32[]{:S(2)}) %all-to-all-start.1) | async-done | bytes 81952 | tf_op jit(solution)/shard_map/all_to_all | solution.py:52
  63.1 0.1 reduce_sum.22
  63.3 5.2 %all-gather = f32[4,20,8]{1,2,0:T(8,128)S(1)} all-gather(f32[1,20,8]{1,2,0:T(8,128)S(1)} %copy.12), channel_id=1, replica_groups=mesh['groups'=2,'pages'=4,'patches'=4] {'patches'}, dimensions={0}, use_global_device_ids=true | all-gather | bytes 3200 | tf_op jit(solution)/shard_map/all_gather | solution.py:55
  68.6 1.2 %gather_fusion.1 = f32[192]{0:T(256)S(1)} fusion(f32[80,8]{0,1:T(8,128)S(1)} %reshape.242, s32[192]{0:T(256)S(1)} %reshape.220), kind=kCustom, calls=%fused_computation.1 | custom fusion | bytes 3072 | tf_op jit(solution)/shard_map/gather | solution.py:59
  69.8 9.9 %all_to_all.27 = f32[4,1,48]{2,1,0:T(1,128)S(1)} all-to-all(f32[4,1,48]{2,1,0:T(1,128)S(1)} %compare_select_fusion), channel_id=1, replica_groups=mesh['groups'=2,'pages'=4,'patches'=4] {'pages'}, dimensions={0} | all-to-all | bytes 1536 | tf_op jit(solution)/shard_map/all_to_all | solution.py:61
  79.7 0.9 %gather_fusion.2 = f32[64]{0:T(128)S(1)} fusion(f32[4,48]{1,0:T(4,128)S(1)} %bitcast.60, s32[64]{0:T(128)S(1)} %get-tuple-element.41), kind=kCustom, calls=%fused_computation.2 | custom fusion | bytes 1024 | tf_op jit(solution)/shard_map/gather | solution.py:62
  80.6 0.6 reshape.211
  (39 shorter events, 1.3 us)
Async XLA Ops:
  0.0 0.8 copy-start
  14.1 41.3 %all-to-all-start = ((s32[4,1,48]{2,1,0:T(1,128)}), s32[4,1,48]{2,1,0:T(1,128)S(1)}, u32[]{:S(2)}, u32[]{:S(2)}) async-start(s32[4,1,48]{2,1,0:T(1,128)} %bitcast.6), calls=%async_computation | async-start | bytes 4096 | tf_op jit(solution)/shard_map/all_to_all | solution.py:57
  55.4 7.6 %all-to-all-start.1 = ((f32[4,20,256]{2,1,0:T(8,128)}), f32[4,20,256]{2,1,0:T(8,128)S(1)}, u32[]{:S(2)}, u32[]{:S(2)}) async-start(f32[4,20,256]{2,1,0:T(8,128)} %all_to_all.20), calls=%async_computation.1 | async-start | bytes 196608 | tf_op jit(solution)/shard_map/all_to_all | solution.py:52
where the time goes:
time: 82.3 us; the launch traced here: 81.3 us
  blocking collectives  34.2 us (42%)
  local copies, waits for them, and re-layouts  16.2 us (20%)
  matrix products  14.9 us (18%)
  starting transfers between devices  9.65 us (12%)
  waiting for transfers between devices  3.93 us (5%)
  other arithmetic  2.15 us (3%)
    dot_general x10, matrix products, per_block(): jnp.einsum('rd,bpd->brp', query_rows, block, preferred_element_type=jnp.f...  14.9 us
    all_gather x1, blocking collectives, body(): shard_rows = lax.all_gather(local_tokens, 'pages', axis=0, tiled=True)  13.7 us
    scatter x1, local copies, waits for them, and re-layouts, slot_plan(): codes = jnp.full((owner_count, CAP), -1, jnp.int32).at[holder, rank].set(...  10.2 us
    all_to_all x1, blocking collectives, body(): lax.all_to_all(picked, 'pages', split_axis=0, concat_axis=0, tiled=True)  9.92 us
    all_to_all x1, starting transfers between devices, body(): lax.all_to_all(codes, 'pages', split_axis=0, concat_axis=0, tiled=True)  6.35 us
    all_gather x1, blocking collectives, body(): local_tokens = lax.all_gather(queries, 'patches', axis=1, tiled=True)  5.37 us
    all_gather x1, blocking collectives, body(): page_scores = lax.all_gather(share_scores, 'patches', axis=0, tiled=True)  5.19 us
    all_to_all x1, waiting for transfers between devices, body(): lax.all_to_all(maxima, 'patches', split_axis=0, concat_axis=0, tiled=True)  3.93 us
  transfers between devices with their start and end apart: 2, of which 1 were waited for; matrix products, arithmetic and copies ran while one was open for 19% of the time, Pallas kernels for 0%

commit v1 on v0

v1 whole, which is shorter than its diff:
```python
import functools

import jax
import jax.numpy as jnp
from jax import lax
from jax.experimental import pallas as pl
from jax.experimental.pallas import tpu as pltpu
from jax.sharding import PartitionSpec as P

LANES = 128
BASE = 128
GROUP = ("pages", "patches")
VMEM = pl.BlockSpec(memory_space=pltpu.VMEM)


def lookup_kernel(candidates_ref, page_rows_ref, info_ref):
    queries, cand = candidates_ref.shape
    pages = page_rows_ref.shape[1]
    count = queries * cand
    repeat = max(1, LANES // count)
    blocks = count * repeat // LANES
    table = page_rows_ref[...].astype(jnp.float32)
    high = jnp.floor(table * (1.0 / BASE))
    low = table - high * BASE
    digits = jnp.concatenate([high, low, jnp.zeros((6, pages), jnp.float32)], axis=0)
    info_ref[...] = jnp.zeros_like(info_ref)
    found = []
    for q in range(queries):
        ids = candidates_ref[q : q + 1, :]
        hit = lax.broadcasted_iota(jnp.int32, (pages, cand), 0) == ids
        found.append(
            lax.dot_general(
                digits.astype(jnp.bfloat16),
                hit.astype(jnp.float32).astype(jnp.bfloat16),
                (((1,), (0,)), ((), ())),
                preferred_element_type=jnp.float32,
            )
        )
    line = jnp.concatenate(found * repeat, axis=1)
    for r in range(blocks):
        part = line[:, r * LANES : (r + 1) * LANES].astype(jnp.bfloat16)
        info_ref[r : r + 1, :] = part[0:1, :]
        info_ref[blocks + r : blocks + r + 1, :] = part[1:2, :]


def lookup(candidates, page_rows):
    return pl.pallas_call(
        lookup_kernel,
        out_shape=jax.ShapeDtypeStruct((16, LANES), jnp.bfloat16),
        in_specs=[VMEM, VMEM],
        out_specs=VMEM,
        compiler_params=pltpu.CompilerParams(vmem_limit_bytes=4 << 20),
        name="lookup",
    )(candidates, page_rows.reshape(1, -1))


def main_kernel(planes, parts, queries, cand, tokens, packed_ref, gallery_ref, out_ref, token_ref, best_ref):
    pages, patches, dim = gallery_ref.shape
    plane_rows = queries * tokens
    stride = plane_rows + 16
    count = queries * cand
    repeat = max(1, LANES // count)
    blocks = count * repeat // LANES
    held_tokens = tokens // repeat
    me = lax.axis_index("pages")
    for d in range(planes):
        token_ref[d * plane_rows : (d + 1) * plane_rows, :] = packed_ref[d * stride : d * stride + plane_rows, :]
    columns = planes * plane_rows
    step = min(columns, 256)

    def one_page(p, carry):
        patch = gallery_ref[p]
        for c in range(0, columns, step):
            sims = lax.dot_general(
                patch,
                token_ref[c : c + step, :],
                (((1,), (1,)), ((), ())),
                preferred_element_type=jnp.float32,
            )
            best_ref[pl.ds(p, 1), c : c + step] = jnp.max(sims, axis=0, keepdims=True)
        return carry

    lax.fori_loop(0, pages, one_page, 0, unroll=4 if columns == step else 1)

    lane = lax.broadcasted_iota(jnp.int32, (1, LANES), 1)
    for d in range(planes):
        dest = jnp.bitwise_xor(me, d)
        base = d * stride + plane_rows
        block = best_ref[:, d * plane_rows : (d + 1) * plane_rows]
        for r in range(blocks):
            high = packed_ref[base : base + 16, :].astype(jnp.float32)
            rows = (high[r : r + 1, :] * BASE + high[blocks + r : blocks + r + 1, :]).astype(jnp.int32)
            local = rows - me * pages
            held = (local >= 0) & (local < pages)
            pick = (lax.broadcasted_iota(jnp.int32, (pages, LANES), 0) == local).astype(jnp.float32)
            got = lax.dot_general(
                block,
                pick,
                (((0,), (0,)), ((), ())),
                precision=lax.Precision.HIGHEST,
                preferred_element_type=jnp.float32,
            )
            owner = ((r * LANES + lane) % count) // cand
            mine = got[0:tokens, :]
            for q in range(1, queries):
                mine = jnp.where(owner == q, got[q * tokens : (q + 1) * tokens, :], mine)
            mine = jnp.where(held, mine, -jnp.inf)
            line = mine[0:held_tokens, :]
            for k in range(1, repeat):
                line = jnp.where(lane // count == k, mine[k * held_tokens : (k + 1) * held_tokens, :], line)
            for j in range(parts):
                out_ref[dest * parts + j, r] = line


def finish_kernel(queries, cand, tokens, arrived_ref, scores_ref):
    count = queries * cand
    repeat = max(1, LANES // count)
    sources, blocks = arrived_ref.shape[:2]
    lines = []
    for r in range(blocks):
        best = arrived_ref[0, r]
        for s in range(1, sources):
            best = jnp.maximum(best, arrived_ref[s, r])
        total = jnp.sum(best, axis=0, keepdims=True)
        line = total[:, : LANES // repeat]
        for k in range(1, repeat):
            line = line + total[:, k * count : (k + 1) * count]
        lines.append(line)
    line = lines[0] if blocks == 1 else jnp.concatenate(lines, axis=1)
    for q in range(queries):
        scores_ref[q : q + 1, :] = line[:, q * cand : (q + 1) * cand] * (1.0 / tokens)


def body(queries, gallery, page_rows, candidates):
    planes = lax.axis_size("pages")
    parts = lax.axis_size("patches")
    everyone = planes * parts
    query_count, _, dim = queries.shape
    tokens = queries.shape[1] * parts
    cand = candidates.shape[1]
    count = query_count * cand
    repeat = max(1, LANES // count)
    blocks = count * repeat // LANES
    pages, patches, _ = gallery.shape
    here = lax.axis_index("patches")

    def swap(x, mask):
        return lax.ppermute(x, GROUP, [(i, i ^ mask) for i in range(everyone)])

    held = queries
    bit = 1
    while bit < parts:
        other = swap(held, bit if bit == 1 else bit | 1)
        upper = (here & bit) != 0
        first = jnp.where(upper, other, held)
        second = jnp.where(upper, held, other)
        held = jnp.concatenate([first, second], axis=1)
        bit *= 2
    info = lookup(candidates, page_rows)
    packed = jnp.concatenate([held.reshape(query_count * tokens, dim), info], axis=0)
    bit = 1
    while bit < planes:
        packed = jnp.concatenate([packed, swap(packed, (bit * parts) | 1)], axis=0)
        bit *= 2

    columns = planes * query_count * tokens
    message = (everyone, blocks, tokens // repeat, LANES)
    sent = pl.pallas_call(
        functools.partial(main_kernel, planes, parts, query_count, cand, tokens),
        out_shape=jax.ShapeDtypeStruct(message, jnp.float32),
        in_specs=[VMEM, VMEM],
        out_specs=VMEM,
        scratch_shapes=[
            pltpu.VMEM((columns, dim), jnp.bfloat16),
            pltpu.VMEM((pages, columns), jnp.float32),
        ],
        compiler_params=pltpu.CompilerParams(vmem_limit_bytes=40 << 20),
        name="maxima",
    )(packed, gallery)
    arrived = lax.all_to_all(sent, GROUP, split_axis=0, concat_axis=0, tiled=True)
    return pl.pallas_call(
        functools.partial(finish_kernel, query_count, cand, tokens),
        out_shape=jax.ShapeDtypeStruct((query_count, cand), jnp.float32),
        in_specs=[VMEM],
        out_specs=VMEM,
        compiler_params=pltpu.CompilerParams(vmem_limit_bytes=40 << 20),
        name="finish",
    )(arrived)


def solution(mesh):
    in_specs = (
        P(("groups", "pages"), "patches", None),
        P(("groups", "pages"), "patches", None),
        P("groups"),
        P(("groups", "pages"), None),
    )
    out_specs = P(("groups", "pages"), None)
    return jax.shard_map(body, mesh=mesh, in_specs=in_specs, out_specs=out_specs, check_vma=False)
```

time: 82.3 us -> 39.2 us (0.48)
  blocking collectives: 34.2 us -> 15 us
  matrix products: 14.9 us -> 0 us
  local copies, waits for them, and re-layouts: 16.2 us -> 3.84 us
  Pallas kernels: 0 us -> 7.58 us
  starting transfers between devices: 9.65 us -> 7.26 us
  other arithmetic: 2.15 us -> 0.73 us
    all_gather x3 -> x0, blocking collectives: 24.2 us -> none  [the longest x1 13.7 us: body(): shard_rows = lax.all_gather(local_tokens, 'pages', axis=0, tiled=True)]
    dot_general x10 -> x0, matrix products: 14.9 us -> none  [per_block(): jnp.einsum('rd,bpd->brp', query_rows, block, preferred_element_type=jnp.f...]
    scatter x1 -> x0, local copies, waits for them, and re-layouts: 10.2 us -> none  [slot_plan(): codes = jnp.full((owner_count, CAP), -1, jnp.int32).at[holder, rank].set(...]
    all_to_all x2 -> x0, starting transfers between devices: 9.65 us -> none  [the longest x1 6.35 us: body(): lax.all_to_all(codes, 'pages', split_axis=0, concat_axis=0, tiled=True)]
    pallas_call x0 -> x3, Pallas kernels: none -> 7.58 us  [the longest x1 6.64 us: body(): pl.pallas_call(functools.partial(main_kernel, planes, parts, query_count,...]
    ppermute x0 -> x4, starting transfers between devices: none -> 7.26 us  [swap(): return lax.ppermute(x, GROUP, [(i, i ^ mask) for i in range(everyone)])]
    all_to_all x1, blocking collectives: 9.92 us -> 15 us  [body(): lax.all_to_all(sent, GROUP, split_axis=0, concat_axis=0, tiled=True)]
    ppermute x0 -> x4, waiting for transfers between devices: none -> 4.46 us  [swap(): return lax.ppermute(x, GROUP, [(i, i ^ mask) for i in range(everyone)])]
  transfers between devices with their start and end apart: 2 -> 4, of which waited for: 1 -> 3; matrix products, arithmetic and copies ran while one was open for 19% -> 2% of each run, Pallas kernels for 0% -> 1%
where the time goes in v1:
time: 39.2 us; the launch traced here: 38.9 us
  blocking collectives  15 us (38%)
  Pallas kernels  7.58 us (19%)
  starting transfers between devices  7.26 us (19%)
  waiting for transfers between devices  4.46 us (11%)
  local copies, waits for them, and re-layouts  3.84 us (10%)
  other arithmetic  0.73 us (2%)
    all_to_all x1, blocking collectives, body(): lax.all_to_all(sent, GROUP, split_axis=0, concat_axis=0, tiled=True)  15 us
    ppermute x4, starting transfers between devices, swap(): return lax.ppermute(x, GROUP, [(i, i ^ mask) for i in range(everyone)])  7.26 us
    pallas_call x1, Pallas kernels, body(): pl.pallas_call(functools.partial(main_kernel, planes, parts, query_count,...  6.64 us
    ppermute x4, waiting for transfers between devices, swap(): return lax.ppermute(x, GROUP, [(i, i ^ mask) for i in range(everyone)])  4.46 us
    unnamed x4, local copies, waits for them, and re-layouts  3.16 us
  transfers between devices with their start and end apart: 4, of which 3 were waited for; matrix products, arithmetic and copies ran while one was open for 2% of the time, Pallas kernels for 1%

profile of v1, /device:TPU:0, one launch (start us, length us, event | category | flops | bytes accessed | tf_op | source)
XLA Modules:
  0.0 38.9 jit_solution(12662878287385990963)
XLA Ops:
  0.0 0.5 %collective-permute-start = (bf16[2,8,128]{2,1,0:T(8,128)(2,1)}, bf16[2,8,128]{2,1,0:T(8,128)(2,1)S(1)}, u32[]{:S(2)}, u32[]{:S(2)}) collective-permute-start(bf16[2,8,128]{2,1,0:T(8,128)(2,1)} %param.4), channel_id=1, source_target_pairs={{0,1},{1,0},{2,3},{3,2},{4,5},{5,4},{6,7},{7,6},{8,9},{9,8},{10,11... | collective-permute-start | bytes 12296 | tf_op jit(solution)/shard_map/ppermute | solution.py:148
  0.5 1.0 %collective-permute-done = bf16[2,8,128]{2,1,0:T(8,128)(2,1)S(1)} collective-permute-done((bf16[2,8,128]{2,1,0:T(8,128)(2,1)}, bf16[2,8,128]{2,1,0:T(8,128)(2,1)S(1)}, u32[]{:S(2)}, u32[]{:S(2)}) %collective-permute-start) | collective-permute-done | bytes 4128 | tf_op jit(solution)/shard_map/ppermute | solution.py:148
  1.5 0.7 %broadcast_select_fusion.3 = (bf16[2,8,128]{2,1,0:T(8,128)(2,1)S(1)}, bf16[2,8,128]{2,1,0:T(8,128)(2,1)S(1)}) fusion(bf16[2,8,128]{2,1,0:T(8,128)(2,1)S(1)} %collective-permute-done, bf16[2,8,128]{2,1,0:T(8,128)(2,1)} %param.4, pred[]{:T(512)S(6)} %ne.7), kind=kLoop, calls=%fused_computation.8 | loop fusion | flops 4096 | bytes 16385 | tf_op jit(solution)/shard_map/jit(_where)/select_n | solution.py:155
  2.2 2.6 %collective-permute-start.1 = (bf16[2,16,128]{2,1,0:T(8,128)(2,1)S(1)}, bf16[2,16,128]{2,1,0:T(8,128)(2,1)S(1)}, u32[]{:S(2)}, u32[]{:S(2)}) collective-permute-start(bf16[2,16,128]{2,1,0:T(8,128)(2,1)S(1)} %pad_maximum_fusion.4), channel_id=1, source_target_pairs={{0,3},{1,2},{2,1},{3,0},{4,7},{5,6},{6,5},{7,4},{8,11},{9,10},{10,... | collective-permute-start | bytes 24584 | tf_op jit(solution)/shard_map/ppermute | solution.py:148
  4.8 0.7 %reshape.7.page_rows_ref = s32[1,320]{1,0:T(1,128)S(1)} reshape(s32[320]{0:T(512)} %param.6) | data formatting | bytes 2560 | tf_op jit(solution)/shard_map/reshape | solution.py:54
  5.5 0.0 copy-start.1
  5.5 0.7 %copy-done.1 = s32[2,32]{1,0:T(2,128)S(1)} copy-done((s32[2,32]{1,0:T(2,128)S(1)}, s32[2,32]{1,0:T(2,128)}, u32[]{:S(2)}) %copy-start.1) | copy-done | bytes 280
  6.2 0.2 lookup.1
  6.4 0.0 collective-permute-done.1
  6.5 1.6 %collective-permute-start.2 = (bf16[80,128]{1,0:T(8,128)(2,1)S(1)}, bf16[80,128]{1,0:T(8,128)(2,1)S(1)}, u32[]{:S(2)}, u32[]{:S(2)}) collective-permute-start(bf16[80,128]{1,0:T(8,128)(2,1)S(1)} %pad_maximum_fusion.2), channel_id=1, source_target_pairs={{0,5},{1,4},{2,7},{3,6},{4,1},{5,0},{6,3},{7,2},{8,13},{9,12},{10,... | collective-permute-start | bytes 61448 | tf_op jit(solution)/shard_map/ppermute | solution.py:148
  8.1 1.7 %collective-permute-done.2 = bf16[80,128]{1,0:T(8,128)(2,1)S(1)} collective-permute-done((bf16[80,128]{1,0:T(8,128)(2,1)S(1)}, bf16[80,128]{1,0:T(8,128)(2,1)S(1)}, u32[]{:S(2)}, u32[]{:S(2)}) %collective-permute-start.2) | collective-permute-done | bytes 20512 | tf_op jit(solution)/shard_map/ppermute | solution.py:148
  9.7 2.6 %collective-permute-start.3 = (bf16[160,128]{1,0:T(8,128)(2,1)S(1)}, bf16[160,128]{1,0:T(8,128)(2,1)S(1)}, u32[]{:S(2)}, u32[]{:S(2)}) collective-permute-start(bf16[160,128]{1,0:T(8,128)(2,1)S(1)} %pad_maximum_fusion.1), channel_id=1, source_target_pairs={{0,9},{1,8},{2,11},{3,10},{4,13},{5,12},{6,15},{7,14},{8,1},{9,0},... | collective-permute-start | bytes 122888 | tf_op jit(solution)/shard_map/ppermute | solution.py:148
  12.3 1.8 %collective-permute-done.3 = bf16[160,128]{1,0:T(8,128)(2,1)S(1)} collective-permute-done((bf16[160,128]{1,0:T(8,128)(2,1)S(1)}, bf16[160,128]{1,0:T(8,128)(2,1)S(1)}, u32[]{:S(2)}, u32[]{:S(2)}) %collective-permute-start.3) | collective-permute-done | bytes 40992 | tf_op jit(solution)/shard_map/ppermute | solution.py:148
  14.1 0.0 copy-start
  14.1 2.5 %copy-done = bf16[80,256,128]{2,1,0:T(8,128)(2,1)S(1)} copy-done((bf16[80,256,128]{2,1,0:T(8,128)(2,1)S(1)}, bf16[80,256,128]{2,1,0:T(8,128)(2,1)}, u32[]{:S(2)}) %copy-start) | copy-done | bytes 5242904
  16.6 6.6 %maxima.1 = f32[16,1,16,128]{3,2,1,0:T(8,128)S(1)} custom-call(bf16[320,128]{1,0:T(8,128)(2,1)S(1)} %pad_maximum_fusion.packed_ref, bf16[80,256,128]{2,1,0:T(8,128)(2,1)S(1)} %copy-done), custom_call_target="tpu_custom_call" | custom-call | tf_op jit(solution)/shard_map/maxima/pallas_call | solution.py:168
  23.2 15.0 %all_to_all.5.arrived_ref = f32[16,1,16,128]{3,2,1,0:T(8,128)S(1)} all-to-all(f32[16,1,16,128]{3,2,1,0:T(8,128)S(1)} %maxima.1), channel_id=1, replica_groups=mesh['groups'=2,'pages'=4,'patches'=4] {'pages','patches'}, dimensions={0} | all-to-all | bytes 262144 | tf_op jit(solution)/shard_map/all_to_all | solution.py:180
  38.2 0.7 %finish.1 = f32[2,32]{1,0:T(2,128)} custom-call(f32[16,1,16,128]{3,2,1,0:T(8,128)S(1)} %all_to_all.5.arrived_ref), custom_call_target="tpu_custom_call" | custom-call | tf_op jit(solution)/shard_map/finish/pallas_call | solution.py:181
  (6 shorter events, 0.0 us)
Async XLA Ops:
  0.0 1.5 %collective-permute-start = (bf16[2,8,128]{2,1,0:T(8,128)(2,1)}, bf16[2,8,128]{2,1,0:T(8,128)(2,1)S(1)}, u32[]{:S(2)}, u32[]{:S(2)}) collective-permute-start(bf16[2,8,128]{2,1,0:T(8,128)(2,1)} %param.4), channel_id=1, source_target_pairs={{0,1},{1,0},{2,3},{3,2},{4,5},{5,4},{6,7},{7,6},{8,9},{9,8},{10,11... | collective-permute-start | bytes 12296 | tf_op jit(solution)/shard_map/ppermute | solution.py:148
  2.2 4.2 %collective-permute-start.1 = (bf16[2,16,128]{2,1,0:T(8,128)(2,1)S(1)}, bf16[2,16,128]{2,1,0:T(8,128)(2,1)S(1)}, u32[]{:S(2)}, u32[]{:S(2)}) collective-permute-start(bf16[2,16,128]{2,1,0:T(8,128)(2,1)S(1)} %pad_maximum_fusion.4), channel_id=1, source_target_pairs={{0,3},{1,2},{2,1},{3,0},{4,7},{5,6},{6,5},{7,4},{8,11},{9,10},{10,... | collective-permute-start | bytes 24584 | tf_op jit(solution)/shard_map/ppermute | solution.py:148
  5.5 0.7 %copy-start.1 = (s32[2,32]{1,0:T(2,128)S(1)}, s32[2,32]{1,0:T(2,128)}, u32[]{:S(2)}) copy-start(s32[2,32]{1,0:T(2,128)} %candidates_ref.1) | copy-start | bytes 772
  6.5 3.3 %collective-permute-start.2 = (bf16[80,128]{1,0:T(8,128)(2,1)S(1)}, bf16[80,128]{1,0:T(8,128)(2,1)S(1)}, u32[]{:S(2)}, u32[]{:S(2)}) collective-permute-start(bf16[80,128]{1,0:T(8,128)(2,1)S(1)} %pad_maximum_fusion.2), channel_id=1, source_target_pairs={{0,5},{1,4},{2,7},{3,6},{4,1},{5,0},{6,3},{7,2},{8,13},{9,12},{10,... | collective-permute-start | bytes 61448 | tf_op jit(solution)/shard_map/ppermute | solution.py:148
  9.7 4.3 %collective-permute-start.3 = (bf16[160,128]{1,0:T(8,128)(2,1)S(1)}, bf16[160,128]{1,0:T(8,128)(2,1)S(1)}, u32[]{:S(2)}, u32[]{:S(2)}) collective-permute-start(bf16[160,128]{1,0:T(8,128)(2,1)S(1)} %pad_maximum_fusion.1), channel_id=1, source_target_pairs={{0,9},{1,8},{2,11},{3,10},{4,13},{5,12},{6,15},{7,14},{8,1},{9,0},... | collective-permute-start | bytes 122888 | tf_op jit(solution)/shard_map/ppermute | solution.py:148
  14.1 2.5 %copy-start = (bf16[80,256,128]{2,1,0:T(8,128)(2,1)S(1)}, bf16[80,256,128]{2,1,0:T(8,128)(2,1)}, u32[]{:S(2)}) copy-start(bf16[80,256,128]{2,1,0:T(8,128)(2,1)} %gallery_ref.1) | copy-start | bytes 15728644

commit v2 on v1

v2 whole, which is shorter than its diff:
```python
import functools

import jax
import jax.numpy as jnp
from jax import lax
from jax.experimental import pallas as pl
from jax.experimental.pallas import tpu as pltpu
from jax.sharding import PartitionSpec as P

LANES = 128
SUBLANES = 8
BASE = 128
INFO = 8
GROUP_PAGES = 16
LOADS = 4
GROUP = ("pages", "patches")
VMEM = pl.BlockSpec(memory_space=pltpu.VMEM)
HBM = pl.BlockSpec(memory_space=pltpu.HBM)


def sizes(queries, cand):
    count = queries * cand
    repeat = max(1, LANES // count)
    return count, repeat, count * repeat // LANES


def start_kernel(candidates_hbm, page_rows_hbm, tokens_hbm, info_ref, tokens_ref, candidates_ref, page_rows_ref, sems):
    copies = [
        pltpu.make_async_copy(page_rows_hbm, page_rows_ref, sems.at[0]),
        pltpu.make_async_copy(candidates_hbm, candidates_ref, sems.at[1]),
        pltpu.make_async_copy(tokens_hbm, tokens_ref, sems.at[2]),
    ]
    for copy in copies:
        copy.start()
    for copy in copies:
        copy.wait()
    queries, cand = candidates_ref.shape
    pages = page_rows_ref.shape[0]
    _, repeat, blocks = sizes(queries, cand)
    table = page_rows_ref[...].reshape(1, pages).astype(jnp.float32)
    high = jnp.floor(table * (1.0 / BASE))
    low = table - high * BASE
    digits = jnp.concatenate([high, low, jnp.zeros((6, pages), jnp.float32)], axis=0)
    found = []
    for q in range(queries):
        ids = candidates_ref[q : q + 1, :]
        hit = lax.broadcasted_iota(jnp.int32, (pages, cand), 0) == ids
        found.append(
            lax.dot_general(
                digits.astype(jnp.bfloat16),
                hit.astype(jnp.float32).astype(jnp.bfloat16),
                (((1,), (0,)), ((), ())),
                preferred_element_type=jnp.float32,
            )
        )
    line = jnp.concatenate(found * repeat, axis=1)
    rows = [line[0:1, r * LANES : (r + 1) * LANES] for r in range(blocks)]
    rows += [line[1:2, r * LANES : (r + 1) * LANES] for r in range(blocks)]
    if 2 * blocks < INFO:
        rows.append(jnp.zeros((INFO - 2 * blocks, LANES), jnp.float32))
    info_ref[...] = jnp.concatenate(rows, axis=0).astype(jnp.bfloat16)


def in_hbm(x):
    return pltpu.with_memory_space_constraint(x, pltpu.HBM)


def start(candidates, page_rows, tokens):
    return pl.pallas_call(
        start_kernel,
        out_shape=(jax.ShapeDtypeStruct((INFO, LANES), jnp.bfloat16), jax.ShapeDtypeStruct(tokens.shape, tokens.dtype)),
        in_specs=[HBM, HBM, HBM],
        out_specs=(VMEM, VMEM),
        scratch_shapes=[
            pltpu.VMEM(candidates.shape, jnp.int32),
            pltpu.VMEM(page_rows.shape, jnp.int32),
            pltpu.SemaphoreType.DMA((3,)),
        ],
        compiler_params=pltpu.CompilerParams(vmem_limit_bytes=8 << 20),
        cost_estimate=pl.CostEstimate(flops=1 << 20, transcendentals=0, bytes_accessed=1 << 20),
        name="start",
    )(in_hbm(candidates), in_hbm(page_rows), in_hbm(tokens))


def load_kernel(first, gallery_hbm, out_ref, sems):
    share = out_ref.shape[0] // LOADS
    copies = [
        pltpu.make_async_copy(
            gallery_hbm.at[pl.ds(first + i * share, share)], out_ref.at[pl.ds(i * share, share)], sems.at[i]
        )
        for i in range(LOADS)
    ]
    for copy in copies:
        copy.start()
    for copy in copies:
        copy.wait()


def load(gallery, first, count):
    shape = (count, *gallery.shape[1:])
    return pl.pallas_call(
        functools.partial(load_kernel, first),
        out_shape=jax.ShapeDtypeStruct(shape, gallery.dtype),
        in_specs=[HBM],
        out_specs=VMEM,
        scratch_shapes=[pltpu.SemaphoreType.DMA((LOADS,))],
        cost_estimate=pl.CostEstimate(
            flops=0, transcendentals=0, bytes_accessed=4 * count * gallery.shape[1] * gallery.shape[2]
        ),
        compiler_params=pltpu.CompilerParams(vmem_limit_bytes=8 << 20),
        name="load",
    )(in_hbm(gallery))


def main_kernel(queries, cand, order, shift, packed_ref, *refs):
    *gallery_refs, out_ref, token_ref, best_ref = refs
    patches, dim = gallery_refs[0].shape[1:]
    pages = best_ref.shape[0]
    columns = token_ref.shape[0]
    pieces = len(order[0])
    planes = len(order)
    plane_rows = columns // planes
    piece_rows = plane_rows // pieces
    unit = plane_rows + INFO
    each = piece_rows // queries
    tokens = each * pieces
    count, repeat, blocks = sizes(queries, cand)
    held_tokens = tokens // repeat
    here = lax.shift_right_logical(lax.axis_index("patches"), shift)
    for d in range(planes):
        for i, flip in enumerate(order[d]):
            at = d * plane_rows + jnp.bitwise_xor(here, flip) * piece_rows
            start = d * unit + i * piece_rows
            token_ref[pl.ds(pl.multiple_of(at, piece_rows), piece_rows), :] = packed_ref[start : start + piece_rows, :]

    width = min(columns, 256)

    def some_pages(gallery_ref, begin, i, carry):
        at = pl.multiple_of(i * GROUP_PAGES, GROUP_PAGES)
        patch = gallery_ref[pl.ds(at, GROUP_PAGES)].reshape(GROUP_PAGES * patches, dim)
        for c in range(0, columns, width):
            sims = lax.dot_general(
                patch,
                token_ref[c : c + width, :],
                (((1,), (1,)), ((), ())),
                preferred_element_type=jnp.float32,
            )
            best_ref[pl.ds(begin + at, GROUP_PAGES), c : c + width] = jnp.max(
                sims.reshape(GROUP_PAGES, patches, width), axis=1
            )
        return carry

    begin = 0
    for ref in gallery_refs:
        lax.fori_loop(0, ref.shape[0] // GROUP_PAGES, functools.partial(some_pages, ref, begin), 0)
        begin += ref.shape[0]

    first = lax.axis_index("pages") * pages
    lane = lax.broadcasted_iota(jnp.int32, (1, LANES), 1)
    for d in range(planes):
        block = best_ref[:, d * plane_rows : (d + 1) * plane_rows]
        info = packed_ref[d * unit + plane_rows : (d + 1) * unit, :].astype(jnp.float32)
        for r in range(blocks):
            rows = (info[r : r + 1, :] * BASE + info[blocks + r : blocks + r + 1, :]).astype(jnp.int32)
            local = rows - first
            held = (local >= 0) & (local < pages)
            pick = (lax.broadcasted_iota(jnp.int32, (pages, LANES), 0) == local).astype(jnp.float32)
            got = lax.dot_general(
                block,
                pick,
                (((0,), (0,)), ((), ())),
                precision=lax.Precision.HIGHEST,
                preferred_element_type=jnp.float32,
            )
            owner = ((r * LANES + lane) % count) // cand
            parts = []
            for i in range(pieces):
                at = i * piece_rows
                mine = got[at : at + each, :]
                for q in range(1, queries):
                    mine = jnp.where(owner == q, got[at + q * each : at + (q + 1) * each, :], mine)
                parts.append(mine)
            mine = jnp.where(held, jnp.concatenate(parts, axis=0), -jnp.inf)
            line = mine[0:held_tokens, :]
            for k in range(1, repeat):
                line = jnp.where(lane // count == k, mine[k * held_tokens : (k + 1) * held_tokens, :], line)
            out_ref[d, r] = line


def finish_kernel(queries, cand, tokens, mine_ref, other_ref, scores_ref):
    count, repeat, blocks = sizes(queries, cand)
    lines = []
    for r in range(blocks):
        best = jnp.maximum(mine_ref[r], other_ref[r])
        total = jnp.sum(best, axis=0, keepdims=True)
        line = total[:, : LANES // repeat]
        for k in range(1, repeat):
            line = line + total[:, k * count : (k + 1) * count]
        lines.append(line)
    line = lines[0] if blocks == 1 else jnp.concatenate(lines, axis=1)
    for q in range(queries):
        scores_ref[q : q + 1, :] = line[:, q * cand : (q + 1) * cand] * (1.0 / tokens)


def body(queries, gallery, page_rows, candidates):
    planes = lax.axis_size("pages")
    parts = lax.axis_size("patches")
    everyone = planes * parts
    query_count, own_tokens, dim = queries.shape
    tokens = own_tokens * parts
    cand = candidates.shape[1]
    _, repeat, blocks = sizes(query_count, cand)
    pages, patches, _ = gallery.shape

    def swap(x, mask):
        return lax.ppermute(x, GROUP, [(i, i ^ mask) for i in range(everyone)])

    def mask_of(bit):
        return bit if bit == 1 else bit | 1

    info, own = start(candidates, page_rows, queries)
    parts_of_gallery = [load(gallery, 0, 32), load(gallery, 32, 48)]
    held, bit, shift = queries, 1, 0
    while held.shape[1] % SUBLANES and bit < parts:
        other = swap(held, mask_of(bit))
        upper = (lax.axis_index("patches") & bit) != 0
        held = jnp.concatenate([jnp.where(upper, other, held), jnp.where(upper, held, other)], axis=1)
        bit, shift = bit * 2, shift + 1
    packed = held.reshape(-1, dim)
    order = [0]
    while bit < parts:
        mask = mask_of(bit)
        packed = jnp.concatenate([own.reshape(packed.shape) if bit == 1 else packed, swap(packed, mask)], axis=0)
        order = order + [(mask >> shift) ^ flip for flip in order]
        bit *= 2
    packed = jnp.concatenate([packed, info], axis=0)
    order = [order]
    bit = 1
    while bit < planes:
        mask = (bit * parts) | 1
        packed = jnp.concatenate([packed, swap(packed, mask)], axis=0)
        order = order + [[((mask % parts) >> shift) ^ flip for flip in flips] for flips in order]
        bit *= 2

    columns = planes * query_count * tokens
    best = pl.pallas_call(
        functools.partial(main_kernel, query_count, cand, order, shift),
        out_shape=jax.ShapeDtypeStruct((planes, blocks, tokens // repeat, LANES), jnp.float32),
        in_specs=[VMEM] * (1 + len(parts_of_gallery)),
        out_specs=VMEM,
        scratch_shapes=[
            pltpu.VMEM((columns, dim), jnp.bfloat16),
            pltpu.VMEM((pages, columns), jnp.float32),
        ],
        compiler_params=pltpu.CompilerParams(vmem_limit_bytes=24 << 20),
        name="maxima",
    )(packed, *parts_of_gallery)
    while bit > 1:
        bit //= 2
        best = jnp.maximum(best[:bit], swap(best[bit:], (bit * parts) | 1))
    best = best[0]
    bit = parts // 2
    while bit > 1:
        best = jnp.maximum(best, swap(best, mask_of(bit)))
        bit //= 2
    return pl.pallas_call(
        functools.partial(finish_kernel, query_count, cand, tokens),
        out_shape=jax.ShapeDtypeStruct((query_count, cand), jnp.float32),
        in_specs=[VMEM, VMEM],
        out_specs=VMEM,
        compiler_params=pltpu.CompilerParams(vmem_limit_bytes=8 << 20),
        name="finish",
    )(best, swap(best, 1))


def solution(mesh):
    in_specs = (
        P(("groups", "pages"), "patches", None),
        P(("groups", "pages"), "patches", None),
        P("groups"),
        P(("groups", "pages"), None),
    )
    out_specs = P(("groups", "pages"), None)
    return jax.shard_map(body, mesh=mesh, in_specs=in_specs, out_specs=out_specs, check_vma=False)
```

time: 39.2 us -> 31.5 us (0.80)
  blocking collectives: 15 us -> 0 us
  waiting for transfers between devices: 4.46 us -> 10.1 us
  starting transfers between devices: 7.26 us -> 11.9 us
  local copies, waits for them, and re-layouts: 3.84 us -> 0.06 us
  Pallas kernels: 7.58 us -> 9.12 us
  other arithmetic: 0.73 us -> 0.02 us
    all_to_all x1 -> x0, blocking collectives: 15 us -> none  [body(): lax.all_to_all(sent, GROUP, split_axis=0, concat_axis=0, tiled=True)]
    ppermute x4 -> x8, waiting for transfers between devices: 4.46 us -> 10.1 us  [swap(): return lax.ppermute(x, GROUP, [(i, i ^ mask) for i in range(everyone)])]
    ppermute x4 -> x8, starting transfers between devices: 7.26 us -> 11.9 us  [swap(): return lax.ppermute(x, GROUP, [(i, i ^ mask) for i in range(everyone)])]
    unnamed x4, local copies, waits for them, and re-layouts: 3.16 us -> 0.03 us
    pallas_call x2 -> x4, Pallas kernels: 6.85 us -> 8.42 us  [the longest x1 4.02 us: body(): pl.pallas_call(functools.partial(main_kernel, query_count, cand, order, s...]
    select_n x2 -> x0, other arithmetic: 0.7 us -> none  [body(): first = jnp.where(upper, other, held)]
    reshape x1 -> x0, local copies, waits for them, and re-layouts: 0.68 us -> none  [lookup(): page_rows.reshape(1, -1)]
  transfers between devices with their start and end apart: 4 -> 8, of which waited for: 3 -> 6; matrix products, arithmetic and copies ran while one was open for 2% -> 0% of each run, Pallas kernels for 1% -> 14%
where the time goes in v2:
time: 31.5 us; the launch traced here: 31.3 us
  starting transfers between devices  11.9 us (38%)
  waiting for transfers between devices  10.1 us (32%)
  Pallas kernels  9.12 us (29%)
    ppermute x8, starting transfers between devices, swap(): return lax.ppermute(x, GROUP, [(i, i ^ mask) for i in range(everyone)])  11.9 us
    ppermute x8, waiting for transfers between devices, swap(): return lax.ppermute(x, GROUP, [(i, i ^ mask) for i in range(everyone)])  10.1 us
    pallas_call x1, Pallas kernels, body(): pl.pallas_call(functools.partial(main_kernel, query_count, cand, order, s...  4.02 us
    pallas_call x2, Pallas kernels, load(): pl.pallas_call(functools.partial(load_kernel, first), out_shape=jax.Shape...  3.43 us
    pallas_call x1, Pallas kernels, start(): pl.pallas_call(start_kernel, out_shape=(jax.ShapeDtypeStruct((INFO, LANES...  0.96 us
    pallas_call x1, Pallas kernels, body(): pl.pallas_call(functools.partial(finish_kernel, query_count, cand, tokens...  0.71 us
  transfers between devices with their start and end apart: 8, of which 6 were waited for; matrix products, arithmetic and copies ran while one was open for 0% of the time, Pallas kernels for 14%

profile of v2, /device:TPU:0, one launch (start us, length us, event | category | flops | bytes accessed | tf_op | source)
XLA Modules:
  0.0 31.3 jit_solution(2229000525514754852)
XLA Ops:
  0.0 0.5 %collective-permute-start = (bf16[16,128]{1,0:T(8,128)(2,1)}, bf16[16,128]{1,0:T(8,128)(2,1)S(1)}, u32[]{:S(2)}, u32[]{:S(2)}) collective-permute-start(bf16[16,128]{1,0:T(8,128)(2,1)} %bitcast.8), channel_id=1, source_target_pairs={{0,1},{1,0},{2,3},{3,2},{4,5},{5,4},{6,7},{7,6},{8,9},{9,8},{10,11... | collective-permute-start | bytes 12296 | tf_op jit(solution)/shard_map/ppermute | solution.py:216
  0.5 1.0 %start.1 = (bf16[8,128]{1,0:T(8,128)(2,1)S(1)}, bf16[2,8,128]{2,1,0:T(8,128)(2,1)S(1)}) custom-call(s32[2,32]{1,0:T(2,128)} %candidates_hbm.1, s32[320]{0:T(512)} %page_rows_hbm.1, bf16[2,8,128]{2,1,0:T(8,128)(2,1)} %tokens_hbm.1), custom_call_target="tpu_custom_call" | custom-call | flops 1048576 | bytes 1048576 | tf_op jit(solution)/shard_map/start/pallas_call | solution.py:69
  1.5 0.0 collective-permute-done
  1.5 2.6 %collective-permute-start.1 = (bf16[32,128]{1,0:T(8,128)(2,1)S(1)}, bf16[32,128]{1,0:T(8,128)(2,1)S(1)}, u32[]{:S(2)}, u32[]{:S(2)}) collective-permute-start(bf16[32,128]{1,0:T(8,128)(2,1)S(1)} %pad_maximum_fusion.1), channel_id=1, source_target_pairs={{0,3},{1,2},{2,1},{3,0},{4,7},{5,6},{6,5},{7,4},{8,11},{9,10},{10,... | collective-permute-start | bytes 24584 | tf_op jit(solution)/shard_map/ppermute | solution.py:216
  4.2 1.4 %collective-permute-done.1 = bf16[32,128]{1,0:T(8,128)(2,1)S(1)} collective-permute-done((bf16[32,128]{1,0:T(8,128)(2,1)S(1)}, bf16[32,128]{1,0:T(8,128)(2,1)S(1)}, u32[]{:S(2)}, u32[]{:S(2)}) %collective-permute-start.1) | collective-permute-done | bytes 8224 | tf_op jit(solution)/shard_map/ppermute | solution.py:216
  5.5 1.8 %collective-permute-start.2 = (bf16[72,128]{1,0:T(8,128)(2,1)S(1)}, bf16[72,128]{1,0:T(8,128)(2,1)S(1)}, u32[]{:S(2)}, u32[]{:S(2)}) collective-permute-start(bf16[72,128]{1,0:T(8,128)(2,1)S(1)} %pad_maximum_fusion), channel_id=1, source_target_pairs={{0,5},{1,4},{2,7},{3,6},{4,1},{5,0},{6,3},{7,2},{8,13},{9,12},{10,... | collective-permute-start | bytes 55304 | tf_op jit(solution)/shard_map/ppermute | solution.py:216
  7.3 1.4 %collective-permute-done.2 = bf16[72,128]{1,0:T(8,128)(2,1)S(1)} collective-permute-done((bf16[72,128]{1,0:T(8,128)(2,1)S(1)}, bf16[72,128]{1,0:T(8,128)(2,1)S(1)}, u32[]{:S(2)}, u32[]{:S(2)}) %collective-permute-start.2) | collective-permute-done | bytes 18464 | tf_op jit(solution)/shard_map/ppermute | solution.py:216
  8.8 2.8 %collective-permute-start.3 = (bf16[144,128]{1,0:T(8,128)(2,1)S(1)}, bf16[144,128]{1,0:T(8,128)(2,1)S(1)}, u32[]{:S(2)}, u32[]{:S(2)}) collective-permute-start(bf16[144,128]{1,0:T(8,128)(2,1)S(1)} %get-tuple-element.9), channel_id=1, source_target_pairs={{0,9},{1,8},{2,11},{3,10},{4,13},{5,12},{6,15},{7,14},{8,1},{9,0},... | collective-permute-start | bytes 110600 | tf_op jit(solution)/shard_map/ppermute | solution.py:216
  11.6 1.5 %load.2.refs_0_ = bf16[32,256,128]{2,1,0:T(8,128)(2,1)S(1)} custom-call(bf16[80,256,128]{2,1,0:T(8,128)(2,1)} %gallery_hbm.3), custom_call_target="tpu_custom_call" | custom-call | bytes 4194304 | tf_op jit(solution)/shard_map/load/pallas_call | solution.py:101
  13.2 1.9 %load.3.refs_1_ = bf16[48,256,128]{2,1,0:T(8,128)(2,1)S(1)} custom-call(bf16[80,256,128]{2,1,0:T(8,128)(2,1)} %gallery_hbm.3), custom_call_target="tpu_custom_call" | custom-call | bytes 6291456 | tf_op jit(solution)/shard_map/load/pallas_call | solution.py:101
  15.0 0.0 collective-permute-done.3
  15.1 4.0 %maxima.1 = f32[4,1,16,128]{3,2,1,0:T(8,128)S(1)} custom-call(bf16[288,128]{1,0:T(8,128)(2,1)S(1)} %constant_dynamic-update-slice_fusion.5.packed_ref, bf16[32,256,128]{2,1,0:T(8,128)(2,1)S(1)} %load.2.refs_0_, bf16[48,256,128]{2,1,0:T(8,128)(2,1)S(1)} %load.3.refs_1_), custom_call_target="tpu_custom_call" | custom-call | tf_op jit(solution)/shard_map/maxima/pallas_call | solution.py:246
  19.1 1.0 %collective-permute-start.4 = (f32[2,1,16,128]{3,2,1,0:T(8,128)S(1)}, f32[2,1,16,128]{3,2,1,0:T(8,128)S(1)}, u32[]{:S(2)}, u32[]{:S(2)}) collective-permute-start(f32[2,1,16,128]{3,2,1,0:T(8,128)S(1)} %slice.17), channel_id=1, source_target_pairs={{0,9},{1,8},{2,11},{3,10},{4,13},{5,12},{6,15},{7,14},{8,1},{9,0},... | collective-permute-start | bytes 49160 | tf_op jit(solution)/shard_map/ppermute | solution.py:216
  20.1 3.2 %collective-permute-done.4 = f32[2,1,16,128]{3,2,1,0:T(8,128)S(1)} collective-permute-done((f32[2,1,16,128]{3,2,1,0:T(8,128)S(1)}, f32[2,1,16,128]{3,2,1,0:T(8,128)S(1)}, u32[]{:S(2)}, u32[]{:S(2)}) %collective-permute-start.4) | collective-permute-done | bytes 16416 | tf_op jit(solution)/shard_map/ppermute | solution.py:216
  23.2 1.5 %collective-permute-start.5 = (f32[1,1,16,128]{3,2,1,0:T(8,128)S(1)}, f32[1,1,16,128]{3,2,1,0:T(8,128)S(1)}, u32[]{:S(2)}, u32[]{:S(2)}) collective-permute-start(f32[1,1,16,128]{3,2,1,0:T(8,128)S(1)} %slice.19), channel_id=1, source_target_pairs={{0,5},{1,4},{2,7},{3,6},{4,1},{5,0},{6,3},{7,2},{8,13},{9,12},{10,... | collective-permute-start | bytes 24584 | tf_op jit(solution)/shard_map/ppermute | solution.py:216
  24.7 1.6 %collective-permute-done.5 = f32[1,1,16,128]{3,2,1,0:T(8,128)S(1)} collective-permute-done((f32[1,1,16,128]{3,2,1,0:T(8,128)S(1)}, f32[1,1,16,128]{3,2,1,0:T(8,128)S(1)}, u32[]{:S(2)}, u32[]{:S(2)}) %collective-permute-start.5) | collective-permute-done | bytes 8224 | tf_op jit(solution)/shard_map/ppermute | solution.py:216
  26.3 1.4 %collective-permute-start.6 = (f32[1,16,128]{2,1,0:T(8,128)S(1)}, f32[1,16,128]{2,1,0:T(8,128)S(1)}, u32[]{:S(2)}, u32[]{:S(2)}) collective-permute-start(f32[1,16,128]{2,1,0:T(8,128)S(1)} %fusion), channel_id=1, source_target_pairs={{0,3},{1,2},{2,1},{3,0},{4,7},{5,6},{6,5},{7,4},{8,11},{9,10},{10,... | collective-permute-start | bytes 24584 | tf_op jit(solution)/shard_map/ppermute | solution.py:216
  27.7 1.7 %collective-permute-done.6 = f32[1,16,128]{2,1,0:T(8,128)S(1)} collective-permute-done((f32[1,16,128]{2,1,0:T(8,128)S(1)}, f32[1,16,128]{2,1,0:T(8,128)S(1)}, u32[]{:S(2)}, u32[]{:S(2)}) %collective-permute-start.6) | collective-permute-done | bytes 8224 | tf_op jit(solution)/shard_map/ppermute | solution.py:216
  29.4 0.3 %collective-permute-start.7 = (f32[1,16,128]{2,1,0:T(8,128)S(1)}, f32[1,16,128]{2,1,0:T(8,128)S(1)}, u32[]{:S(2)}, u32[]{:S(2)}) collective-permute-start(f32[1,16,128]{2,1,0:T(8,128)S(1)} %max.11.mine_ref), channel_id=1, source_target_pairs={{0,1},{1,0},{2,3},{3,2},{4,5},{5,4},{6,7},{7,6},{8,9},{9,8},{10,11... | collective-permute-start | bytes 24584 | tf_op jit(solution)/shard_map/ppermute | solution.py:216
  29.7 0.9 %collective-permute-done.7.other_ref = f32[1,16,128]{2,1,0:T(8,128)S(1)} collective-permute-done((f32[1,16,128]{2,1,0:T(8,128)S(1)}, f32[1,16,128]{2,1,0:T(8,128)S(1)}, u32[]{:S(2)}, u32[]{:S(2)}) %collective-permute-start.7) | collective-permute-done | bytes 8224 | tf_op jit(solution)/shard_map/ppermute | solution.py:216
  30.6 0.7 %finish.1 = f32[2,32]{1,0:T(2,128)} custom-call(f32[1,16,128]{2,1,0:T(8,128)S(1)} %max.11.mine_ref, f32[1,16,128]{2,1,0:T(8,128)S(1)} %collective-permute-done.7.other_ref), custom_call_target="tpu_custom_call" | custom-call | tf_op jit(solution)/shard_map/finish/pallas_call | solution.py:266
  (13 shorter events, 0.1 us)
Async XLA Ops:
  0.0 1.5 %collective-permute-start = (bf16[16,128]{1,0:T(8,128)(2,1)}, bf16[16,128]{1,0:T(8,128)(2,1)S(1)}, u32[]{:S(2)}, u32[]{:S(2)}) collective-permute-start(bf16[16,128]{1,0:T(8,128)(2,1)} %bitcast.8), channel_id=1, source_target_pairs={{0,1},{1,0},{2,3},{3,2},{4,5},{5,4},{6,7},{7,6},{8,9},{9,8},{10,11... | collective-permute-start | bytes 12296 | tf_op jit(solution)/shard_map/ppermute | solution.py:216
  1.5 4.0 %collective-permute-start.1 = (bf16[32,128]{1,0:T(8,128)(2,1)S(1)}, bf16[32,128]{1,0:T(8,128)(2,1)S(1)}, u32[]{:S(2)}, u32[]{:S(2)}) collective-permute-start(bf16[32,128]{1,0:T(8,128)(2,1)S(1)} %pad_maximum_fusion.1), channel_id=1, source_target_pairs={{0,3},{1,2},{2,1},{3,0},{4,7},{5,6},{6,5},{7,4},{8,11},{9,10},{10,... | collective-permute-start | bytes 24584 | tf_op jit(solution)/shard_map/ppermute | solution.py:216
  5.5 3.3 %collective-permute-start.2 = (bf16[72,128]{1,0:T(8,128)(2,1)S(1)}, bf16[72,128]{1,0:T(8,128)(2,1)S(1)}, u32[]{:S(2)}, u32[]{:S(2)}) collective-permute-start(bf16[72,128]{1,0:T(8,128)(2,1)S(1)} %pad_maximum_fusion), channel_id=1, source_target_pairs={{0,5},{1,4},{2,7},{3,6},{4,1},{5,0},{6,3},{7,2},{8,13},{9,12},{10,... | collective-permute-start | bytes 55304 | tf_op jit(solution)/shard_map/ppermute | solution.py:216
  8.8 6.2 %collective-permute-start.3 = (bf16[144,128]{1,0:T(8,128)(2,1)S(1)}, bf16[144,128]{1,0:T(8,128)(2,1)S(1)}, u32[]{:S(2)}, u32[]{:S(2)}) collective-permute-start(bf16[144,128]{1,0:T(8,128)(2,1)S(1)} %get-tuple-element.9), channel_id=1, source_target_pairs={{0,9},{1,8},{2,11},{3,10},{4,13},{5,12},{6,15},{7,14},{8,1},{9,0},... | collective-permute-start | bytes 110600 | tf_op jit(solution)/shard_map/ppermute | solution.py:216
  19.1 4.1 %collective-permute-start.4 = (f32[2,1,16,128]{3,2,1,0:T(8,128)S(1)}, f32[2,1,16,128]{3,2,1,0:T(8,128)S(1)}, u32[]{:S(2)}, u32[]{:S(2)}) collective-permute-start(f32[2,1,16,128]{3,2,1,0:T(8,128)S(1)} %slice.17), channel_id=1, source_target_pairs={{0,9},{1,8},{2,11},{3,10},{4,13},{5,12},{6,15},{7,14},{8,1},{9,0},... | collective-permute-start | bytes 49160 | tf_op jit(solution)/shard_map/ppermute | solution.py:216
  23.2 3.1 %collective-permute-start.5 = (f32[1,1,16,128]{3,2,1,0:T(8,128)S(1)}, f32[1,1,16,128]{3,2,1,0:T(8,128)S(1)}, u32[]{:S(2)}, u32[]{:S(2)}) collective-permute-start(f32[1,1,16,128]{3,2,1,0:T(8,128)S(1)} %slice.19), channel_id=1, source_target_pairs={{0,5},{1,4},{2,7},{3,6},{4,1},{5,0},{6,3},{7,2},{8,13},{9,12},{10,... | collective-permute-start | bytes 24584 | tf_op jit(solution)/shard_map/ppermute | solution.py:216
  26.3 3.1 %collective-permute-start.6 = (f32[1,16,128]{2,1,0:T(8,128)S(1)}, f32[1,16,128]{2,1,0:T(8,128)S(1)}, u32[]{:S(2)}, u32[]{:S(2)}) collective-permute-start(f32[1,16,128]{2,1,0:T(8,128)S(1)} %fusion), channel_id=1, source_target_pairs={{0,3},{1,2},{2,1},{3,0},{4,7},{5,6},{6,5},{7,4},{8,11},{9,10},{10,... | collective-permute-start | bytes 24584 | tf_op jit(solution)/shard_map/ppermute | solution.py:216
  29.4 1.2 %collective-permute-start.7 = (f32[1,16,128]{2,1,0:T(8,128)S(1)}, f32[1,16,128]{2,1,0:T(8,128)S(1)}, u32[]{:S(2)}, u32[]{:S(2)}) collective-permute-start(f32[1,16,128]{2,1,0:T(8,128)S(1)} %max.11.mine_ref), channel_id=1, source_target_pairs={{0,1},{1,0},{2,3},{3,2},{4,5},{5,4},{6,7},{7,6},{8,9},{9,8},{10,11... | collective-permute-start | bytes 24584 | tf_op jit(solution)/shard_map/ppermute | solution.py:216

commit v3 on v2

--- a/solution.py
+++ b/solution.py
@@ -13,6 +13,7 @@
 INFO = 8
 GROUP_PAGES = 16
 LOADS = 4
+LOAD_PAGES = 32
 GROUP = ("pages", "patches")
 VMEM = pl.BlockSpec(memory_space=pltpu.VMEM)
 HBM = pl.BlockSpec(memory_space=pltpu.HBM)
@@ -108,17 +109,23 @@
             flops=0, transcendentals=0, bytes_accessed=4 * count * gallery.shape[1] * gallery.shape[2]
         ),
         compiler_params=pltpu.CompilerParams(vmem_limit_bytes=8 << 20),
-        name="load",
     )(in_hbm(gallery))
 
 
-def main_kernel(queries, cand, order, shift, packed_ref, *refs):
-    *gallery_refs, out_ref, token_ref, best_ref = refs
-    patches, dim = gallery_refs[0].shape[1:]
-    pages = best_ref.shape[0]
-    columns = token_ref.shape[0]
+def main_kernel(queries, cand, order, shift, loaded, packed_ref, *refs):
+    *held_refs, gallery_hbm, out_ref, token_ref, best_ref, rest_ref, sems = refs
+    pages, patches, dim = gallery_hbm.shape
+    steps = rest_ref.shape[0] // GROUP_PAGES
+
+    def fetch(i):
+        source = gallery_hbm.at[pl.ds(loaded + i * GROUP_PAGES, GROUP_PAGES)]
+        return pltpu.make_async_copy(source, rest_ref.at[pl.ds(i * GROUP_PAGES, GROUP_PAGES)], sems.at[i])
+
+    for i in range(steps):
+        fetch(i).start()
     pieces = len(order[0])
     planes = len(order)
+    columns = best_ref.shape[1]
     plane_rows = columns // planes
     piece_rows = plane_rows // pieces
     unit = plane_rows + INFO
@@ -127,33 +134,50 @@
     count, repeat, blocks = sizes(queries, cand)
     held_tokens = tokens // repeat
     here = lax.shift_right_logical(lax.axis_index("patches"), shift)
+    double = token_ref.shape[1] // dim
+    if double == 2:
+        token_ref[...] = jnp.zeros_like(token_ref)
     for d in range(planes):
         for i, flip in enumerate(order[d]):
             at = d * plane_rows + jnp.bitwise_xor(here, flip) * piece_rows
             start = d * unit + i * piece_rows
-            token_ref[pl.ds(pl.multiple_of(at, piece_rows), piece_rows), :] = packed_ref[start : start + piece_rows, :]
+            piece = packed_ref[start : start + piece_rows, :]
+            for k in range(double):
+                rows = pl.ds(pl.multiple_of(at + k * columns, piece_rows), piece_rows)
+                token_ref[rows, k * dim : (k + 1) * dim] = piece
 
     width = min(columns, 256)
 
-    def some_pages(gallery_ref, begin, i, carry):
+    def some_pages(gallery_ref, begin, i):
         at = pl.multiple_of(i * GROUP_PAGES, GROUP_PAGES)
-        patch = gallery_ref[pl.ds(at, GROUP_PAGES)].reshape(GROUP_PAGES * patches, dim)
+        share = GROUP_PAGES // double
+        sides = [gallery_ref[pl.ds(at + k * share, share)].reshape(share * patches, dim) for k in range(double)]
+        patch = sides[0] if double == 1 else jnp.concatenate(sides, axis=1)
         for c in range(0, columns, width):
             sims = lax.dot_general(
                 patch,
-                token_ref[c : c + width, :],
+                token_ref[c : c + width * double, :],
                 (((1,), (1,)), ((), ())),
                 preferred_element_type=jnp.float32,
             )
-            best_ref[pl.ds(begin + at, GROUP_PAGES), c : c + width] = jnp.max(
-                sims.reshape(GROUP_PAGES, patches, width), axis=1
-            )
+            top = jnp.max(sims.reshape(share, patches, width * double), axis=1)
+            for k in range(double):
+                best_ref[pl.ds(begin + at + k * share, share), c : c + width] = top[:, k * width : (k + 1) * width]
+
+    def run(ref, begin, i, carry):
+        some_pages(ref, begin, i)
         return carry
 
+    def run_rest(i, carry):
+        fetch(i).wait()
+        some_pages(rest_ref, loaded, i)
+        return carry
+
     begin = 0
-    for ref in gallery_refs:
-        lax.fori_loop(0, ref.shape[0] // GROUP_PAGES, functools.partial(some_pages, ref, begin), 0)
+    for ref in held_refs:
+        lax.fori_loop(0, ref.shape[0] // GROUP_PAGES, functools.partial(run, ref, begin), 0)
         begin += ref.shape[0]
+    lax.fori_loop(0, steps, run_rest, 0)
 
     first = lax.axis_index("pages") * pages
     lane = lax.broadcasted_iota(jnp.int32, (1, LANES), 1)
@@ -219,7 +243,7 @@
         return bit if bit == 1 else bit | 1
 
     info, own = start(candidates, page_rows, queries)
-    parts_of_gallery = [load(gallery, 0, 32), load(gallery, 32, 48)]
+    loaded = [load(gallery, 0, LOAD_PAGES), load(gallery, LOAD_PAGES, LOAD_PAGES)]
     held, bit, shift = queries, 1, 0
     while held.shape[1] % SUBLANES and bit < parts:
         other = swap(held, mask_of(bit))
@@ -230,34 +254,53 @@
     order = [0]
     while bit < parts:
         mask = mask_of(bit)
-        packed = jnp.concatenate([own.reshape(packed.shape) if bit == 1 else packed, swap(packed, mask)], axis=0)
+        other = swap(packed, mask)
+        packed = jnp.concatenate([own.reshape(packed.shape) if bit == 1 else packed, other], axis=0)
         order = order + [(mask >> shift) ^ flip for flip in order]
         bit *= 2
     packed = jnp.concatenate([packed, info], axis=0)
     order = [order]
+
+    def maxima(packed, order):
+        columns = len(order) * query_count * tokens
+        double = 2 if columns <= 128 else 1
+        rest = pages - 2 * LOAD_PAGES
+        return pl.pallas_call(
+            functools.partial(main_kernel, query_count, cand, order, shift, 2 * LOAD_PAGES),
+            out_shape=jax.ShapeDtypeStruct((len(order), blocks, tokens // repeat, LANES), jnp.float32),
+            in_specs=[VMEM, VMEM, VMEM, HBM],
+            out_specs=VMEM,
+            scratch_shapes=[
+                pltpu.VMEM((columns * double, dim * double), jnp.bfloat16),
+                pltpu.VMEM((pages, columns), jnp.float32),
+                pltpu.VMEM((rest, patches, dim), jnp.bfloat16),
+                pltpu.SemaphoreType.DMA((rest // GROUP_PAGES,)),
+            ],
+            cost_estimate=pl.CostEstimate(
+                flops=2 * pages * patches * dim * columns, transcendentals=0, bytes_accessed=2 * gallery.size
+            ),
+            compiler_params=pltpu.CompilerParams(vmem_limit_bytes=24 << 20),
+        )(packed, *loaded, in_hbm(gallery))
+
     bit = 1
     while bit < planes:
         mask = (bit * parts) | 1
-        packed = jnp.concatenate([packed, swap(packed, mask)], axis=0)
-        order = order + [[((mask % parts) >> shift) ^ flip for flip in flips] for flips in order]
+        last = bit == planes // 2
+        other = swap(packed, mask)
+        flips = [[((mask % parts) >> shift) ^ flip for flip in flips] for flips in order]
+        if last:
+            near = maxima(packed, order)
+            far = maxima(other, flips)
+        else:
+            packed = jnp.concatenate([packed, other], axis=0)
+            order = order + flips
         bit *= 2
 
-    columns = planes * query_count * tokens
-    best = pl.pallas_call(
-        functools.partial(main_kernel, query_count, cand, order, shift),
-        out_shape=jax.ShapeDtypeStruct((planes, blocks, tokens // repeat, LANES), jnp.float32),
-        in_specs=[VMEM] * (1 + len(parts_of_gallery)),
-        out_specs=VMEM,
-        scratch_shapes=[
-            pltpu.VMEM((columns, dim), jnp.bfloat16),
-            pltpu.VMEM((pages, columns), jnp.float32),
-        ],
-        compiler_params=pltpu.CompilerParams(vmem_limit_bytes=24 << 20),
-        name="maxima",
-    )(packed, *parts_of_gallery)
     while bit > 1:
         bit //= 2
-        best = jnp.maximum(best[:bit], swap(best[bit:], (bit * parts) | 1))
+        arrived = swap(far, (bit * parts) | 1)
+        best = jnp.maximum(near, arrived)
+        near, far = best[: bit // 2], best[bit // 2 :]
     best = best[0]
     bit = parts // 2
     while bit > 1:

time: 31.5 us -> 30.6 us (0.971)
  waiting for transfers between devices: 10.1 us -> 7.21 us
  Pallas kernels: 9.12 us -> 10.4 us
  starting transfers between devices: 11.9 us -> 12.7 us
    ppermute x8, waiting for transfers between devices: 10.1 us -> 7.21 us  [swap(): return lax.ppermute(x, GROUP, [(i, i ^ mask) for i in range(everyone)])]
    pallas_call x1 -> x2, Pallas kernels: 4.02 us -> 5.58 us  [maxima(): pl.pallas_call(functools.partial(main_kernel, query_count, cand, order, s...]
    ppermute x8, starting transfers between devices: 11.9 us -> 12.7 us  [swap(): return lax.ppermute(x, GROUP, [(i, i ^ mask) for i in range(everyone)])]
    pallas_call x2, Pallas kernels: 3.43 us -> 3.1 us  [load(): pl.pallas_call(functools.partial(load_kernel, first), out_shape=jax.Shape...]
  transfers between devices with their start and end apart: 8 -> 8, of which waited for: 6 -> 6; matrix products, arithmetic and copies ran while one was open for 0% -> 0% of each run, Pallas kernels for 14% -> 23%
where the time goes in v3:
time: 30.6 us; the launch traced here: 30.4 us
  starting transfers between devices  12.7 us (42%)
  Pallas kernels  10.4 us (34%)
  waiting for transfers between devices  7.21 us (24%)
    ppermute x8, starting transfers between devices, swap(): return lax.ppermute(x, GROUP, [(i, i ^ mask) for i in range(everyone)])  12.7 us
    ppermute x8, waiting for transfers between devices, swap(): return lax.ppermute(x, GROUP, [(i, i ^ mask) for i in range(everyone)])  7.21 us
    pallas_call x2, Pallas kernels, maxima(): pl.pallas_call(functools.partial(main_kernel, query_count, cand, order, s...  5.58 us
    pallas_call x2, Pallas kernels, load(): pl.pallas_call(functools.partial(load_kernel, first), out_shape=jax.Shape...  3.1 us
    pallas_call x1, Pallas kernels, start(): pl.pallas_call(start_kernel, out_shape=(jax.ShapeDtypeStruct((INFO, LANES...  0.96 us
    pallas_call x1, Pallas kernels, body(): pl.pallas_call(functools.partial(finish_kernel, query_count, cand, tokens...  0.71 us
  transfers between devices with their start and end apart: 8, of which 6 were waited for; matrix products, arithmetic and copies ran while one was open for 0% of the time, Pallas kernels for 23%

profile of v3, /device:TPU:0, one launch (start us, length us, event | category | flops | bytes accessed | tf_op | source)
XLA Modules:
  0.0 30.4 jit_solution(13012533573781780851)
XLA Ops:
  0.0 0.5 %collective-permute-start = (bf16[16,128]{1,0:T(8,128)(2,1)}, bf16[16,128]{1,0:T(8,128)(2,1)S(1)}, u32[]{:S(2)}, u32[]{:S(2)}) collective-permute-start(bf16[16,128]{1,0:T(8,128)(2,1)} %bitcast.7), channel_id=1, source_target_pairs={{0,1},{1,0},{2,3},{3,2},{4,5},{5,4},{6,7},{7,6},{8,9},{9,8},{10,11... | collective-permute-start | bytes 12296 | tf_op jit(solution)/shard_map/ppermute | solution.py:240
  0.5 1.0 %start.1 = (bf16[8,128]{1,0:T(8,128)(2,1)S(1)}, bf16[2,8,128]{2,1,0:T(8,128)(2,1)S(1)}) custom-call(s32[2,32]{1,0:T(2,128)} %candidates_hbm.1, s32[320]{0:T(512)} %page_rows_hbm.1, bf16[2,8,128]{2,1,0:T(8,128)(2,1)} %tokens_hbm.1), custom_call_target="tpu_custom_call" | custom-call | flops 1048576 | bytes 1048576 | tf_op jit(solution)/shard_map/start/pallas_call | solution.py:70
  1.5 0.1 collective-permute-done
  1.5 2.6 %collective-permute-start.1 = (bf16[32,128]{1,0:T(8,128)(2,1)S(1)}, bf16[32,128]{1,0:T(8,128)(2,1)S(1)}, u32[]{:S(2)}, u32[]{:S(2)}) collective-permute-start(bf16[32,128]{1,0:T(8,128)(2,1)S(1)} %pad_maximum_fusion.1), channel_id=1, source_target_pairs={{0,3},{1,2},{2,1},{3,0},{4,7},{5,6},{6,5},{7,4},{8,11},{9,10},{10,... | collective-permute-start | bytes 24584 | tf_op jit(solution)/shard_map/ppermute | solution.py:240
  4.2 1.4 %collective-permute-done.1 = bf16[32,128]{1,0:T(8,128)(2,1)S(1)} collective-permute-done((bf16[32,128]{1,0:T(8,128)(2,1)S(1)}, bf16[32,128]{1,0:T(8,128)(2,1)S(1)}, u32[]{:S(2)}, u32[]{:S(2)}) %collective-permute-start.1) | collective-permute-done | bytes 8224 | tf_op jit(solution)/shard_map/ppermute | solution.py:240
  5.5 1.8 %collective-permute-start.2 = (bf16[72,128]{1,0:T(8,128)(2,1)S(1)}, bf16[72,128]{1,0:T(8,128)(2,1)S(1)}, u32[]{:S(2)}, u32[]{:S(2)}) collective-permute-start(bf16[72,128]{1,0:T(8,128)(2,1)S(1)} %pad_maximum_fusion), channel_id=1, source_target_pairs={{0,5},{1,4},{2,7},{3,6},{4,1},{5,0},{6,3},{7,2},{8,13},{9,12},{10,... | collective-permute-start | bytes 55304 | tf_op jit(solution)/shard_map/ppermute | solution.py:240
  7.3 1.4 %collective-permute-done.2 = bf16[72,128]{1,0:T(8,128)(2,1)S(1)} collective-permute-done((bf16[72,128]{1,0:T(8,128)(2,1)S(1)}, bf16[72,128]{1,0:T(8,128)(2,1)S(1)}, u32[]{:S(2)}, u32[]{:S(2)}) %collective-permute-start.2) | collective-permute-done | bytes 18464 | tf_op jit(solution)/shard_map/ppermute | solution.py:240
  8.8 2.7 %collective-permute-start.3 = (bf16[144,128]{1,0:T(8,128)(2,1)S(1)}, bf16[144,128]{1,0:T(8,128)(2,1)S(1)}, u32[]{:S(2)}, u32[]{:S(2)}) collective-permute-start(bf16[144,128]{1,0:T(8,128)(2,1)S(1)} %constant_dynamic-update-slice_fusion.packed_ref), channel_id=1, source_target_pairs={{0,9},{1,8},{2,11},{3,10},{4,13},{5,12},{6,15},{7,14},{8,1},{9,0},... | collective-permute-start | bytes 110600 | tf_op jit(solution)/shard_map/ppermute | solution.py:240
  11.5 1.5 %shard_map.47.refs_1_ = bf16[32,256,128]{2,1,0:T(8,128)(2,1)S(1)} custom-call(bf16[80,256,128]{2,1,0:T(8,128)(2,1)} %refs_2_.3), custom_call_target="tpu_custom_call" | custom-call | bytes 4194304 | tf_op jit(solution)/shard_map/pallas_call | solution.py:102
  13.1 1.6 %shard_map.46.refs_0_ = bf16[32,256,128]{2,1,0:T(8,128)(2,1)S(1)} custom-call(bf16[80,256,128]{2,1,0:T(8,128)(2,1)} %refs_2_.3), custom_call_target="tpu_custom_call" | custom-call | bytes 4194304 | tf_op jit(solution)/shard_map/pallas_call | solution.py:102
  14.6 0.0 collective-permute-done.3.packed_ref
  14.7 2.8 %shard_map.49 = f32[2,1,16,128]{3,2,1,0:T(8,128)S(1)} custom-call(bf16[144,128]{1,0:T(8,128)(2,1)S(1)} %collective-permute-done.3.packed_ref, bf16[32,256,128]{2,1,0:T(8,128)(2,1)S(1)} %shard_map.46.refs_0_, bf16[32,256,128]{2,1,0:T(8,128)(2,1)S(1)} %shard_map.47.refs_1_, bf16[80,256,128]{2,1,0:T(8,128)(2,1)} %refs_2_.3), custom_call_target="tpu_custom_call" | custom-call | flops 671088640 | bytes 5242880 | tf_op jit(solution)/shard_map/pallas_call | solution.py:268
  17.5 1.3 %collective-permute-start.4 = (f32[2,1,16,128]{3,2,1,0:T(8,128)S(1)}, f32[2,1,16,128]{3,2,1,0:T(8,128)S(1)}, u32[]{:S(2)}, u32[]{:S(2)}) collective-permute-start(f32[2,1,16,128]{3,2,1,0:T(8,128)S(1)} %shard_map.49), channel_id=1, source_target_pairs={{0,9},{1,8},{2,11},{3,10},{4,13},{5,12},{6,15},{7,14},{8,1},{9,0},... | collective-permute-start | bytes 49160 | tf_op jit(solution)/shard_map/ppermute | solution.py:240
  18.8 2.8 %shard_map.48 = f32[2,1,16,128]{3,2,1,0:T(8,128)S(1)} custom-call(bf16[144,128]{1,0:T(8,128)(2,1)S(1)} %constant_dynamic-update-slice_fusion.packed_ref, bf16[32,256,128]{2,1,0:T(8,128)(2,1)S(1)} %shard_map.46.refs_0_, bf16[32,256,128]{2,1,0:T(8,128)(2,1)S(1)} %shard_map.47.refs_1_, bf16[80,256,128]{2,1,0:T(8,128)(2,1)} %refs_2_.3), custom_call_target="tpu_custom_call" | custom-call | flops 671088640 | bytes 5242880 | tf_op jit(solution)/shard_map/pallas_call | solution.py:268
  21.6 0.0 collective-permute-done.4
  21.6 2.5 %collective-permute-start.5 = (f32[1,1,16,128]{3,2,1,0:T(8,128)S(1)}, f32[1,1,16,128]{3,2,1,0:T(8,128)S(1)}, u32[]{:S(2)}, u32[]{:S(2)}) collective-permute-start(f32[1,1,16,128]{3,2,1,0:T(8,128)S(1)} %slice.9), channel_id=1, source_target_pairs={{0,5},{1,4},{2,7},{3,6},{4,1},{5,0},{6,3},{7,2},{8,13},{9,12},{10,... | collective-permute-start | bytes 24584 | tf_op jit(solution)/shard_map/ppermute | solution.py:240
  24.1 1.4 %collective-permute-done.5 = f32[1,1,16,128]{3,2,1,0:T(8,128)S(1)} collective-permute-done((f32[1,1,16,128]{3,2,1,0:T(8,128)S(1)}, f32[1,1,16,128]{3,2,1,0:T(8,128)S(1)}, u32[]{:S(2)}, u32[]{:S(2)}) %collective-permute-start.5) | collective-permute-done | bytes 8224 | tf_op jit(solution)/shard_map/ppermute | solution.py:240
  25.5 1.2 %collective-permute-start.6 = (f32[1,16,128]{2,1,0:T(8,128)S(1)}, f32[1,16,128]{2,1,0:T(8,128)S(1)}, u32[]{:S(2)}, u32[]{:S(2)}) collective-permute-start(f32[1,16,128]{2,1,0:T(8,128)S(1)} %fusion), channel_id=1, source_target_pairs={{0,3},{1,2},{2,1},{3,0},{4,7},{5,6},{6,5},{7,4},{8,11},{9,10},{10,... | collective-permute-start | bytes 24584 | tf_op jit(solution)/shard_map/ppermute | solution.py:240
  26.6 1.9 %collective-permute-done.6 = f32[1,16,128]{2,1,0:T(8,128)S(1)} collective-permute-done((f32[1,16,128]{2,1,0:T(8,128)S(1)}, f32[1,16,128]{2,1,0:T(8,128)S(1)}, u32[]{:S(2)}, u32[]{:S(2)}) %collective-permute-start.6) | collective-permute-done | bytes 8224 | tf_op jit(solution)/shard_map/ppermute | solution.py:240
  28.5 0.1 collective-permute-start.7
  28.7 1.1 %collective-permute-done.7.other_ref = f32[1,16,128]{2,1,0:T(8,128)S(1)} collective-permute-done((f32[1,16,128]{2,1,0:T(8,128)S(1)}, f32[1,16,128]{2,1,0:T(8,128)S(1)}, u32[]{:S(2)}, u32[]{:S(2)}) %collective-permute-start.7) | collective-permute-done | bytes 8224 | tf_op jit(solution)/shard_map/ppermute | solution.py:240
  29.7 0.7 %finish.1 = f32[2,32]{1,0:T(2,128)} custom-call(f32[1,16,128]{2,1,0:T(8,128)S(1)} %max.11.mine_ref, f32[1,16,128]{2,1,0:T(8,128)S(1)} %collective-permute-done.7.other_ref), custom_call_target="tpu_custom_call" | custom-call | tf_op jit(solution)/shard_map/finish/pallas_call | solution.py:309
  (11 shorter events, 0.1 us)
Async XLA Ops:
  0.0 1.5 %collective-permute-start = (bf16[16,128]{1,0:T(8,128)(2,1)}, bf16[16,128]{1,0:T(8,128)(2,1)S(1)}, u32[]{:S(2)}, u32[]{:S(2)}) collective-permute-start(bf16[16,128]{1,0:T(8,128)(2,1)} %bitcast.7), channel_id=1, source_target_pairs={{0,1},{1,0},{2,3},{3,2},{4,5},{5,4},{6,7},{7,6},{8,9},{9,8},{10,11... | collective-permute-start | bytes 12296 | tf_op jit(solution)/shard_map/ppermute | solution.py:240
  1.5 4.0 %collective-permute-start.1 = (bf16[32,128]{1,0:T(8,128)(2,1)S(1)}, bf16[32,128]{1,0:T(8,128)(2,1)S(1)}, u32[]{:S(2)}, u32[]{:S(2)}) collective-permute-start(bf16[32,128]{1,0:T(8,128)(2,1)S(1)} %pad_maximum_fusion.1), channel_id=1, source_target_pairs={{0,3},{1,2},{2,1},{3,0},{4,7},{5,6},{6,5},{7,4},{8,11},{9,10},{10,... | collective-permute-start | bytes 24584 | tf_op jit(solution)/shard_map/ppermute | solution.py:240
  5.5 3.3 %collective-permute-start.2 = (bf16[72,128]{1,0:T(8,128)(2,1)S(1)}, bf16[72,128]{1,0:T(8,128)(2,1)S(1)}, u32[]{:S(2)}, u32[]{:S(2)}) collective-permute-start(bf16[72,128]{1,0:T(8,128)(2,1)S(1)} %pad_maximum_fusion), channel_id=1, source_target_pairs={{0,5},{1,4},{2,7},{3,6},{4,1},{5,0},{6,3},{7,2},{8,13},{9,12},{10,... | collective-permute-start | bytes 55304 | tf_op jit(solution)/shard_map/ppermute | solution.py:240
  8.8 5.9 %collective-permute-start.3 = (bf16[144,128]{1,0:T(8,128)(2,1)S(1)}, bf16[144,128]{1,0:T(8,128)(2,1)S(1)}, u32[]{:S(2)}, u32[]{:S(2)}) collective-permute-start(bf16[144,128]{1,0:T(8,128)(2,1)S(1)} %constant_dynamic-update-slice_fusion.packed_ref), channel_id=1, source_target_pairs={{0,9},{1,8},{2,11},{3,10},{4,13},{5,12},{6,15},{7,14},{8,1},{9,0},... | collective-permute-start | bytes 110600 | tf_op jit(solution)/shard_map/ppermute | solution.py:240
  17.5 4.1 %collective-permute-start.4 = (f32[2,1,16,128]{3,2,1,0:T(8,128)S(1)}, f32[2,1,16,128]{3,2,1,0:T(8,128)S(1)}, u32[]{:S(2)}, u32[]{:S(2)}) collective-permute-start(f32[2,1,16,128]{3,2,1,0:T(8,128)S(1)} %shard_map.49), channel_id=1, source_target_pairs={{0,9},{1,8},{2,11},{3,10},{4,13},{5,12},{6,15},{7,14},{8,1},{9,0},... | collective-permute-start | bytes 49160 | tf_op jit(solution)/shard_map/ppermute | solution.py:240
  21.6 3.9 %collective-permute-start.5 = (f32[1,1,16,128]{3,2,1,0:T(8,128)S(1)}, f32[1,1,16,128]{3,2,1,0:T(8,128)S(1)}, u32[]{:S(2)}, u32[]{:S(2)}) collective-permute-start(f32[1,1,16,128]{3,2,1,0:T(8,128)S(1)} %slice.9), channel_id=1, source_target_pairs={{0,5},{1,4},{2,7},{3,6},{4,1},{5,0},{6,3},{7,2},{8,13},{9,12},{10,... | collective-permute-start | bytes 24584 | tf_op jit(solution)/shard_map/ppermute | solution.py:240
  25.5 3.1 %collective-permute-start.6 = (f32[1,16,128]{2,1,0:T(8,128)S(1)}, f32[1,16,128]{2,1,0:T(8,128)S(1)}, u32[]{:S(2)}, u32[]{:S(2)}) collective-permute-start(f32[1,16,128]{2,1,0:T(8,128)S(1)} %fusion), channel_id=1, source_target_pairs={{0,3},{1,2},{2,1},{3,0},{4,7},{5,6},{6,5},{7,4},{8,11},{9,10},{10,... | collective-permute-start | bytes 24584 | tf_op jit(solution)/shard_map/ppermute | solution.py:240
  28.5 1.2 %collective-permute-start.7 = (f32[1,16,128]{2,1,0:T(8,128)S(1)}, f32[1,16,128]{2,1,0:T(8,128)S(1)}, u32[]{:S(2)}, u32[]{:S(2)}) collective-permute-start(f32[1,16,128]{2,1,0:T(8,128)S(1)} %max.11.mine_ref), channel_id=1, source_target_pairs={{0,1},{1,0},{2,3},{3,2},{4,5},{5,4},{6,7},{7,6},{8,9},{9,8},{10,11... | collective-permute-start | bytes 24584 | tf_op jit(solution)/shard_map/ppermute | solution.py:240

commit v4 on v3

--- a/solution.py
+++ b/solution.py
@@ -13,7 +13,6 @@
 INFO = 8
 GROUP_PAGES = 16
 LOADS = 4
-LOAD_PAGES = 32
 GROUP = ("pages", "patches")
 VMEM = pl.BlockSpec(memory_space=pltpu.VMEM)
 HBM = pl.BlockSpec(memory_space=pltpu.HBM)
@@ -112,32 +111,21 @@
     )(in_hbm(gallery))
 
 
-def main_kernel(queries, cand, order, shift, loaded, packed_ref, *refs):
-    *held_refs, gallery_hbm, out_ref, token_ref, best_ref, rest_ref, sems = refs
-    pages, patches, dim = gallery_hbm.shape
-    steps = rest_ref.shape[0] // GROUP_PAGES
-
-    def fetch(i):
-        source = gallery_hbm.at[pl.ds(loaded + i * GROUP_PAGES, GROUP_PAGES)]
-        return pltpu.make_async_copy(source, rest_ref.at[pl.ds(i * GROUP_PAGES, GROUP_PAGES)], sems.at[i])
-
-    for i in range(steps):
-        fetch(i).start()
-    pieces = len(order[0])
-    planes = len(order)
-    columns = best_ref.shape[1]
-    plane_rows = columns // planes
-    piece_rows = plane_rows // pieces
+def shapes(order, columns, queries):
+    plane_rows = columns // len(order)
+    piece_rows = plane_rows // len(order[0])
+    return plane_rows, piece_rows, piece_rows // queries
+
+
+def arrange(order, columns, queries, shift, packed_ref, token_ref):
+    plane_rows, piece_rows, _ = shapes(order, columns, queries)
+    dim = packed_ref.shape[1]
     unit = plane_rows + INFO
-    each = piece_rows // queries
-    tokens = each * pieces
-    count, repeat, blocks = sizes(queries, cand)
-    held_tokens = tokens // repeat
     here = lax.shift_right_logical(lax.axis_index("patches"), shift)
     double = token_ref.shape[1] // dim
     if double == 2:
         token_ref[...] = jnp.zeros_like(token_ref)
-    for d in range(planes):
+    for d in range(len(order)):
         for i, flip in enumerate(order[d]):
             at = d * plane_rows + jnp.bitwise_xor(here, flip) * piece_rows
             start = d * unit + i * piece_rows
@@ -146,11 +134,16 @@
                 rows = pl.ds(pl.multiple_of(at + k * columns, piece_rows), piece_rows)
                 token_ref[rows, k * dim : (k + 1) * dim] = piece
 
+
+def scan(gallery_ref, begin, token_ref, best_ref):
+    pages, patches, dim = gallery_ref.shape
+    columns = best_ref.shape[1]
+    double = token_ref.shape[1] // dim
     width = min(columns, 256)
-
-    def some_pages(gallery_ref, begin, i):
+    share = GROUP_PAGES // double
+
+    def step(i, carry):
         at = pl.multiple_of(i * GROUP_PAGES, GROUP_PAGES)
-        share = GROUP_PAGES // double
         sides = [gallery_ref[pl.ds(at + k * share, share)].reshape(share * patches, dim) for k in range(double)]
         patch = sides[0] if double == 1 else jnp.concatenate(sides, axis=1)
         for c in range(0, columns, width):
@@ -163,25 +156,21 @@
             top = jnp.max(sims.reshape(share, patches, width * double), axis=1)
             for k in range(double):
                 best_ref[pl.ds(begin + at + k * share, share), c : c + width] = top[:, k * width : (k + 1) * width]
-
-    def run(ref, begin, i, carry):
-        some_pages(ref, begin, i)
         return carry
 
-    def run_rest(i, carry):
-        fetch(i).wait()
-        some_pages(rest_ref, loaded, i)
-        return carry
-
-    begin = 0
-    for ref in held_refs:
-        lax.fori_loop(0, ref.shape[0] // GROUP_PAGES, functools.partial(run, ref, begin), 0)
-        begin += ref.shape[0]
-    lax.fori_loop(0, steps, run_rest, 0)
-
+    lax.fori_loop(0, pages // GROUP_PAGES, step, 0)
+
+
+def select(order, queries, cand, packed_ref, best_ref, out_ref):
+    pages, columns = best_ref.shape
+    plane_rows, piece_rows, each = shapes(order, columns, queries)
+    pieces = len(order[0])
+    unit = plane_rows + INFO
+    count, repeat, blocks = sizes(queries, cand)
+    held_tokens = each * pieces // repeat
     first = lax.axis_index("pages") * pages
     lane = lax.broadcasted_iota(jnp.int32, (1, LANES), 1)
-    for d in range(planes):
+    for d in range(len(order)):
         block = best_ref[:, d * plane_rows : (d + 1) * plane_rows]
         info = packed_ref[d * unit + plane_rows : (d + 1) * unit, :].astype(jnp.float32)
         for r in range(blocks):
@@ -211,6 +200,37 @@
             out_ref[d, r] = line
 
 
+def near_first_kernel(queries, order, shift, packed_ref, gallery_ref, gallery_hbm, best_ref, rest_ref, token_ref, sem):
+    pages = gallery_hbm.shape[0]
+    rest = rest_ref.shape[0]
+    copy = pltpu.make_async_copy(gallery_hbm.at[pl.ds(pages - rest, rest)], rest_ref, sem)
+    copy.start()
+    arrange(order, best_ref.shape[1], queries, shift, packed_ref, token_ref)
+    scan(gallery_ref, 0, token_ref, best_ref)
+    copy.wait()
+
+
+def near_second_kernel(queries, cand, order, shift, packed_ref, first_ref, *refs):
+    *gallery_refs, out_ref, token_ref, best_ref = refs
+    arrange(order, best_ref.shape[1], queries, shift, packed_ref, token_ref)
+    begin = first_ref.shape[0]
+    best_ref[0:begin, :] = first_ref[...]
+    for ref in gallery_refs:
+        scan(ref, begin, token_ref, best_ref)
+        begin += ref.shape[0]
+    select(order, queries, cand, packed_ref, best_ref, out_ref)
+
+
+def far_kernel(queries, cand, order, shift, packed_ref, *refs):
+    *gallery_refs, out_ref, token_ref, best_ref = refs
+    arrange(order, best_ref.shape[1], queries, shift, packed_ref, token_ref)
+    begin = 0
+    for ref in gallery_refs:
+        scan(ref, begin, token_ref, best_ref)
+        begin += ref.shape[0]
+    select(order, queries, cand, packed_ref, best_ref, out_ref)
+
+
 def finish_kernel(queries, cand, tokens, mine_ref, other_ref, scores_ref):
     count, repeat, blocks = sizes(queries, cand)
     lines = []
@@ -243,7 +263,10 @@
         return bit if bit == 1 else bit | 1
 
     info, own = start(candidates, page_rows, queries)
-    loaded = [load(gallery, 0, LOAD_PAGES), load(gallery, LOAD_PAGES, LOAD_PAGES)]
+    rest = GROUP_PAGES * max(1, pages // GROUP_PAGES // 5)
+    most = pages - 2 * rest
+    gallery_a = load(gallery, 0, most)
+    gallery_b = load(gallery, most, rest)
     held, bit, shift = queries, 1, 0
     while held.shape[1] % SUBLANES and bit < parts:
         other = swap(held, mask_of(bit))
@@ -261,26 +284,21 @@
     packed = jnp.concatenate([packed, info], axis=0)
     order = [order]
 
-    def maxima(packed, order):
-        columns = len(order) * query_count * tokens
-        double = 2 if columns <= 128 else 1
-        rest = pages - 2 * LOAD_PAGES
+    columns = planes // 2 * query_count * tokens
+    double = 2 if columns <= 128 else 1
+    token_scratch = pltpu.VMEM((columns * double, dim * double), jnp.bfloat16)
+    best_scratch = pltpu.VMEM((pages, columns), jnp.float32)
+    message = jax.ShapeDtypeStruct((planes // 2, blocks, tokens // repeat, LANES), jnp.float32)
+
+    def call(kernel, count, **kwargs):
         return pl.pallas_call(
-            functools.partial(main_kernel, query_count, cand, order, shift, 2 * LOAD_PAGES),
-            out_shape=jax.ShapeDtypeStruct((len(order), blocks, tokens // repeat, LANES), jnp.float32),
-            in_specs=[VMEM, VMEM, VMEM, HBM],
-            out_specs=VMEM,
-            scratch_shapes=[
-                pltpu.VMEM((columns * double, dim * double), jnp.bfloat16),
-                pltpu.VMEM((pages, columns), jnp.float32),
-                pltpu.VMEM((rest, patches, dim), jnp.bfloat16),
-                pltpu.SemaphoreType.DMA((rest // GROUP_PAGES,)),
-            ],
+            kernel,
             cost_estimate=pl.CostEstimate(
-                flops=2 * pages * patches * dim * columns, transcendentals=0, bytes_accessed=2 * gallery.size
+                flops=2 * count * patches * dim * columns, transcendentals=0, bytes_accessed=count * patches * dim * 2
             ),
             compiler_params=pltpu.CompilerParams(vmem_limit_bytes=24 << 20),
-        )(packed, *loaded, in_hbm(gallery))
+            **kwargs,
+        )
 
     bit = 1
     while bit < planes:
@@ -289,8 +307,33 @@
         other = swap(packed, mask)
         flips = [[((mask % parts) >> shift) ^ flip for flip in flips] for flips in order]
         if last:
-            near = maxima(packed, order)
-            far = maxima(other, flips)
+            near_best, gallery_c = call(
+                functools.partial(near_first_kernel, query_count, order, shift),
+                most,
+                out_shape=(
+                    jax.ShapeDtypeStruct((most, columns), jnp.float32),
+                    jax.ShapeDtypeStruct((rest, patches, dim), gallery.dtype),
+                ),
+                in_specs=[VMEM, VMEM, HBM],
+                out_specs=(VMEM, VMEM),
+                scratch_shapes=[token_scratch, pltpu.SemaphoreType.DMA],
+            )(packed, gallery_a, in_hbm(gallery))
+            far = call(
+                functools.partial(far_kernel, query_count, cand, flips, shift),
+                pages,
+                out_shape=message,
+                in_specs=[VMEM] * 4,
+                out_specs=VMEM,
+                scratch_shapes=[token_scratch, best_scratch],
+            )(other, gallery_a, gallery_b, gallery_c)
+            near = call(
+                functools.partial(near_second_kernel, query_count, cand, order, shift),
+                2 * rest,
+                out_shape=message,
+                in_specs=[VMEM] * 4,
+                out_specs=VMEM,
+                scratch_shapes=[token_scratch, best_scratch],
+            )(packed, near_best, gallery_b, gallery_c)
         else:
             packed = jnp.concatenate([packed, other], axis=0)
             order = order + flips

time: 30.6 us -> 31.5 us (1.029)
  waiting for transfers between devices: 7.21 us -> 7.93 us
  starting transfers between devices: 12.7 us -> 13.3 us
  Pallas kernels: 10.4 us -> 9.84 us
    ppermute x8, waiting for transfers between devices: 7.21 us -> 7.93 us  [swap(): return lax.ppermute(x, GROUP, [(i, i ^ mask) for i in range(everyone)])]
    ppermute x8, starting transfers between devices: 12.7 us -> 13.3 us  [swap(): return lax.ppermute(x, GROUP, [(i, i ^ mask) for i in range(everyone)])]
    pallas_call x2 -> x3, Pallas kernels: 5.58 us -> 5.06 us  [the longest x1 2.51 us: body(): call(functools.partial(far_kernel, query_count, cand, flips, shift), page...]
  transfers between devices with their start and end apart: 8 -> 8, of which waited for: 6 -> 7; matrix products, arithmetic and copies ran while one was open for 0% -> 0% of each run, Pallas kernels for 23% -> 21%
where the time goes in v4:
time: 31.5 us; the launch traced here: 31.2 us
  starting transfers between devices  13.3 us (42%)
  Pallas kernels  9.84 us (31%)
  waiting for transfers between devices  7.93 us (25%)
    ppermute x8, starting transfers between devices, swap(): return lax.ppermute(x, GROUP, [(i, i ^ mask) for i in range(everyone)])  13.3 us
    ppermute x8, waiting for transfers between devices, swap(): return lax.ppermute(x, GROUP, [(i, i ^ mask) for i in range(everyone)])  7.93 us
    pallas_call x2, Pallas kernels, load(): pl.pallas_call(functools.partial(load_kernel, first), out_shape=jax.Shape...  3.11 us
    pallas_call x1, Pallas kernels, body(): call(functools.partial(far_kernel, query_count, cand, flips, shift), page...  2.51 us
    pallas_call x1, Pallas kernels, body(): call(functools.partial(near_first_kernel, query_count, order, shift), mos...  1.47 us
    pallas_call x1, Pallas kernels, body(): call(functools.partial(near_second_kernel, query_count, cand, order, shif...  1.07 us
    pallas_call x1, Pallas kernels, start(): pl.pallas_call(start_kernel, out_shape=(jax.ShapeDtypeStruct((INFO, LANES...  0.96 us
    pallas_call x1, Pallas kernels, body(): pl.pallas_call(functools.partial(finish_kernel, query_count, cand, tokens...  0.71 us
  transfers between devices with their start and end apart: 8, of which 7 were waited for; matrix products, arithmetic and copies ran while one was open for 0% of the time, Pallas kernels for 21%

profile of v4, /device:TPU:0, one launch (start us, length us, event | category | flops | bytes accessed | tf_op | source)
XLA Modules:
  0.0 31.2 jit_solution(383101913361830795)
XLA Ops:
  0.0 0.5 %collective-permute-start = (bf16[16,128]{1,0:T(8,128)(2,1)}, bf16[16,128]{1,0:T(8,128)(2,1)S(1)}, u32[]{:S(2)}, u32[]{:S(2)}) collective-permute-start(bf16[16,128]{1,0:T(8,128)(2,1)} %bitcast.7), channel_id=1, source_target_pairs={{0,1},{1,0},{2,3},{3,2},{4,5},{5,4},{6,7},{7,6},{8,9},{9,8},{10,11... | collective-permute-start | bytes 12296 | tf_op jit(solution)/shard_map/ppermute | solution.py:260
  0.5 1.0 %start.1 = (bf16[8,128]{1,0:T(8,128)(2,1)S(1)}, bf16[2,8,128]{2,1,0:T(8,128)(2,1)S(1)}) custom-call(s32[2,32]{1,0:T(2,128)} %candidates_hbm.1, s32[320]{0:T(512)} %page_rows_hbm.1, bf16[2,8,128]{2,1,0:T(8,128)(2,1)} %tokens_hbm.1), custom_call_target="tpu_custom_call" | custom-call | flops 1048576 | bytes 1048576 | tf_op jit(solution)/shard_map/start/pallas_call | solution.py:69
  1.5 1.9 %shard_map.46.gallery_ref.refs_0_ = bf16[48,256,128]{2,1,0:T(8,128)(2,1)S(1)} custom-call(bf16[80,256,128]{2,1,0:T(8,128)(2,1)} %gallery_hbm.5), custom_call_target="tpu_custom_call" | custom-call | bytes 6291456 | tf_op jit(solution)/shard_map/pallas_call | solution.py:101
  3.4 1.2 %shard_map.48.refs_0_.refs_1_ = bf16[16,256,128]{2,1,0:T(8,128)(2,1)S(1)} custom-call(bf16[80,256,128]{2,1,0:T(8,128)(2,1)} %gallery_hbm.5), custom_call_target="tpu_custom_call" | custom-call | bytes 2097152 | tf_op jit(solution)/shard_map/pallas_call | solution.py:101
  4.6 0.0 collective-permute-done
  4.6 2.7 %collective-permute-start.1 = (bf16[32,128]{1,0:T(8,128)(2,1)S(1)}, bf16[32,128]{1,0:T(8,128)(2,1)S(1)}, u32[]{:S(2)}, u32[]{:S(2)}) collective-permute-start(bf16[32,128]{1,0:T(8,128)(2,1)S(1)} %pad_maximum_fusion.1), channel_id=1, source_target_pairs={{0,3},{1,2},{2,1},{3,0},{4,7},{5,6},{6,5},{7,4},{8,11},{9,10},{10,... | collective-permute-start | bytes 24584 | tf_op jit(solution)/shard_map/ppermute | solution.py:260
  7.3 1.4 %collective-permute-done.1 = bf16[32,128]{1,0:T(8,128)(2,1)S(1)} collective-permute-done((bf16[32,128]{1,0:T(8,128)(2,1)S(1)}, bf16[32,128]{1,0:T(8,128)(2,1)S(1)}, u32[]{:S(2)}, u32[]{:S(2)}) %collective-permute-start.1) | collective-permute-done | bytes 8224 | tf_op jit(solution)/shard_map/ppermute | solution.py:260
  8.6 1.8 %collective-permute-start.2 = (bf16[72,128]{1,0:T(8,128)(2,1)S(1)}, bf16[72,128]{1,0:T(8,128)(2,1)S(1)}, u32[]{:S(2)}, u32[]{:S(2)}) collective-permute-start(bf16[72,128]{1,0:T(8,128)(2,1)S(1)} %pad_maximum_fusion), channel_id=1, source_target_pairs={{0,5},{1,4},{2,7},{3,6},{4,1},{5,0},{6,3},{7,2},{8,13},{9,12},{10,... | collective-permute-start | bytes 55304 | tf_op jit(solution)/shard_map/ppermute | solution.py:260
  10.5 1.4 %collective-permute-done.2 = bf16[72,128]{1,0:T(8,128)(2,1)S(1)} collective-permute-done((bf16[72,128]{1,0:T(8,128)(2,1)S(1)}, bf16[72,128]{1,0:T(8,128)(2,1)S(1)}, u32[]{:S(2)}, u32[]{:S(2)}) %collective-permute-start.2) | collective-permute-done | bytes 18464 | tf_op jit(solution)/shard_map/ppermute | solution.py:260
  11.9 2.7 %collective-permute-start.3 = (bf16[144,128]{1,0:T(8,128)(2,1)S(1)}, bf16[144,128]{1,0:T(8,128)(2,1)S(1)}, u32[]{:S(2)}, u32[]{:S(2)}) collective-permute-start(bf16[144,128]{1,0:T(8,128)(2,1)S(1)} %constant_dynamic-update-slice_fusion.packed_ref), channel_id=1, source_target_pairs={{0,9},{1,8},{2,11},{3,10},{4,13},{5,12},{6,15},{7,14},{8,1},{9,0},... | collective-permute-start | bytes 110600 | tf_op jit(solution)/shard_map/ppermute | solution.py:260
  14.7 1.5 %shard_map.47 = (f32[48,128]{1,0:T(8,128)S(1)}, bf16[16,256,128]{2,1,0:T(8,128)(2,1)S(1)}) custom-call(bf16[144,128]{1,0:T(8,128)(2,1)S(1)} %constant_dynamic-update-slice_fusion.packed_ref, bf16[48,256,128]{2,1,0:T(8,128)(2,1)S(1)} %shard_map.46.gallery_ref.refs_0_, bf16[80,256,128]{2,1,0:T(8,128)(2,1)} %gallery_hbm.5), custom_call_target="tpu_custom_call" | custom-call | flops 402653184 | bytes 3145728 | tf_op jit(solution)/shard_map/pallas_call | solution.py:310
  16.1 0.4 %collective-permute-done.3.packed_ref = bf16[144,128]{1,0:T(8,128)(2,1)S(1)} collective-permute-done((bf16[144,128]{1,0:T(8,128)(2,1)S(1)}, bf16[144,128]{1,0:T(8,128)(2,1)S(1)}, u32[]{:S(2)}, u32[]{:S(2)}) %collective-permute-start.3) | collective-permute-done | bytes 36896 | tf_op jit(solution)/shard_map/ppermute | solution.py:260
  16.5 2.5 %shard_map.50 = f32[2,1,16,128]{3,2,1,0:T(8,128)S(1)} custom-call(bf16[144,128]{1,0:T(8,128)(2,1)S(1)} %collective-permute-done.3.packed_ref, bf16[48,256,128]{2,1,0:T(8,128)(2,1)S(1)} %shard_map.46.gallery_ref.refs_0_, bf16[16,256,128]{2,1,0:T(8,128)(2,1)S(1)} %shard_map.48.refs_0_.refs_1_, bf16[16,256,128]{2,1,0:T(8,128)(2,1)S(1)} %get-tuple-element.12.refs_1_.refs_2_), custom_call_target="tpu_custom_call" | custom-call | flops 671088640 | bytes 5242880 | tf_op jit(solution)/shard_map/pallas_call | solution.py:321
  19.0 2.5 %collective-permute-start.4 = (f32[2,1,16,128]{3,2,1,0:T(8,128)S(1)}, f32[2,1,16,128]{3,2,1,0:T(8,128)S(1)}, u32[]{:S(2)}, u32[]{:S(2)}) collective-permute-start(f32[2,1,16,128]{3,2,1,0:T(8,128)S(1)} %shard_map.50), channel_id=1, source_target_pairs={{0,9},{1,8},{2,11},{3,10},{4,13},{5,12},{6,15},{7,14},{8,1},{9,0},... | collective-permute-start | bytes 49160 | tf_op jit(solution)/shard_map/ppermute | solution.py:260
  21.5 1.1 %shard_map.49 = f32[2,1,16,128]{3,2,1,0:T(8,128)S(1)} custom-call(bf16[144,128]{1,0:T(8,128)(2,1)S(1)} %constant_dynamic-update-slice_fusion.packed_ref, f32[48,128]{1,0:T(8,128)S(1)} %get-tuple-element.11.first_ref, bf16[16,256,128]{2,1,0:T(8,128)(2,1)S(1)} %shard_map.48.refs_0_.refs_1_, bf16[16,256,128]{2,1,0:T(8,128)(2,1)S(1)} %get-tuple-element.12.refs_1_.refs_2_), custom_call_target="tpu_custom_call" | custom-call | flops 268435456 | bytes 2097152 | tf_op jit(solution)/shard_map/pallas_call | solution.py:329
  22.6 0.5 %collective-permute-done.4 = f32[2,1,16,128]{3,2,1,0:T(8,128)S(1)} collective-permute-done((f32[2,1,16,128]{3,2,1,0:T(8,128)S(1)}, f32[2,1,16,128]{3,2,1,0:T(8,128)S(1)}, u32[]{:S(2)}, u32[]{:S(2)}) %collective-permute-start.4) | collective-permute-done | bytes 16416 | tf_op jit(solution)/shard_map/ppermute | solution.py:260
  23.2 1.8 %collective-permute-start.5 = (f32[1,1,16,128]{3,2,1,0:T(8,128)S(1)}, f32[1,1,16,128]{3,2,1,0:T(8,128)S(1)}, u32[]{:S(2)}, u32[]{:S(2)}) collective-permute-start(f32[1,1,16,128]{3,2,1,0:T(8,128)S(1)} %slice.9), channel_id=1, source_target_pairs={{0,5},{1,4},{2,7},{3,6},{4,1},{5,0},{6,3},{7,2},{8,13},{9,12},{10,... | collective-permute-start | bytes 24584 | tf_op jit(solution)/shard_map/ppermute | solution.py:260
  24.9 1.4 %collective-permute-done.5 = f32[1,1,16,128]{3,2,1,0:T(8,128)S(1)} collective-permute-done((f32[1,1,16,128]{3,2,1,0:T(8,128)S(1)}, f32[1,1,16,128]{3,2,1,0:T(8,128)S(1)}, u32[]{:S(2)}, u32[]{:S(2)}) %collective-permute-start.5) | collective-permute-done | bytes 8224 | tf_op jit(solution)/shard_map/ppermute | solution.py:260
  26.3 1.3 %collective-permute-start.6 = (f32[1,16,128]{2,1,0:T(8,128)S(1)}, f32[1,16,128]{2,1,0:T(8,128)S(1)}, u32[]{:S(2)}, u32[]{:S(2)}) collective-permute-start(f32[1,16,128]{2,1,0:T(8,128)S(1)} %fusion), channel_id=1, source_target_pairs={{0,3},{1,2},{2,1},{3,0},{4,7},{5,6},{6,5},{7,4},{8,11},{9,10},{10,... | collective-permute-start | bytes 24584 | tf_op jit(solution)/shard_map/ppermute | solution.py:260
  27.6 1.8 %collective-permute-done.6 = f32[1,16,128]{2,1,0:T(8,128)S(1)} collective-permute-done((f32[1,16,128]{2,1,0:T(8,128)S(1)}, f32[1,16,128]{2,1,0:T(8,128)S(1)}, u32[]{:S(2)}, u32[]{:S(2)}) %collective-permute-start.6) | collective-permute-done | bytes 8224 | tf_op jit(solution)/shard_map/ppermute | solution.py:260
  29.4 0.1 collective-permute-start.7
  29.5 1.1 %collective-permute-done.7.other_ref = f32[1,16,128]{2,1,0:T(8,128)S(1)} collective-permute-done((f32[1,16,128]{2,1,0:T(8,128)S(1)}, f32[1,16,128]{2,1,0:T(8,128)S(1)}, u32[]{:S(2)}, u32[]{:S(2)}) %collective-permute-start.7) | collective-permute-done | bytes 8224 | tf_op jit(solution)/shard_map/ppermute | solution.py:260
  30.5 0.7 %finish.1 = f32[2,32]{1,0:T(2,128)} custom-call(f32[1,16,128]{2,1,0:T(8,128)S(1)} %max.11.mine_ref, f32[1,16,128]{2,1,0:T(8,128)S(1)} %collective-permute-done.7.other_ref), custom_call_target="tpu_custom_call" | custom-call | tf_op jit(solution)/shard_map/finish/pallas_call | solution.py:352
  (11 shorter events, 0.1 us)
Async XLA Ops:
  0.0 4.6 %collective-permute-start = (bf16[16,128]{1,0:T(8,128)(2,1)}, bf16[16,128]{1,0:T(8,128)(2,1)S(1)}, u32[]{:S(2)}, u32[]{:S(2)}) collective-permute-start(bf16[16,128]{1,0:T(8,128)(2,1)} %bitcast.7), channel_id=1, source_target_pairs={{0,1},{1,0},{2,3},{3,2},{4,5},{5,4},{6,7},{7,6},{8,9},{9,8},{10,11... | collective-permute-start | bytes 12296 | tf_op jit(solution)/shard_map/ppermute | solution.py:260
  4.6 4.0 %collective-permute-start.1 = (bf16[32,128]{1,0:T(8,128)(2,1)S(1)}, bf16[32,128]{1,0:T(8,128)(2,1)S(1)}, u32[]{:S(2)}, u32[]{:S(2)}) collective-permute-start(bf16[32,128]{1,0:T(8,128)(2,1)S(1)} %pad_maximum_fusion.1), channel_id=1, source_target_pairs={{0,3},{1,2},{2,1},{3,0},{4,7},{5,6},{6,5},{7,4},{8,11},{9,10},{10,... | collective-permute-start | bytes 24584 | tf_op jit(solution)/shard_map/ppermute | solution.py:260
  8.6 3.3 %collective-permute-start.2 = (bf16[72,128]{1,0:T(8,128)(2,1)S(1)}, bf16[72,128]{1,0:T(8,128)(2,1)S(1)}, u32[]{:S(2)}, u32[]{:S(2)}) collective-permute-start(bf16[72,128]{1,0:T(8,128)(2,1)S(1)} %pad_maximum_fusion), channel_id=1, source_target_pairs={{0,5},{1,4},{2,7},{3,6},{4,1},{5,0},{6,3},{7,2},{8,13},{9,12},{10,... | collective-permute-start | bytes 55304 | tf_op jit(solution)/shard_map/ppermute | solution.py:260
  11.9 4.6 %collective-permute-start.3 = (bf16[144,128]{1,0:T(8,128)(2,1)S(1)}, bf16[144,128]{1,0:T(8,128)(2,1)S(1)}, u32[]{:S(2)}, u32[]{:S(2)}) collective-permute-start(bf16[144,128]{1,0:T(8,128)(2,1)S(1)} %constant_dynamic-update-slice_fusion.packed_ref), channel_id=1, source_target_pairs={{0,9},{1,8},{2,11},{3,10},{4,13},{5,12},{6,15},{7,14},{8,1},{9,0},... | collective-permute-start | bytes 110600 | tf_op jit(solution)/shard_map/ppermute | solution.py:260
  19.0 4.1 %collective-permute-start.4 = (f32[2,1,16,128]{3,2,1,0:T(8,128)S(1)}, f32[2,1,16,128]{3,2,1,0:T(8,128)S(1)}, u32[]{:S(2)}, u32[]{:S(2)}) collective-permute-start(f32[2,1,16,128]{3,2,1,0:T(8,128)S(1)} %shard_map.50), channel_id=1, source_target_pairs={{0,9},{1,8},{2,11},{3,10},{4,13},{5,12},{6,15},{7,14},{8,1},{9,0},... | collective-permute-start | bytes 49160 | tf_op jit(solution)/shard_map/ppermute | solution.py:260
  23.2 3.1 %collective-permute-start.5 = (f32[1,1,16,128]{3,2,1,0:T(8,128)S(1)}, f32[1,1,16,128]{3,2,1,0:T(8,128)S(1)}, u32[]{:S(2)}, u32[]{:S(2)}) collective-permute-start(f32[1,1,16,128]{3,2,1,0:T(8,128)S(1)} %slice.9), channel_id=1, source_target_pairs={{0,5},{1,4},{2,7},{3,6},{4,1},{5,0},{6,3},{7,2},{8,13},{9,12},{10,... | collective-permute-start | bytes 24584 | tf_op jit(solution)/shard_map/ppermute | solution.py:260
  26.3 3.1 %collective-permute-start.6 = (f32[1,16,128]{2,1,0:T(8,128)S(1)}, f32[1,16,128]{2,1,0:T(8,128)S(1)}, u32[]{:S(2)}, u32[]{:S(2)}) collective-permute-start(f32[1,16,128]{2,1,0:T(8,128)S(1)} %fusion), channel_id=1, source_target_pairs={{0,3},{1,2},{2,1},{3,0},{4,7},{5,6},{6,5},{7,4},{8,11},{9,10},{10,... | collective-permute-start | bytes 24584 | tf_op jit(solution)/shard_map/ppermute | solution.py:260
  29.4 1.2 %collective-permute-start.7 = (f32[1,16,128]{2,1,0:T(8,128)S(1)}, f32[1,16,128]{2,1,0:T(8,128)S(1)}, u32[]{:S(2)}, u32[]{:S(2)}) collective-permute-start(f32[1,16,128]{2,1,0:T(8,128)S(1)} %max.11.mine_ref), channel_id=1, source_target_pairs={{0,1},{1,0},{2,3},{3,2},{4,5},{5,4},{6,7},{7,6},{8,9},{9,8},{10,11... | collective-permute-start | bytes 24584 | tf_op jit(solution)/shard_map/ppermute | solution.py:260

commit v5 on v4

--- a/solution.py
+++ b/solution.py
@@ -12,6 +12,7 @@
 BASE = 128
 INFO = 8
 GROUP_PAGES = 16
+UNROLLED = 3
 LOADS = 4
 GROUP = ("pages", "patches")
 VMEM = pl.BlockSpec(memory_space=pltpu.VMEM)
@@ -111,28 +112,21 @@
     )(in_hbm(gallery))
 
 
-def shapes(order, columns, queries):
-    plane_rows = columns // len(order)
-    piece_rows = plane_rows // len(order[0])
-    return plane_rows, piece_rows, piece_rows // queries
-
-
-def arrange(order, columns, queries, shift, packed_ref, token_ref):
-    plane_rows, piece_rows, _ = shapes(order, columns, queries)
+def arrange(order, shift, packed_ref, token_ref, columns):
     dim = packed_ref.shape[1]
-    unit = plane_rows + INFO
+    piece_rows = columns // len(order)
+    planes = 1 + max(plane for plane, _ in order)
+    plane_rows = columns // planes
     here = lax.shift_right_logical(lax.axis_index("patches"), shift)
     double = token_ref.shape[1] // dim
     if double == 2:
         token_ref[...] = jnp.zeros_like(token_ref)
-    for d in range(len(order)):
-        for i, flip in enumerate(order[d]):
-            at = d * plane_rows + jnp.bitwise_xor(here, flip) * piece_rows
-            start = d * unit + i * piece_rows
-            piece = packed_ref[start : start + piece_rows, :]
-            for k in range(double):
-                rows = pl.ds(pl.multiple_of(at + k * columns, piece_rows), piece_rows)
-                token_ref[rows, k * dim : (k + 1) * dim] = piece
+    for i, (plane, flip) in enumerate(order):
+        at = plane * plane_rows + jnp.bitwise_xor(here, flip) * piece_rows
+        piece = packed_ref[i * piece_rows : (i + 1) * piece_rows, :]
+        for k in range(double):
+            rows = pl.ds(pl.multiple_of(at + k * columns, piece_rows), piece_rows)
+            token_ref[rows, k * dim : (k + 1) * dim] = piece
 
 
 def scan(gallery_ref, begin, token_ref, best_ref):
@@ -143,7 +137,9 @@
     share = GROUP_PAGES // double
 
     def step(i, carry):
-        at = pl.multiple_of(i * GROUP_PAGES, GROUP_PAGES)
+        at = i * GROUP_PAGES
+        if not isinstance(i, int):
+            at = pl.multiple_of(at, GROUP_PAGES)
         sides = [gallery_ref[pl.ds(at + k * share, share)].reshape(share * patches, dim) for k in range(double)]
         patch = sides[0] if double == 1 else jnp.concatenate(sides, axis=1)
         for c in range(0, columns, width):
@@ -158,21 +154,28 @@
                 best_ref[pl.ds(begin + at + k * share, share), c : c + width] = top[:, k * width : (k + 1) * width]
         return carry
 
-    lax.fori_loop(0, pages // GROUP_PAGES, step, 0)
+    steps = pages // GROUP_PAGES
+    if double == 2 and steps <= UNROLLED:
+        for i in range(steps):
+            step(i, 0)
+    else:
+        lax.fori_loop(0, steps, step, 0)
 
 
 def select(order, queries, cand, packed_ref, best_ref, out_ref):
     pages, columns = best_ref.shape
-    plane_rows, piece_rows, each = shapes(order, columns, queries)
-    pieces = len(order[0])
-    unit = plane_rows + INFO
+    planes = 1 + max(plane for plane, _ in order)
+    pieces = len(order) // planes
+    plane_rows = columns // planes
+    piece_rows = plane_rows // pieces
+    each = piece_rows // queries
     count, repeat, blocks = sizes(queries, cand)
     held_tokens = each * pieces // repeat
     first = lax.axis_index("pages") * pages
     lane = lax.broadcasted_iota(jnp.int32, (1, LANES), 1)
-    for d in range(len(order)):
+    for d in range(planes):
         block = best_ref[:, d * plane_rows : (d + 1) * plane_rows]
-        info = packed_ref[d * unit + plane_rows : (d + 1) * unit, :].astype(jnp.float32)
+        info = packed_ref[columns + d * INFO : columns + (d + 1) * INFO, :].astype(jnp.float32)
         for r in range(blocks):
             rows = (info[r : r + 1, :] * BASE + info[blocks + r : blocks + r + 1, :]).astype(jnp.int32)
             local = rows - first
@@ -200,19 +203,19 @@
             out_ref[d, r] = line
 
 
-def near_first_kernel(queries, order, shift, packed_ref, gallery_ref, gallery_hbm, best_ref, rest_ref, token_ref, sem):
+def near_first_kernel(order, shift, packed_ref, gallery_ref, gallery_hbm, best_ref, rest_ref, token_ref, sem):
     pages = gallery_hbm.shape[0]
     rest = rest_ref.shape[0]
     copy = pltpu.make_async_copy(gallery_hbm.at[pl.ds(pages - rest, rest)], rest_ref, sem)
     copy.start()
-    arrange(order, best_ref.shape[1], queries, shift, packed_ref, token_ref)
+    arrange(order, shift, packed_ref, token_ref, best_ref.shape[1])
     scan(gallery_ref, 0, token_ref, best_ref)
     copy.wait()
 
 
 def near_second_kernel(queries, cand, order, shift, packed_ref, first_ref, *refs):
     *gallery_refs, out_ref, token_ref, best_ref = refs
-    arrange(order, best_ref.shape[1], queries, shift, packed_ref, token_ref)
+    arrange(order, shift, packed_ref, token_ref, best_ref.shape[1])
     begin = first_ref.shape[0]
     best_ref[0:begin, :] = first_ref[...]
     for ref in gallery_refs:
@@ -223,7 +226,7 @@
 
 def far_kernel(queries, cand, order, shift, packed_ref, *refs):
     *gallery_refs, out_ref, token_ref, best_ref = refs
-    arrange(order, best_ref.shape[1], queries, shift, packed_ref, token_ref)
+    arrange(order, shift, packed_ref, token_ref, best_ref.shape[1])
     begin = 0
     for ref in gallery_refs:
         scan(ref, begin, token_ref, best_ref)
@@ -263,26 +266,39 @@
         return bit if bit == 1 else bit | 1
 
     info, own = start(candidates, page_rows, queries)
-    rest = GROUP_PAGES * max(1, pages // GROUP_PAGES // 5)
-    most = pages - 2 * rest
+    rest = GROUP_PAGES * max(1, 2 * (pages // GROUP_PAGES) // 5)
+    most = pages - rest
     gallery_a = load(gallery, 0, most)
-    gallery_b = load(gallery, most, rest)
     held, bit, shift = queries, 1, 0
     while held.shape[1] % SUBLANES and bit < parts:
         other = swap(held, mask_of(bit))
         upper = (lax.axis_index("patches") & bit) != 0
         held = jnp.concatenate([jnp.where(upper, other, held), jnp.where(upper, held, other)], axis=1)
         bit, shift = bit * 2, shift + 1
-    packed = held.reshape(-1, dim)
-    order = [0]
-    while bit < parts:
-        mask = mask_of(bit)
-        other = swap(packed, mask)
-        packed = jnp.concatenate([own.reshape(packed.shape) if bit == 1 else packed, other], axis=0)
-        order = order + [(mask >> shift) ^ flip for flip in order]
-        bit *= 2
-    packed = jnp.concatenate([packed, info], axis=0)
-    order = [order]
+    pieces = held.reshape(-1, dim)
+    order = [(0, 0)]
+
+    def double_up(pieces, order, mask):
+        other = swap(pieces, mask)
+        mine = own.reshape(pieces.shape) if len(order) == 1 and not shift else pieces
+        return jnp.concatenate([mine, other], axis=0), order + [(p, (mask % parts >> shift) ^ f) for p, f in order]
+
+    for bit in [1 << k for k in range(max(1, shift), parts.bit_length() - 1)]:
+        pieces, order = double_up(pieces, order, mask_of(bit))
+    infos = info
+    for bit in [1 << k for k in range(planes.bit_length() - 2)]:
+        mask = (bit * parts) | 1
+        split = pieces.shape[0]
+        other = swap(jnp.concatenate([pieces, infos], axis=0), mask)
+        pieces = jnp.concatenate([pieces, other[:split]], axis=0)
+        infos = jnp.concatenate([infos, other[split:]], axis=0)
+        order = order + [(p + bit, (mask % parts >> shift) ^ f) for p, f in order]
+    if not shift:
+        pieces, order = double_up(pieces, order, 1)
+    packed = jnp.concatenate([pieces, infos], axis=0)
+    mask = (planes // 2 * parts) | 1
+    other = swap(packed, mask)
+    flips = [(p, (mask % parts >> shift) ^ f) for p, f in order]
 
     columns = planes // 2 * query_count * tokens
     double = 2 if columns <= 128 else 1
@@ -300,45 +316,34 @@
             **kwargs,
         )
 
-    bit = 1
-    while bit < planes:
-        mask = (bit * parts) | 1
-        last = bit == planes // 2
-        other = swap(packed, mask)
-        flips = [[((mask % parts) >> shift) ^ flip for flip in flips] for flips in order]
-        if last:
-            near_best, gallery_c = call(
-                functools.partial(near_first_kernel, query_count, order, shift),
-                most,
-                out_shape=(
-                    jax.ShapeDtypeStruct((most, columns), jnp.float32),
-                    jax.ShapeDtypeStruct((rest, patches, dim), gallery.dtype),
-                ),
-                in_specs=[VMEM, VMEM, HBM],
-                out_specs=(VMEM, VMEM),
-                scratch_shapes=[token_scratch, pltpu.SemaphoreType.DMA],
-            )(packed, gallery_a, in_hbm(gallery))
-            far = call(
-                functools.partial(far_kernel, query_count, cand, flips, shift),
-                pages,
-                out_shape=message,
-                in_specs=[VMEM] * 4,
-                out_specs=VMEM,
-                scratch_shapes=[token_scratch, best_scratch],
-            )(other, gallery_a, gallery_b, gallery_c)
-            near = call(
-                functools.partial(near_second_kernel, query_count, cand, order, shift),
-                2 * rest,
-                out_shape=message,
-                in_specs=[VMEM] * 4,
-                out_specs=VMEM,
-                scratch_shapes=[token_scratch, best_scratch],
-            )(packed, near_best, gallery_b, gallery_c)
-        else:
-            packed = jnp.concatenate([packed, other], axis=0)
-            order = order + flips
-        bit *= 2
-
+    near_best, gallery_c = call(
+        functools.partial(near_first_kernel, order, shift),
+        most,
+        out_shape=(
+            jax.ShapeDtypeStruct((most, columns), jnp.float32),
+            jax.ShapeDtypeStruct((rest, patches, dim), gallery.dtype),
+        ),
+        in_specs=[VMEM, VMEM, HBM],
+        out_specs=(VMEM, VMEM),
+        scratch_shapes=[token_scratch, pltpu.SemaphoreType.DMA],
+    )(packed, gallery_a, in_hbm(gallery))
+    far = call(
+        functools.partial(far_kernel, query_count, cand, flips, shift),
+        pages,
+        out_shape=message,
+        in_specs=[VMEM] * 3,
+        out_specs=VMEM,
+        scratch_shapes=[token_scratch, best_scratch],
+    )(other, gallery_a, gallery_c)
+    near = call(
+        functools.partial(near_second_kernel, query_count, cand, order, shift),
+        rest,
+        out_shape=message,
+        in_specs=[VMEM] * 3,
+        out_specs=VMEM,
+        scratch_shapes=[token_scratch, best_scratch],
+    )(packed, near_best, gallery_c)
+    bit = planes
     while bit > 1:
         bit //= 2
         arrived = swap(far, (bit * parts) | 1)

time: 31.5 us -> 29.1 us (0.924)
  Pallas kernels: 9.84 us -> 8.19 us
  waiting for transfers between devices: 7.93 us -> 6.78 us
  starting transfers between devices: 13.3 us -> 13.7 us
    pallas_call x2 -> x1, Pallas kernels: 3.11 us -> 1.88 us  [load(): pl.pallas_call(functools.partial(load_kernel, first), out_shape=jax.Shape...]
    ppermute x8, waiting for transfers between devices: 7.93 us -> 6.78 us  [swap(): return lax.ppermute(x, GROUP, [(i, i ^ mask) for i in range(everyone)])]
    pallas_call x1, Pallas kernels: 2.51 us -> 1.96 us  [body(): call(functools.partial(far_kernel, query_count, cand, flips, shift), page...]
    ppermute x8, starting transfers between devices: 13.3 us -> 13.7 us  [swap(): return lax.ppermute(x, GROUP, [(i, i ^ mask) for i in range(everyone)])]
  transfers between devices with their start and end apart: 8 -> 8, of which waited for: 7 -> 7; matrix products, arithmetic and copies ran while one was open for 0% -> 0% of each run, Pallas kernels for 21% -> 19%
where the time goes in v5:
time: 29.1 us; the launch traced here: 28.9 us
  starting transfers between devices  13.7 us (47%)
  Pallas kernels  8.19 us (28%)
  waiting for transfers between devices  6.78 us (23%)
    ppermute x8, starting transfers between devices, swap(): return lax.ppermute(x, GROUP, [(i, i ^ mask) for i in range(everyone)])  13.7 us
    ppermute x8, waiting for transfers between devices, swap(): return lax.ppermute(x, GROUP, [(i, i ^ mask) for i in range(everyone)])  6.78 us
    pallas_call x1, Pallas kernels, body(): call(functools.partial(far_kernel, query_count, cand, flips, shift), page...  1.96 us
    pallas_call x1, Pallas kernels, load(): pl.pallas_call(functools.partial(load_kernel, first), out_shape=jax.Shape...  1.88 us
    pallas_call x1, Pallas kernels, body(): call(functools.partial(near_first_kernel, order, shift), most, out_shape=...  1.62 us
    pallas_call x1, Pallas kernels, body(): call(functools.partial(near_second_kernel, query_count, cand, order, shif...  1.06 us
    pallas_call x1, Pallas kernels, start(): pl.pallas_call(start_kernel, out_shape=(jax.ShapeDtypeStruct((INFO, LANES...  0.97 us
    pallas_call x1, Pallas kernels, body(): pl.pallas_call(functools.partial(finish_kernel, query_count, cand, tokens...  0.71 us
  transfers between devices with their start and end apart: 8, of which 7 were waited for; matrix products, arithmetic and copies ran while one was open for 0% of the time, Pallas kernels for 19%

profile of v5, /device:TPU:0, one launch (start us, length us, event | category | flops | bytes accessed | tf_op | source)
XLA Modules:
  0.0 28.9 jit_solution(14913121402156687832)
XLA Ops:
  0.0 2.4 %collective-permute-start = (bf16[16,128]{1,0:T(8,128)(2,1)}, bf16[16,128]{1,0:T(8,128)(2,1)S(1)}, u32[]{:S(2)}, u32[]{:S(2)}) collective-permute-start(bf16[16,128]{1,0:T(8,128)(2,1)} %bitcast.7), channel_id=1, source_target_pairs={{0,3},{1,2},{2,1},{3,0},{4,7},{5,6},{6,5},{7,4},{8,11},{9,10},{10,... | collective-permute-start | bytes 12296 | tf_op jit(solution)/shard_map/ppermute | solution.py:263
  2.4 1.0 %start.1 = (bf16[8,128]{1,0:T(8,128)(2,1)S(1)}, bf16[2,8,128]{2,1,0:T(8,128)(2,1)S(1)}) custom-call(s32[2,32]{1,0:T(2,128)} %candidates_hbm.1, s32[320]{0:T(512)} %page_rows_hbm.1, bf16[2,8,128]{2,1,0:T(8,128)(2,1)} %tokens_hbm.1), custom_call_target="tpu_custom_call" | custom-call | flops 1048576 | bytes 1048576 | tf_op jit(solution)/shard_map/start/pallas_call | solution.py:70
  3.4 0.6 %collective-permute-done = bf16[16,128]{1,0:T(8,128)(2,1)S(1)} collective-permute-done((bf16[16,128]{1,0:T(8,128)(2,1)}, bf16[16,128]{1,0:T(8,128)(2,1)S(1)}, u32[]{:S(2)}, u32[]{:S(2)}) %collective-permute-start) | collective-permute-done | bytes 4128 | tf_op jit(solution)/shard_map/ppermute | solution.py:263
  4.0 2.1 %collective-permute-start.1 = (bf16[40,128]{1,0:T(8,128)(2,1)S(1)}, bf16[40,128]{1,0:T(8,128)(2,1)S(1)}, u32[]{:S(2)}, u32[]{:S(2)}) collective-permute-start(bf16[40,128]{1,0:T(8,128)(2,1)S(1)} %pad_maximum_fusion.1), channel_id=1, source_target_pairs={{0,5},{1,4},{2,7},{3,6},{4,1},{5,0},{6,3},{7,2},{8,13},{9,12},{10,... | collective-permute-start | bytes 30728 | tf_op jit(solution)/shard_map/ppermute | solution.py:263
  6.0 1.4 %collective-permute-done.1 = bf16[40,128]{1,0:T(8,128)(2,1)S(1)} collective-permute-done((bf16[40,128]{1,0:T(8,128)(2,1)S(1)}, bf16[40,128]{1,0:T(8,128)(2,1)S(1)}, u32[]{:S(2)}, u32[]{:S(2)}) %collective-permute-start.1) | collective-permute-done | bytes 10272 | tf_op jit(solution)/shard_map/ppermute | solution.py:263
  7.4 0.4 %collective-permute-start.2 = (bf16[64,128]{1,0:T(8,128)(2,1)S(1)}, bf16[64,128]{1,0:T(8,128)(2,1)S(1)}, u32[]{:S(2)}, u32[]{:S(2)}) collective-permute-start(bf16[64,128]{1,0:T(8,128)(2,1)S(1)} %pad_maximum_fusion), channel_id=1, source_target_pairs={{0,1},{1,0},{2,3},{3,2},{4,5},{5,4},{6,7},{7,6},{8,9},{9,8},{10,11... | collective-permute-start | bytes 49160 | tf_op jit(solution)/shard_map/ppermute | solution.py:263
  7.8 1.9 %shard_map.46.gallery_ref.refs_0_ = bf16[48,256,128]{2,1,0:T(8,128)(2,1)S(1)} custom-call(bf16[80,256,128]{2,1,0:T(8,128)(2,1)} %gallery_hbm.3), custom_call_target="tpu_custom_call" | custom-call | bytes 6291456 | tf_op jit(solution)/shard_map/pallas_call | solution.py:102
  9.7 0.0 collective-permute-done.2
  9.8 2.8 %collective-permute-start.3 = (bf16[144,128]{1,0:T(8,128)(2,1)S(1)}, bf16[144,128]{1,0:T(8,128)(2,1)S(1)}, u32[]{:S(2)}, u32[]{:S(2)}) collective-permute-start(bf16[144,128]{1,0:T(8,128)(2,1)S(1)} %constant_dynamic-update-slice_fusion.packed_ref), channel_id=1, source_target_pairs={{0,9},{1,8},{2,11},{3,10},{4,13},{5,12},{6,15},{7,14},{8,1},{9,0},... | collective-permute-start | bytes 110600 | tf_op jit(solution)/shard_map/ppermute | solution.py:263
  12.6 1.6 %shard_map.47 = (f32[48,128]{1,0:T(8,128)S(1)}, bf16[32,256,128]{2,1,0:T(8,128)(2,1)S(1)}) custom-call(bf16[144,128]{1,0:T(8,128)(2,1)S(1)} %constant_dynamic-update-slice_fusion.packed_ref, bf16[48,256,128]{2,1,0:T(8,128)(2,1)S(1)} %shard_map.46.gallery_ref.refs_0_, bf16[80,256,128]{2,1,0:T(8,128)(2,1)} %gallery_hbm.3), custom_call_target="tpu_custom_call" | custom-call | flops 402653184 | bytes 3145728 | tf_op jit(solution)/shard_map/pallas_call | solution.py:319
  14.2 0.1 collective-permute-done.3.packed_ref
  14.3 2.0 %shard_map.49 = f32[2,1,16,128]{3,2,1,0:T(8,128)S(1)} custom-call(bf16[144,128]{1,0:T(8,128)(2,1)S(1)} %collective-permute-done.3.packed_ref, bf16[48,256,128]{2,1,0:T(8,128)(2,1)S(1)} %shard_map.46.gallery_ref.refs_0_, bf16[32,256,128]{2,1,0:T(8,128)(2,1)S(1)} %get-tuple-element.12.refs_0_.refs_1_), custom_call_target="tpu_custom_call" | custom-call | flops 671088640 | bytes 5242880 | tf_op jit(solution)/shard_map/pallas_call | solution.py:330
  16.3 2.6 %collective-permute-start.4 = (f32[2,1,16,128]{3,2,1,0:T(8,128)S(1)}, f32[2,1,16,128]{3,2,1,0:T(8,128)S(1)}, u32[]{:S(2)}, u32[]{:S(2)}) collective-permute-start(f32[2,1,16,128]{3,2,1,0:T(8,128)S(1)} %shard_map.49), channel_id=1, source_target_pairs={{0,9},{1,8},{2,11},{3,10},{4,13},{5,12},{6,15},{7,14},{8,1},{9,0},... | collective-permute-start | bytes 49160 | tf_op jit(solution)/shard_map/ppermute | solution.py:263
  18.9 1.1 %shard_map.48 = f32[2,1,16,128]{3,2,1,0:T(8,128)S(1)} custom-call(bf16[144,128]{1,0:T(8,128)(2,1)S(1)} %constant_dynamic-update-slice_fusion.packed_ref, f32[48,128]{1,0:T(8,128)S(1)} %get-tuple-element.11.first_ref, bf16[32,256,128]{2,1,0:T(8,128)(2,1)S(1)} %get-tuple-element.12.refs_0_.refs_1_), custom_call_target="tpu_custom_call" | custom-call | flops 268435456 | bytes 2097152 | tf_op jit(solution)/shard_map/pallas_call | solution.py:338
  20.0 0.5 %collective-permute-done.4 = f32[2,1,16,128]{3,2,1,0:T(8,128)S(1)} collective-permute-done((f32[2,1,16,128]{3,2,1,0:T(8,128)S(1)}, f32[2,1,16,128]{3,2,1,0:T(8,128)S(1)}, u32[]{:S(2)}, u32[]{:S(2)}) %collective-permute-start.4) | collective-permute-done | bytes 16416 | tf_op jit(solution)/shard_map/ppermute | solution.py:263
  20.4 2.1 %collective-permute-start.5 = (f32[1,1,16,128]{3,2,1,0:T(8,128)S(1)}, f32[1,1,16,128]{3,2,1,0:T(8,128)S(1)}, u32[]{:S(2)}, u32[]{:S(2)}) collective-permute-start(f32[1,1,16,128]{3,2,1,0:T(8,128)S(1)} %slice.19), channel_id=1, source_target_pairs={{0,5},{1,4},{2,7},{3,6},{4,1},{5,0},{6,3},{7,2},{8,13},{9,12},{10,... | collective-permute-start | bytes 24584 | tf_op jit(solution)/shard_map/ppermute | solution.py:263
  22.5 1.4 %collective-permute-done.5 = f32[1,1,16,128]{3,2,1,0:T(8,128)S(1)} collective-permute-done((f32[1,1,16,128]{3,2,1,0:T(8,128)S(1)}, f32[1,1,16,128]{3,2,1,0:T(8,128)S(1)}, u32[]{:S(2)}, u32[]{:S(2)}) %collective-permute-start.5) | collective-permute-done | bytes 8224 | tf_op jit(solution)/shard_map/ppermute | solution.py:263
  23.9 1.2 %collective-permute-start.6 = (f32[1,16,128]{2,1,0:T(8,128)S(1)}, f32[1,16,128]{2,1,0:T(8,128)S(1)}, u32[]{:S(2)}, u32[]{:S(2)}) collective-permute-start(f32[1,16,128]{2,1,0:T(8,128)S(1)} %fusion), channel_id=1, source_target_pairs={{0,3},{1,2},{2,1},{3,0},{4,7},{5,6},{6,5},{7,4},{8,11},{9,10},{10,... | collective-permute-start | bytes 24584 | tf_op jit(solution)/shard_map/ppermute | solution.py:263
  25.1 1.8 %collective-permute-done.6 = f32[1,16,128]{2,1,0:T(8,128)S(1)} collective-permute-done((f32[1,16,128]{2,1,0:T(8,128)S(1)}, f32[1,16,128]{2,1,0:T(8,128)S(1)}, u32[]{:S(2)}, u32[]{:S(2)}) %collective-permute-start.6) | collective-permute-done | bytes 8224 | tf_op jit(solution)/shard_map/ppermute | solution.py:263
  27.0 0.1 collective-permute-start.7
  27.1 1.1 %collective-permute-done.7.other_ref = f32[1,16,128]{2,1,0:T(8,128)S(1)} collective-permute-done((f32[1,16,128]{2,1,0:T(8,128)S(1)}, f32[1,16,128]{2,1,0:T(8,128)S(1)}, u32[]{:S(2)}, u32[]{:S(2)}) %collective-permute-start.7) | collective-permute-done | bytes 8224 | tf_op jit(solution)/shard_map/ppermute | solution.py:263
  28.2 0.7 %finish.1 = f32[2,32]{1,0:T(2,128)} custom-call(f32[1,16,128]{2,1,0:T(8,128)S(1)} %max.11.mine_ref, f32[1,16,128]{2,1,0:T(8,128)S(1)} %collective-permute-done.7.other_ref), custom_call_target="tpu_custom_call" | custom-call | tf_op jit(solution)/shard_map/finish/pallas_call | solution.py:357
  (12 shorter events, 0.1 us)
Async XLA Ops:
  0.0 3.9 %collective-permute-start = (bf16[16,128]{1,0:T(8,128)(2,1)}, bf16[16,128]{1,0:T(8,128)(2,1)S(1)}, u32[]{:S(2)}, u32[]{:S(2)}) collective-permute-start(bf16[16,128]{1,0:T(8,128)(2,1)} %bitcast.7), channel_id=1, source_target_pairs={{0,3},{1,2},{2,1},{3,0},{4,7},{5,6},{6,5},{7,4},{8,11},{9,10},{10,... | collective-permute-start | bytes 12296 | tf_op jit(solution)/shard_map/ppermute | solution.py:263
  4.0 3.5 %collective-permute-start.1 = (bf16[40,128]{1,0:T(8,128)(2,1)S(1)}, bf16[40,128]{1,0:T(8,128)(2,1)S(1)}, u32[]{:S(2)}, u32[]{:S(2)}) collective-permute-start(bf16[40,128]{1,0:T(8,128)(2,1)S(1)} %pad_maximum_fusion.1), channel_id=1, source_target_pairs={{0,5},{1,4},{2,7},{3,6},{4,1},{5,0},{6,3},{7,2},{8,13},{9,12},{10,... | collective-permute-start | bytes 30728 | tf_op jit(solution)/shard_map/ppermute | solution.py:263
  7.4 2.3 %collective-permute-start.2 = (bf16[64,128]{1,0:T(8,128)(2,1)S(1)}, bf16[64,128]{1,0:T(8,128)(2,1)S(1)}, u32[]{:S(2)}, u32[]{:S(2)}) collective-permute-start(bf16[64,128]{1,0:T(8,128)(2,1)S(1)} %pad_maximum_fusion), channel_id=1, source_target_pairs={{0,1},{1,0},{2,3},{3,2},{4,5},{5,4},{6,7},{7,6},{8,9},{9,8},{10,11... | collective-permute-start | bytes 49160 | tf_op jit(solution)/shard_map/ppermute | solution.py:263
  9.8 4.6 %collective-permute-start.3 = (bf16[144,128]{1,0:T(8,128)(2,1)S(1)}, bf16[144,128]{1,0:T(8,128)(2,1)S(1)}, u32[]{:S(2)}, u32[]{:S(2)}) collective-permute-start(bf16[144,128]{1,0:T(8,128)(2,1)S(1)} %constant_dynamic-update-slice_fusion.packed_ref), channel_id=1, source_target_pairs={{0,9},{1,8},{2,11},{3,10},{4,13},{5,12},{6,15},{7,14},{8,1},{9,0},... | collective-permute-start | bytes 110600 | tf_op jit(solution)/shard_map/ppermute | solution.py:263
  16.3 4.1 %collective-permute-start.4 = (f32[2,1,16,128]{3,2,1,0:T(8,128)S(1)}, f32[2,1,16,128]{3,2,1,0:T(8,128)S(1)}, u32[]{:S(2)}, u32[]{:S(2)}) collective-permute-start(f32[2,1,16,128]{3,2,1,0:T(8,128)S(1)} %shard_map.49), channel_id=1, source_target_pairs={{0,9},{1,8},{2,11},{3,10},{4,13},{5,12},{6,15},{7,14},{8,1},{9,0},... | collective-permute-start | bytes 49160 | tf_op jit(solution)/shard_map/ppermute | solution.py:263
  20.4 3.4 %collective-permute-start.5 = (f32[1,1,16,128]{3,2,1,0:T(8,128)S(1)}, f32[1,1,16,128]{3,2,1,0:T(8,128)S(1)}, u32[]{:S(2)}, u32[]{:S(2)}) collective-permute-start(f32[1,1,16,128]{3,2,1,0:T(8,128)S(1)} %slice.19), channel_id=1, source_target_pairs={{0,5},{1,4},{2,7},{3,6},{4,1},{5,0},{6,3},{7,2},{8,13},{9,12},{10,... | collective-permute-start | bytes 24584 | tf_op jit(solution)/shard_map/ppermute | solution.py:263
  23.9 3.1 %collective-permute-start.6 = (f32[1,16,128]{2,1,0:T(8,128)S(1)}, f32[1,16,128]{2,1,0:T(8,128)S(1)}, u32[]{:S(2)}, u32[]{:S(2)}) collective-permute-start(f32[1,16,128]{2,1,0:T(8,128)S(1)} %fusion), channel_id=1, source_target_pairs={{0,3},{1,2},{2,1},{3,0},{4,7},{5,6},{6,5},{7,4},{8,11},{9,10},{10,... | collective-permute-start | bytes 24584 | tf_op jit(solution)/shard_map/ppermute | solution.py:263
  27.0 1.2 %collective-permute-start.7 = (f32[1,16,128]{2,1,0:T(8,128)S(1)}, f32[1,16,128]{2,1,0:T(8,128)S(1)}, u32[]{:S(2)}, u32[]{:S(2)}) collective-permute-start(f32[1,16,128]{2,1,0:T(8,128)S(1)} %max.11.mine_ref), channel_id=1, source_target_pairs={{0,1},{1,0},{2,3},{3,2},{4,5},{5,4},{6,7},{7,6},{8,9},{9,8},{10,11... | collective-permute-start | bytes 24584 | tf_op jit(solution)/shard_map/ppermute | solution.py:263

commit v6 on v5

--- a/solution.py
+++ b/solution.py
@@ -25,15 +25,18 @@
     return count, repeat, count * repeat // LANES
 
 
-def start_kernel(candidates_hbm, page_rows_hbm, tokens_hbm, info_ref, tokens_ref, candidates_ref, page_rows_ref, sems):
+def start_kernel(
+    candidates_hbm, page_rows_hbm, tokens_hbm, gallery_hbm, info_ref, tokens_ref, first_ref, candidates_ref, page_rows_ref, sems
+):
     copies = [
         pltpu.make_async_copy(page_rows_hbm, page_rows_ref, sems.at[0]),
         pltpu.make_async_copy(candidates_hbm, candidates_ref, sems.at[1]),
         pltpu.make_async_copy(tokens_hbm, tokens_ref, sems.at[2]),
+        pltpu.make_async_copy(gallery_hbm.at[pl.ds(0, first_ref.shape[0])], first_ref, sems.at[3]),
     ]
     for copy in copies:
         copy.start()
-    for copy in copies:
+    for copy in copies[:2]:
         copy.wait()
     queries, cand = candidates_ref.shape
     pages = page_rows_ref.shape[0]
@@ -60,27 +63,33 @@
     if 2 * blocks < INFO:
         rows.append(jnp.zeros((INFO - 2 * blocks, LANES), jnp.float32))
     info_ref[...] = jnp.concatenate(rows, axis=0).astype(jnp.bfloat16)
+    for copy in copies[2:]:
+        copy.wait()
 
 
 def in_hbm(x):
     return pltpu.with_memory_space_constraint(x, pltpu.HBM)
 
 
-def start(candidates, page_rows, tokens):
+def start(candidates, page_rows, tokens, gallery, first):
     return pl.pallas_call(
         start_kernel,
-        out_shape=(jax.ShapeDtypeStruct((INFO, LANES), jnp.bfloat16), jax.ShapeDtypeStruct(tokens.shape, tokens.dtype)),
-        in_specs=[HBM, HBM, HBM],
-        out_specs=(VMEM, VMEM),
+        out_shape=(
+            jax.ShapeDtypeStruct((INFO, LANES), jnp.bfloat16),
+            jax.ShapeDtypeStruct(tokens.shape, tokens.dtype),
+            jax.ShapeDtypeStruct((first, *gallery.shape[1:]), gallery.dtype),
+        ),
+        in_specs=[HBM] * 4,
+        out_specs=(VMEM, VMEM, VMEM),
         scratch_shapes=[
             pltpu.VMEM(candidates.shape, jnp.int32),
             pltpu.VMEM(page_rows.shape, jnp.int32),
-            pltpu.SemaphoreType.DMA((3,)),
+            pltpu.SemaphoreType.DMA((4,)),
         ],
         compiler_params=pltpu.CompilerParams(vmem_limit_bytes=8 << 20),
         cost_estimate=pl.CostEstimate(flops=1 << 20, transcendentals=0, bytes_accessed=1 << 20),
         name="start",
-    )(in_hbm(candidates), in_hbm(page_rows), in_hbm(tokens))
+    )(in_hbm(candidates), in_hbm(page_rows), in_hbm(tokens), in_hbm(gallery))
 
 
 def load_kernel(first, gallery_hbm, out_ref, sems):
@@ -174,18 +183,23 @@
     first = lax.axis_index("pages") * pages
     lane = lax.broadcasted_iota(jnp.int32, (1, LANES), 1)
     for d in range(planes):
-        block = best_ref[:, d * plane_rows : (d + 1) * plane_rows]
+        left = best_ref[:, d * plane_rows : (d + 1) * plane_rows]
+        digits = []
+        for _ in range(3):
+            digits.append(left.astype(jnp.bfloat16))
+            left = left - digits[-1].astype(jnp.float32)
+        block = jnp.concatenate(digits, axis=0)
         info = packed_ref[columns + d * INFO : columns + (d + 1) * INFO, :].astype(jnp.float32)
         for r in range(blocks):
             rows = (info[r : r + 1, :] * BASE + info[blocks + r : blocks + r + 1, :]).astype(jnp.int32)
             local = rows - first
             held = (local >= 0) & (local < pages)
             pick = (lax.broadcasted_iota(jnp.int32, (pages, LANES), 0) == local).astype(jnp.float32)
+            pick = pick.astype(jnp.bfloat16)
             got = lax.dot_general(
                 block,
-                pick,
+                jnp.concatenate([pick] * 3, axis=0),
                 (((0,), (0,)), ((), ())),
-                precision=lax.Precision.HIGHEST,
                 preferred_element_type=jnp.float32,
             )
             owner = ((r * LANES + lane) % count) // cand
@@ -265,10 +279,11 @@
     def mask_of(bit):
         return bit if bit == 1 else bit | 1
 
-    info, own = start(candidates, page_rows, queries)
-    rest = GROUP_PAGES * max(1, 2 * (pages // GROUP_PAGES) // 5)
-    most = pages - rest
-    gallery_a = load(gallery, 0, most)
+    last = GROUP_PAGES * max(1, pages // GROUP_PAGES // 5)
+    first = GROUP_PAGES * ((pages - last) // GROUP_PAGES // 2)
+    middle = pages - first - last
+    info, own, gallery_a = start(candidates, page_rows, queries, gallery, first)
+    gallery_b = load(gallery, first, middle)
     held, bit, shift = queries, 1, 0
     while held.shape[1] % SUBLANES and bit < parts:
         other = swap(held, mask_of(bit))
@@ -318,10 +333,10 @@
 
     near_best, gallery_c = call(
         functools.partial(near_first_kernel, order, shift),
-        most,
+        first,
         out_shape=(
-            jax.ShapeDtypeStruct((most, columns), jnp.float32),
-            jax.ShapeDtypeStruct((rest, patches, dim), gallery.dtype),
+            jax.ShapeDtypeStruct((first, columns), jnp.float32),
+            jax.ShapeDtypeStruct((last, patches, dim), gallery.dtype),
         ),
         in_specs=[VMEM, VMEM, HBM],
         out_specs=(VMEM, VMEM),
@@ -331,18 +346,18 @@
         functools.partial(far_kernel, query_count, cand, flips, shift),
         pages,
         out_shape=message,
-        in_specs=[VMEM] * 3,
+        in_specs=[VMEM] * 4,
         out_specs=VMEM,
         scratch_shapes=[token_scratch, best_scratch],
-    )(other, gallery_a, gallery_c)
+    )(other, gallery_a, gallery_b, gallery_c)
     near = call(
         functools.partial(near_second_kernel, query_count, cand, order, shift),
-        rest,
+        pages - first,
         out_shape=message,
-        in_specs=[VMEM] * 3,
+        in_specs=[VMEM] * 4,
         out_specs=VMEM,
         scratch_shapes=[token_scratch, best_scratch],
-    )(packed, near_best, gallery_c)
+    )(packed, near_best, gallery_b, gallery_c)
     bit = planes
     while bit > 1:
         bit //= 2

time: 29.1 us -> 28.6 us (0.983)
  starting transfers between devices: 13.7 us -> 12.5 us
  waiting for transfers between devices: 6.78 us -> 7.36 us
    ppermute x8, starting transfers between devices: 13.7 us -> 12.5 us  [swap(): return lax.ppermute(x, GROUP, [(i, i ^ mask) for i in range(everyone)])]
    pallas_call x1, Pallas kernels: 0.97 us -> 1.67 us  [start(): pl.pallas_call(start_kernel, out_shape=(jax.ShapeDtypeStruct((INFO, LANES...]
    ppermute x8, waiting for transfers between devices: 6.78 us -> 7.36 us  [swap(): return lax.ppermute(x, GROUP, [(i, i ^ mask) for i in range(everyone)])]
    pallas_call x1, Pallas kernels: 1.62 us -> 1.26 us  [body(): call(functools.partial(near_first_kernel, order, shift), first, out_shape...]
    pallas_call x1, Pallas kernels: 1.88 us -> 1.55 us  [load(): pl.pallas_call(functools.partial(load_kernel, first), out_shape=jax.Shape...]
  transfers between devices with their start and end apart: 8 -> 8, of which waited for: 7 -> 6; matrix products, arithmetic and copies ran while one was open for 0% -> 0% of each run, Pallas kernels for 19% -> 20%
where the time goes in v6:
time: 28.6 us; the launch traced here: 28.4 us
  starting transfers between devices  12.5 us (44%)
  Pallas kernels  8.38 us (29%)
  waiting for transfers between devices  7.36 us (26%)
    ppermute x8, starting transfers between devices, swap(): return lax.ppermute(x, GROUP, [(i, i ^ mask) for i in range(everyone)])  12.5 us
    ppermute x8, waiting for transfers between devices, swap(): return lax.ppermute(x, GROUP, [(i, i ^ mask) for i in range(everyone)])  7.36 us
    pallas_call x1, Pallas kernels, body(): call(functools.partial(far_kernel, query_count, cand, flips, shift), page...  1.87 us
    pallas_call x1, Pallas kernels, start(): pl.pallas_call(start_kernel, out_shape=(jax.ShapeDtypeStruct((INFO, LANES...  1.67 us
    pallas_call x1, Pallas kernels, load(): pl.pallas_call(functools.partial(load_kernel, first), out_shape=jax.Shape...  1.55 us
    pallas_call x1, Pallas kernels, body(): call(functools.partial(near_second_kernel, query_count, cand, order, shif...  1.32 us
    pallas_call x1, Pallas kernels, body(): call(functools.partial(near_first_kernel, order, shift), first, out_shape...  1.26 us
    pallas_call x1, Pallas kernels, body(): pl.pallas_call(functools.partial(finish_kernel, query_count, cand, tokens...  0.71 us
  transfers between devices with their start and end apart: 8, of which 6 were waited for; matrix products, arithmetic and copies ran while one was open for 0% of the time, Pallas kernels for 20%

profile of v6, /device:TPU:0, one launch (start us, length us, event | category | flops | bytes accessed | tf_op | source)
XLA Modules:
  0.0 28.4 jit_solution(6268240327747144822)
XLA Ops:
  0.0 2.4 %collective-permute-start = (bf16[16,128]{1,0:T(8,128)(2,1)}, bf16[16,128]{1,0:T(8,128)(2,1)S(1)}, u32[]{:S(2)}, u32[]{:S(2)}) collective-permute-start(bf16[16,128]{1,0:T(8,128)(2,1)} %bitcast.7), channel_id=1, source_target_pairs={{0,3},{1,2},{2,1},{3,0},{4,7},{5,6},{6,5},{7,4},{8,11},{9,10},{10,... | collective-permute-start | bytes 12296 | tf_op jit(solution)/shard_map/ppermute | solution.py:277
  2.4 1.7 %start.1 = (bf16[8,128]{1,0:T(8,128)(2,1)S(1)}, bf16[2,8,128]{2,1,0:T(8,128)(2,1)S(1)}, bf16[32,256,128]{2,1,0:T(8,128)(2,1)S(1)}) custom-call(s32[2,32]{1,0:T(2,128)} %candidates_hbm.1, s32[320]{0:T(512)} %page_rows_hbm.1, bf16[2,8,128]{2,1,0:T(8,128)(2,1)} %tokens_hbm.1, bf16[80,256,128]{2,1,0:T(8,128)(2,1)} %gallery_hbm.5), custom_call_target="tpu_custom_call" | custom-call | flops 1048576 | bytes 1048576 | tf_op jit(solution)/shard_map/start/pallas_call | solution.py:75
  4.1 0.0 collective-permute-done
  4.1 1.9 %collective-permute-start.1 = (bf16[40,128]{1,0:T(8,128)(2,1)S(1)}, bf16[40,128]{1,0:T(8,128)(2,1)S(1)}, u32[]{:S(2)}, u32[]{:S(2)}) collective-permute-start(bf16[40,128]{1,0:T(8,128)(2,1)S(1)} %pad_maximum_fusion.1), channel_id=1, source_target_pairs={{0,5},{1,4},{2,7},{3,6},{4,1},{5,0},{6,3},{7,2},{8,13},{9,12},{10,... | collective-permute-start | bytes 30728 | tf_op jit(solution)/shard_map/ppermute | solution.py:277
  6.1 1.4 %collective-permute-done.1 = bf16[40,128]{1,0:T(8,128)(2,1)S(1)} collective-permute-done((bf16[40,128]{1,0:T(8,128)(2,1)S(1)}, bf16[40,128]{1,0:T(8,128)(2,1)S(1)}, u32[]{:S(2)}, u32[]{:S(2)}) %collective-permute-start.1) | collective-permute-done | bytes 10272 | tf_op jit(solution)/shard_map/ppermute | solution.py:277
  7.4 0.6 %collective-permute-start.2 = (bf16[64,128]{1,0:T(8,128)(2,1)S(1)}, bf16[64,128]{1,0:T(8,128)(2,1)S(1)}, u32[]{:S(2)}, u32[]{:S(2)}) collective-permute-start(bf16[64,128]{1,0:T(8,128)(2,1)S(1)} %pad_maximum_fusion), channel_id=1, source_target_pairs={{0,1},{1,0},{2,3},{3,2},{4,5},{5,4},{6,7},{7,6},{8,9},{9,8},{10,11... | collective-permute-start | bytes 49160 | tf_op jit(solution)/shard_map/ppermute | solution.py:277
  8.0 0.8 %collective-permute-done.2 = bf16[64,128]{1,0:T(8,128)(2,1)S(1)} collective-permute-done((bf16[64,128]{1,0:T(8,128)(2,1)S(1)}, bf16[64,128]{1,0:T(8,128)(2,1)S(1)}, u32[]{:S(2)}, u32[]{:S(2)}) %collective-permute-start.2) | collective-permute-done | bytes 16416 | tf_op jit(solution)/shard_map/ppermute | solution.py:277
  8.9 2.6 %collective-permute-start.3 = (bf16[144,128]{1,0:T(8,128)(2,1)S(1)}, bf16[144,128]{1,0:T(8,128)(2,1)S(1)}, u32[]{:S(2)}, u32[]{:S(2)}) collective-permute-start(bf16[144,128]{1,0:T(8,128)(2,1)S(1)} %constant_dynamic-update-slice_fusion.packed_ref), channel_id=1, source_target_pairs={{0,9},{1,8},{2,11},{3,10},{4,13},{5,12},{6,15},{7,14},{8,1},{9,0},... | collective-permute-start | bytes 110600 | tf_op jit(solution)/shard_map/ppermute | solution.py:277
  11.5 1.5 %shard_map.47.refs_0_.refs_1_ = bf16[32,256,128]{2,1,0:T(8,128)(2,1)S(1)} custom-call(bf16[80,256,128]{2,1,0:T(8,128)(2,1)} %gallery_hbm.5), custom_call_target="tpu_custom_call" | custom-call | bytes 4194304 | tf_op jit(solution)/shard_map/pallas_call | solution.py:111
  13.1 1.3 %shard_map.46 = (f32[32,128]{1,0:T(8,128)S(1)}, bf16[16,256,128]{2,1,0:T(8,128)(2,1)S(1)}) custom-call(bf16[144,128]{1,0:T(8,128)(2,1)S(1)} %constant_dynamic-update-slice_fusion.packed_ref, bf16[32,256,128]{2,1,0:T(8,128)(2,1)S(1)} %get-tuple-element.12.gallery_ref.refs_0_, bf16[80,256,128]{2,1,0:T(8,128)(2,1)} %gallery_hbm.5), custom_call_target="tpu_custom_call" | custom-call | flops 268435456 | bytes 2097152 | tf_op jit(solution)/shard_map/pallas_call | solution.py:334
  14.3 0.0 collective-permute-done.3.packed_ref
  14.4 1.9 %shard_map.49 = f32[2,1,16,128]{3,2,1,0:T(8,128)S(1)} custom-call(bf16[144,128]{1,0:T(8,128)(2,1)S(1)} %collective-permute-done.3.packed_ref, bf16[32,256,128]{2,1,0:T(8,128)(2,1)S(1)} %get-tuple-element.12.gallery_ref.refs_0_, bf16[32,256,128]{2,1,0:T(8,128)(2,1)S(1)} %shard_map.47.refs_0_.refs_1_, bf16[16,256,128]{2,1,0:T(8,128)(2,1)S(1)} %get-tuple-element.14.refs_1_.refs_2_), custom_call_target="tpu_custom_call" | custom-call | flops 671088640 | bytes 5242880 | tf_op jit(solution)/shard_map/pallas_call | solution.py:345
  16.2 1.6 %collective-permute-start.4 = (f32[2,1,16,128]{3,2,1,0:T(8,128)S(1)}, f32[2,1,16,128]{3,2,1,0:T(8,128)S(1)}, u32[]{:S(2)}, u32[]{:S(2)}) collective-permute-start(f32[2,1,16,128]{3,2,1,0:T(8,128)S(1)} %shard_map.49), channel_id=1, source_target_pairs={{0,9},{1,8},{2,11},{3,10},{4,13},{5,12},{6,15},{7,14},{8,1},{9,0},... | collective-permute-start | bytes 49160 | tf_op jit(solution)/shard_map/ppermute | solution.py:277
  17.9 1.3 %shard_map.48 = f32[2,1,16,128]{3,2,1,0:T(8,128)S(1)} custom-call(bf16[144,128]{1,0:T(8,128)(2,1)S(1)} %constant_dynamic-update-slice_fusion.packed_ref, f32[32,128]{1,0:T(8,128)S(1)} %get-tuple-element.13.first_ref, bf16[32,256,128]{2,1,0:T(8,128)(2,1)S(1)} %shard_map.47.refs_0_.refs_1_, bf16[16,256,128]{2,1,0:T(8,128)(2,1)S(1)} %get-tuple-element.14.refs_1_.refs_2_), custom_call_target="tpu_custom_call" | custom-call | flops 402653184 | bytes 3145728 | tf_op jit(solution)/shard_map/pallas_call | solution.py:353
  19.2 1.2 %collective-permute-done.4 = f32[2,1,16,128]{3,2,1,0:T(8,128)S(1)} collective-permute-done((f32[2,1,16,128]{3,2,1,0:T(8,128)S(1)}, f32[2,1,16,128]{3,2,1,0:T(8,128)S(1)}, u32[]{:S(2)}, u32[]{:S(2)}) %collective-permute-start.4) | collective-permute-done | bytes 16416 | tf_op jit(solution)/shard_map/ppermute | solution.py:277
  20.4 1.5 %collective-permute-start.5 = (f32[1,1,16,128]{3,2,1,0:T(8,128)S(1)}, f32[1,1,16,128]{3,2,1,0:T(8,128)S(1)}, u32[]{:S(2)}, u32[]{:S(2)}) collective-permute-start(f32[1,1,16,128]{3,2,1,0:T(8,128)S(1)} %slice.19), channel_id=1, source_target_pairs={{0,5},{1,4},{2,7},{3,6},{4,1},{5,0},{6,3},{7,2},{8,13},{9,12},{10,... | collective-permute-start | bytes 24584 | tf_op jit(solution)/shard_map/ppermute | solution.py:277
  21.9 1.5 %collective-permute-done.5 = f32[1,1,16,128]{3,2,1,0:T(8,128)S(1)} collective-permute-done((f32[1,1,16,128]{3,2,1,0:T(8,128)S(1)}, f32[1,1,16,128]{3,2,1,0:T(8,128)S(1)}, u32[]{:S(2)}, u32[]{:S(2)}) %collective-permute-start.5) | collective-permute-done | bytes 8224 | tf_op jit(solution)/shard_map/ppermute | solution.py:277
  23.5 1.5 %collective-permute-start.6 = (f32[1,16,128]{2,1,0:T(8,128)S(1)}, f32[1,16,128]{2,1,0:T(8,128)S(1)}, u32[]{:S(2)}, u32[]{:S(2)}) collective-permute-start(f32[1,16,128]{2,1,0:T(8,128)S(1)} %fusion), channel_id=1, source_target_pairs={{0,3},{1,2},{2,1},{3,0},{4,7},{5,6},{6,5},{7,4},{8,11},{9,10},{10,... | collective-permute-start | bytes 24584 | tf_op jit(solution)/shard_map/ppermute | solution.py:277
  24.9 1.6 %collective-permute-done.6 = f32[1,16,128]{2,1,0:T(8,128)S(1)} collective-permute-done((f32[1,16,128]{2,1,0:T(8,128)S(1)}, f32[1,16,128]{2,1,0:T(8,128)S(1)}, u32[]{:S(2)}, u32[]{:S(2)}) %collective-permute-start.6) | collective-permute-done | bytes 8224 | tf_op jit(solution)/shard_map/ppermute | solution.py:277
  26.5 0.3 %collective-permute-start.7 = (f32[1,16,128]{2,1,0:T(8,128)S(1)}, f32[1,16,128]{2,1,0:T(8,128)S(1)}, u32[]{:S(2)}, u32[]{:S(2)}) collective-permute-start(f32[1,16,128]{2,1,0:T(8,128)S(1)} %max.11.mine_ref), channel_id=1, source_target_pairs={{0,1},{1,0},{2,3},{3,2},{4,5},{5,4},{6,7},{7,6},{8,9},{9,8},{10,11... | collective-permute-start | bytes 24584 | tf_op jit(solution)/shard_map/ppermute | solution.py:277
  26.9 0.8 %collective-permute-done.7.other_ref = f32[1,16,128]{2,1,0:T(8,128)S(1)} collective-permute-done((f32[1,16,128]{2,1,0:T(8,128)S(1)}, f32[1,16,128]{2,1,0:T(8,128)S(1)}, u32[]{:S(2)}, u32[]{:S(2)}) %collective-permute-start.7) | collective-permute-done | bytes 8224 | tf_op jit(solution)/shard_map/ppermute | solution.py:277
  27.7 0.7 %finish.1 = f32[2,32]{1,0:T(2,128)} custom-call(f32[1,16,128]{2,1,0:T(8,128)S(1)} %max.11.mine_ref, f32[1,16,128]{2,1,0:T(8,128)S(1)} %collective-permute-done.7.other_ref), custom_call_target="tpu_custom_call" | custom-call | tf_op jit(solution)/shard_map/finish/pallas_call | solution.py:372
  (12 shorter events, 0.1 us)
Async XLA Ops:
  0.0 4.1 %collective-permute-start = (bf16[16,128]{1,0:T(8,128)(2,1)}, bf16[16,128]{1,0:T(8,128)(2,1)S(1)}, u32[]{:S(2)}, u32[]{:S(2)}) collective-permute-start(bf16[16,128]{1,0:T(8,128)(2,1)} %bitcast.7), channel_id=1, source_target_pairs={{0,3},{1,2},{2,1},{3,0},{4,7},{5,6},{6,5},{7,4},{8,11},{9,10},{10,... | collective-permute-start | bytes 12296 | tf_op jit(solution)/shard_map/ppermute | solution.py:277
  4.1 3.3 %collective-permute-start.1 = (bf16[40,128]{1,0:T(8,128)(2,1)S(1)}, bf16[40,128]{1,0:T(8,128)(2,1)S(1)}, u32[]{:S(2)}, u32[]{:S(2)}) collective-permute-start(bf16[40,128]{1,0:T(8,128)(2,1)S(1)} %pad_maximum_fusion.1), channel_id=1, source_target_pairs={{0,5},{1,4},{2,7},{3,6},{4,1},{5,0},{6,3},{7,2},{8,13},{9,12},{10,... | collective-permute-start | bytes 30728 | tf_op jit(solution)/shard_map/ppermute | solution.py:277
  7.4 1.4 %collective-permute-start.2 = (bf16[64,128]{1,0:T(8,128)(2,1)S(1)}, bf16[64,128]{1,0:T(8,128)(2,1)S(1)}, u32[]{:S(2)}, u32[]{:S(2)}) collective-permute-start(bf16[64,128]{1,0:T(8,128)(2,1)S(1)} %pad_maximum_fusion), channel_id=1, source_target_pairs={{0,1},{1,0},{2,3},{3,2},{4,5},{5,4},{6,7},{7,6},{8,9},{9,8},{10,11... | collective-permute-start | bytes 49160 | tf_op jit(solution)/shard_map/ppermute | solution.py:277
  8.9 5.4 %collective-permute-start.3 = (bf16[144,128]{1,0:T(8,128)(2,1)S(1)}, bf16[144,128]{1,0:T(8,128)(2,1)S(1)}, u32[]{:S(2)}, u32[]{:S(2)}) collective-permute-start(bf16[144,128]{1,0:T(8,128)(2,1)S(1)} %constant_dynamic-update-slice_fusion.packed_ref), channel_id=1, source_target_pairs={{0,9},{1,8},{2,11},{3,10},{4,13},{5,12},{6,15},{7,14},{8,1},{9,0},... | collective-permute-start | bytes 110600 | tf_op jit(solution)/shard_map/ppermute | solution.py:277
  16.2 4.1 %collective-permute-start.4 = (f32[2,1,16,128]{3,2,1,0:T(8,128)S(1)}, f32[2,1,16,128]{3,2,1,0:T(8,128)S(1)}, u32[]{:S(2)}, u32[]{:S(2)}) collective-permute-start(f32[2,1,16,128]{3,2,1,0:T(8,128)S(1)} %shard_map.49), channel_id=1, source_target_pairs={{0,9},{1,8},{2,11},{3,10},{4,13},{5,12},{6,15},{7,14},{8,1},{9,0},... | collective-permute-start | bytes 49160 | tf_op jit(solution)/shard_map/ppermute | solution.py:277
  20.4 3.1 %collective-permute-start.5 = (f32[1,1,16,128]{3,2,1,0:T(8,128)S(1)}, f32[1,1,16,128]{3,2,1,0:T(8,128)S(1)}, u32[]{:S(2)}, u32[]{:S(2)}) collective-permute-start(f32[1,1,16,128]{3,2,1,0:T(8,128)S(1)} %slice.19), channel_id=1, source_target_pairs={{0,5},{1,4},{2,7},{3,6},{4,1},{5,0},{6,3},{7,2},{8,13},{9,12},{10,... | collective-permute-start | bytes 24584 | tf_op jit(solution)/shard_map/ppermute | solution.py:277
  23.5 3.1 %collective-permute-start.6 = (f32[1,16,128]{2,1,0:T(8,128)S(1)}, f32[1,16,128]{2,1,0:T(8,128)S(1)}, u32[]{:S(2)}, u32[]{:S(2)}) collective-permute-start(f32[1,16,128]{2,1,0:T(8,128)S(1)} %fusion), channel_id=1, source_target_pairs={{0,3},{1,2},{2,1},{3,0},{4,7},{5,6},{6,5},{7,4},{8,11},{9,10},{10,... | collective-permute-start | bytes 24584 | tf_op jit(solution)/shard_map/ppermute | solution.py:277
  26.5 1.2 %collective-permute-start.7 = (f32[1,16,128]{2,1,0:T(8,128)S(1)}, f32[1,16,128]{2,1,0:T(8,128)S(1)}, u32[]{:S(2)}, u32[]{:S(2)}) collective-permute-start(f32[1,16,128]{2,1,0:T(8,128)S(1)} %max.11.mine_ref), channel_id=1, source_target_pairs={{0,1},{1,0},{2,3},{3,2},{4,5},{5,4},{6,7},{7,6},{8,9},{9,8},{10,11... | collective-permute-start | bytes 24584 | tf_op jit(solution)/shard_map/ppermute | solution.py:277

commit v7 on v6

--- a/solution.py
+++ b/solution.py
@@ -301,17 +301,19 @@
     for bit in [1 << k for k in range(max(1, shift), parts.bit_length() - 1)]:
         pieces, order = double_up(pieces, order, mask_of(bit))
     infos = info
-    for bit in [1 << k for k in range(planes.bit_length() - 2)]:
+    hops = [1 << k for k in reversed(range(planes.bit_length() - 1))]
+    for bit in hops[:-1]:
         mask = (bit * parts) | 1
+        known = infos.shape[0] // INFO
         split = pieces.shape[0]
         other = swap(jnp.concatenate([pieces, infos], axis=0), mask)
         pieces = jnp.concatenate([pieces, other[:split]], axis=0)
         infos = jnp.concatenate([infos, other[split:]], axis=0)
-        order = order + [(p + bit, (mask % parts >> shift) ^ f) for p, f in order]
+        order = order + [(p + known, (mask % parts >> shift) ^ f) for p, f in order]
     if not shift:
         pieces, order = double_up(pieces, order, 1)
     packed = jnp.concatenate([pieces, infos], axis=0)
-    mask = (planes // 2 * parts) | 1
+    mask = (hops[-1] * parts) | 1
     other = swap(packed, mask)
     flips = [(p, (mask % parts >> shift) ^ f) for p, f in order]
 
@@ -358,12 +360,11 @@
         out_specs=VMEM,
         scratch_shapes=[token_scratch, best_scratch],
     )(packed, near_best, gallery_b, gallery_c)
-    bit = planes
-    while bit > 1:
-        bit //= 2
+    for bit in reversed(hops):
         arrived = swap(far, (bit * parts) | 1)
         best = jnp.maximum(near, arrived)
-        near, far = best[: bit // 2], best[bit // 2 :]
+        half = best.shape[0] // 2
+        near, far = best[:half], best[half:]
     best = best[0]
     bit = parts // 2
     while bit > 1:

time: 28.6 us -> 28.5 us (level)
  transfers between devices with their start and end apart: 8 -> 8, of which waited for: 6 -> 6; matrix products, arithmetic and copies ran while one was open for 0% -> 0% of each run, Pallas kernels for 20% -> 21%
where the time goes in v7:
time: 28.5 us; the launch traced here: 28.3 us
  starting transfers between devices  12.4 us (44%)
  Pallas kernels  8.39 us (29%)
  waiting for transfers between devices  7.34 us (26%)
    ppermute x8, starting transfers between devices, swap(): return lax.ppermute(x, GROUP, [(i, i ^ mask) for i in range(everyone)])  12.4 us
    ppermute x8, waiting for transfers between devices, swap(): return lax.ppermute(x, GROUP, [(i, i ^ mask) for i in range(everyone)])  7.34 us
    pallas_call x1, Pallas kernels, body(): call(functools.partial(far_kernel, query_count, cand, flips, shift), page...  1.88 us
    pallas_call x1, Pallas kernels, start(): pl.pallas_call(start_kernel, out_shape=(jax.ShapeDtypeStruct((INFO, LANES...  1.67 us
    pallas_call x1, Pallas kernels, load(): pl.pallas_call(functools.partial(load_kernel, first), out_shape=jax.Shape...  1.55 us
    pallas_call x1, Pallas kernels, body(): call(functools.partial(near_second_kernel, query_count, cand, order, shif...  1.32 us
    pallas_call x1, Pallas kernels, body(): call(functools.partial(near_first_kernel, order, shift), first, out_shape...  1.26 us
    pallas_call x1, Pallas kernels, body(): pl.pallas_call(functools.partial(finish_kernel, query_count, cand, tokens...  0.71 us
  transfers between devices with their start and end apart: 8, of which 6 were waited for; matrix products, arithmetic and copies ran while one was open for 0% of the time, Pallas kernels for 21%

profile of v7, /device:TPU:0, one launch (start us, length us, event | category | flops | bytes accessed | tf_op | source)
XLA Modules:
  0.0 28.3 jit_solution(1708456027828917808)
XLA Ops:
  0.0 2.4 %collective-permute-start = (bf16[16,128]{1,0:T(8,128)(2,1)}, bf16[16,128]{1,0:T(8,128)(2,1)S(1)}, u32[]{:S(2)}, u32[]{:S(2)}) collective-permute-start(bf16[16,128]{1,0:T(8,128)(2,1)} %bitcast.7), channel_id=1, source_target_pairs={{0,3},{1,2},{2,1},{3,0},{4,7},{5,6},{6,5},{7,4},{8,11},{9,10},{10,... | collective-permute-start | bytes 12296 | tf_op jit(solution)/shard_map/ppermute | solution.py:277
  2.4 1.7 %start.1 = (bf16[8,128]{1,0:T(8,128)(2,1)S(1)}, bf16[2,8,128]{2,1,0:T(8,128)(2,1)S(1)}, bf16[32,256,128]{2,1,0:T(8,128)(2,1)S(1)}) custom-call(s32[2,32]{1,0:T(2,128)} %candidates_hbm.1, s32[320]{0:T(512)} %page_rows_hbm.1, bf16[2,8,128]{2,1,0:T(8,128)(2,1)} %tokens_hbm.1, bf16[80,256,128]{2,1,0:T(8,128)(2,1)} %gallery_hbm.5), custom_call_target="tpu_custom_call" | custom-call | flops 1048576 | bytes 1048576 | tf_op jit(solution)/shard_map/start/pallas_call | solution.py:75
  4.1 0.0 collective-permute-done
  4.1 2.9 %collective-permute-start.1 = (bf16[40,128]{1,0:T(8,128)(2,1)S(1)}, bf16[40,128]{1,0:T(8,128)(2,1)S(1)}, u32[]{:S(2)}, u32[]{:S(2)}) collective-permute-start(bf16[40,128]{1,0:T(8,128)(2,1)S(1)} %pad_maximum_fusion.1), channel_id=1, source_target_pairs={{0,9},{1,8},{2,11},{3,10},{4,13},{5,12},{6,15},{7,14},{8,1},{9,0},... | collective-permute-start | bytes 30728 | tf_op jit(solution)/shard_map/ppermute | solution.py:277
  7.1 1.4 %collective-permute-done.1 = bf16[40,128]{1,0:T(8,128)(2,1)S(1)} collective-permute-done((bf16[40,128]{1,0:T(8,128)(2,1)S(1)}, bf16[40,128]{1,0:T(8,128)(2,1)S(1)}, u32[]{:S(2)}, u32[]{:S(2)}) %collective-permute-start.1) | collective-permute-done | bytes 10272 | tf_op jit(solution)/shard_map/ppermute | solution.py:277
  8.5 0.5 %collective-permute-start.2 = (bf16[64,128]{1,0:T(8,128)(2,1)S(1)}, bf16[64,128]{1,0:T(8,128)(2,1)S(1)}, u32[]{:S(2)}, u32[]{:S(2)}) collective-permute-start(bf16[64,128]{1,0:T(8,128)(2,1)S(1)} %pad_maximum_fusion), channel_id=1, source_target_pairs={{0,1},{1,0},{2,3},{3,2},{4,5},{5,4},{6,7},{7,6},{8,9},{9,8},{10,11... | collective-permute-start | bytes 49160 | tf_op jit(solution)/shard_map/ppermute | solution.py:277
  8.9 0.8 %collective-permute-done.2 = bf16[64,128]{1,0:T(8,128)(2,1)S(1)} collective-permute-done((bf16[64,128]{1,0:T(8,128)(2,1)S(1)}, bf16[64,128]{1,0:T(8,128)(2,1)S(1)}, u32[]{:S(2)}, u32[]{:S(2)}) %collective-permute-start.2) | collective-permute-done | bytes 16416 | tf_op jit(solution)/shard_map/ppermute | solution.py:277
  9.8 1.6 %collective-permute-start.3 = (bf16[144,128]{1,0:T(8,128)(2,1)S(1)}, bf16[144,128]{1,0:T(8,128)(2,1)S(1)}, u32[]{:S(2)}, u32[]{:S(2)}) collective-permute-start(bf16[144,128]{1,0:T(8,128)(2,1)S(1)} %constant_dynamic-update-slice_fusion.packed_ref), channel_id=1, source_target_pairs={{0,5},{1,4},{2,7},{3,6},{4,1},{5,0},{6,3},{7,2},{8,13},{9,12},{10,... | collective-permute-start | bytes 110600 | tf_op jit(solution)/shard_map/ppermute | solution.py:277
  11.4 1.5 %shard_map.47.refs_0_.refs_1_ = bf16[32,256,128]{2,1,0:T(8,128)(2,1)S(1)} custom-call(bf16[80,256,128]{2,1,0:T(8,128)(2,1)} %gallery_hbm.5), custom_call_target="tpu_custom_call" | custom-call | bytes 4194304 | tf_op jit(solution)/shard_map/pallas_call | solution.py:111
  13.0 1.3 %shard_map.46 = (f32[32,128]{1,0:T(8,128)S(1)}, bf16[16,256,128]{2,1,0:T(8,128)(2,1)S(1)}) custom-call(bf16[144,128]{1,0:T(8,128)(2,1)S(1)} %constant_dynamic-update-slice_fusion.packed_ref, bf16[32,256,128]{2,1,0:T(8,128)(2,1)S(1)} %get-tuple-element.12.gallery_ref.refs_0_, bf16[80,256,128]{2,1,0:T(8,128)(2,1)} %gallery_hbm.5), custom_call_target="tpu_custom_call" | custom-call | flops 268435456 | bytes 2097152 | tf_op jit(solution)/shard_map/pallas_call | solution.py:336
  14.2 0.0 collective-permute-done.3.packed_ref
  14.2 1.9 %shard_map.49 = f32[2,1,16,128]{3,2,1,0:T(8,128)S(1)} custom-call(bf16[144,128]{1,0:T(8,128)(2,1)S(1)} %collective-permute-done.3.packed_ref, bf16[32,256,128]{2,1,0:T(8,128)(2,1)S(1)} %get-tuple-element.12.gallery_ref.refs_0_, bf16[32,256,128]{2,1,0:T(8,128)(2,1)S(1)} %shard_map.47.refs_0_.refs_1_, bf16[16,256,128]{2,1,0:T(8,128)(2,1)S(1)} %get-tuple-element.14.refs_1_.refs_2_), custom_call_target="tpu_custom_call" | custom-call | flops 671088640 | bytes 5242880 | tf_op jit(solution)/shard_map/pallas_call | solution.py:347
  16.1 0.7 %collective-permute-start.4 = (f32[2,1,16,128]{3,2,1,0:T(8,128)S(1)}, f32[2,1,16,128]{3,2,1,0:T(8,128)S(1)}, u32[]{:S(2)}, u32[]{:S(2)}) collective-permute-start(f32[2,1,16,128]{3,2,1,0:T(8,128)S(1)} %shard_map.49), channel_id=1, source_target_pairs={{0,5},{1,4},{2,7},{3,6},{4,1},{5,0},{6,3},{7,2},{8,13},{9,12},{10,... | collective-permute-start | bytes 49160 | tf_op jit(solution)/shard_map/ppermute | solution.py:277
  16.8 1.3 %shard_map.48 = f32[2,1,16,128]{3,2,1,0:T(8,128)S(1)} custom-call(bf16[144,128]{1,0:T(8,128)(2,1)S(1)} %constant_dynamic-update-slice_fusion.packed_ref, f32[32,128]{1,0:T(8,128)S(1)} %get-tuple-element.13.first_ref, bf16[32,256,128]{2,1,0:T(8,128)(2,1)S(1)} %shard_map.47.refs_0_.refs_1_, bf16[16,256,128]{2,1,0:T(8,128)(2,1)S(1)} %get-tuple-element.14.refs_1_.refs_2_), custom_call_target="tpu_custom_call" | custom-call | flops 402653184 | bytes 3145728 | tf_op jit(solution)/shard_map/pallas_call | solution.py:355
  18.1 1.2 %collective-permute-done.4 = f32[2,1,16,128]{3,2,1,0:T(8,128)S(1)} collective-permute-done((f32[2,1,16,128]{3,2,1,0:T(8,128)S(1)}, f32[2,1,16,128]{3,2,1,0:T(8,128)S(1)}, u32[]{:S(2)}, u32[]{:S(2)}) %collective-permute-start.4) | collective-permute-done | bytes 16416 | tf_op jit(solution)/shard_map/ppermute | solution.py:277
  19.4 2.5 %collective-permute-start.5 = (f32[1,1,16,128]{3,2,1,0:T(8,128)S(1)}, f32[1,1,16,128]{3,2,1,0:T(8,128)S(1)}, u32[]{:S(2)}, u32[]{:S(2)}) collective-permute-start(f32[1,1,16,128]{3,2,1,0:T(8,128)S(1)} %slice.19), channel_id=1, source_target_pairs={{0,9},{1,8},{2,11},{3,10},{4,13},{5,12},{6,15},{7,14},{8,1},{9,0},... | collective-permute-start | bytes 24584 | tf_op jit(solution)/shard_map/ppermute | solution.py:277
  21.9 1.4 %collective-permute-done.5 = f32[1,1,16,128]{3,2,1,0:T(8,128)S(1)} collective-permute-done((f32[1,1,16,128]{3,2,1,0:T(8,128)S(1)}, f32[1,1,16,128]{3,2,1,0:T(8,128)S(1)}, u32[]{:S(2)}, u32[]{:S(2)}) %collective-permute-start.5) | collective-permute-done | bytes 8224 | tf_op jit(solution)/shard_map/ppermute | solution.py:277
  23.3 1.5 %collective-permute-start.6 = (f32[1,16,128]{2,1,0:T(8,128)S(1)}, f32[1,16,128]{2,1,0:T(8,128)S(1)}, u32[]{:S(2)}, u32[]{:S(2)}) collective-permute-start(f32[1,16,128]{2,1,0:T(8,128)S(1)} %fusion), channel_id=1, source_target_pairs={{0,3},{1,2},{2,1},{3,0},{4,7},{5,6},{6,5},{7,4},{8,11},{9,10},{10,... | collective-permute-start | bytes 24584 | tf_op jit(solution)/shard_map/ppermute | solution.py:277
  24.8 1.6 %collective-permute-done.6 = f32[1,16,128]{2,1,0:T(8,128)S(1)} collective-permute-done((f32[1,16,128]{2,1,0:T(8,128)S(1)}, f32[1,16,128]{2,1,0:T(8,128)S(1)}, u32[]{:S(2)}, u32[]{:S(2)}) %collective-permute-start.6) | collective-permute-done | bytes 8224 | tf_op jit(solution)/shard_map/ppermute | solution.py:277
  26.4 0.4 %collective-permute-start.7 = (f32[1,16,128]{2,1,0:T(8,128)S(1)}, f32[1,16,128]{2,1,0:T(8,128)S(1)}, u32[]{:S(2)}, u32[]{:S(2)}) collective-permute-start(f32[1,16,128]{2,1,0:T(8,128)S(1)} %max.11.mine_ref), channel_id=1, source_target_pairs={{0,1},{1,0},{2,3},{3,2},{4,5},{5,4},{6,7},{7,6},{8,9},{9,8},{10,11... | collective-permute-start | bytes 24584 | tf_op jit(solution)/shard_map/ppermute | solution.py:277
  26.8 0.8 %collective-permute-done.7.other_ref = f32[1,16,128]{2,1,0:T(8,128)S(1)} collective-permute-done((f32[1,16,128]{2,1,0:T(8,128)S(1)}, f32[1,16,128]{2,1,0:T(8,128)S(1)}, u32[]{:S(2)}, u32[]{:S(2)}) %collective-permute-start.7) | collective-permute-done | bytes 8224 | tf_op jit(solution)/shard_map/ppermute | solution.py:277
  27.6 0.7 %finish.1 = f32[2,32]{1,0:T(2,128)} custom-call(f32[1,16,128]{2,1,0:T(8,128)S(1)} %max.11.mine_ref, f32[1,16,128]{2,1,0:T(8,128)S(1)} %collective-permute-done.7.other_ref), custom_call_target="tpu_custom_call" | custom-call | tf_op jit(solution)/shard_map/finish/pallas_call | solution.py:373
  (12 shorter events, 0.1 us)
Async XLA Ops:
  0.0 4.1 %collective-permute-start = (bf16[16,128]{1,0:T(8,128)(2,1)}, bf16[16,128]{1,0:T(8,128)(2,1)S(1)}, u32[]{:S(2)}, u32[]{:S(2)}) collective-permute-start(bf16[16,128]{1,0:T(8,128)(2,1)} %bitcast.7), channel_id=1, source_target_pairs={{0,3},{1,2},{2,1},{3,0},{4,7},{5,6},{6,5},{7,4},{8,11},{9,10},{10,... | collective-permute-start | bytes 12296 | tf_op jit(solution)/shard_map/ppermute | solution.py:277
  4.1 4.3 %collective-permute-start.1 = (bf16[40,128]{1,0:T(8,128)(2,1)S(1)}, bf16[40,128]{1,0:T(8,128)(2,1)S(1)}, u32[]{:S(2)}, u32[]{:S(2)}) collective-permute-start(bf16[40,128]{1,0:T(8,128)(2,1)S(1)} %pad_maximum_fusion.1), channel_id=1, source_target_pairs={{0,9},{1,8},{2,11},{3,10},{4,13},{5,12},{6,15},{7,14},{8,1},{9,0},... | collective-permute-start | bytes 30728 | tf_op jit(solution)/shard_map/ppermute | solution.py:277
  8.5 1.3 %collective-permute-start.2 = (bf16[64,128]{1,0:T(8,128)(2,1)S(1)}, bf16[64,128]{1,0:T(8,128)(2,1)S(1)}, u32[]{:S(2)}, u32[]{:S(2)}) collective-permute-start(bf16[64,128]{1,0:T(8,128)(2,1)S(1)} %pad_maximum_fusion), channel_id=1, source_target_pairs={{0,1},{1,0},{2,3},{3,2},{4,5},{5,4},{6,7},{7,6},{8,9},{9,8},{10,11... | collective-permute-start | bytes 49160 | tf_op jit(solution)/shard_map/ppermute | solution.py:277
  9.8 4.4 %collective-permute-start.3 = (bf16[144,128]{1,0:T(8,128)(2,1)S(1)}, bf16[144,128]{1,0:T(8,128)(2,1)S(1)}, u32[]{:S(2)}, u32[]{:S(2)}) collective-permute-start(bf16[144,128]{1,0:T(8,128)(2,1)S(1)} %constant_dynamic-update-slice_fusion.packed_ref), channel_id=1, source_target_pairs={{0,5},{1,4},{2,7},{3,6},{4,1},{5,0},{6,3},{7,2},{8,13},{9,12},{10,... | collective-permute-start | bytes 110600 | tf_op jit(solution)/shard_map/ppermute | solution.py:277
  16.1 3.2 %collective-permute-start.4 = (f32[2,1,16,128]{3,2,1,0:T(8,128)S(1)}, f32[2,1,16,128]{3,2,1,0:T(8,128)S(1)}, u32[]{:S(2)}, u32[]{:S(2)}) collective-permute-start(f32[2,1,16,128]{3,2,1,0:T(8,128)S(1)} %shard_map.49), channel_id=1, source_target_pairs={{0,5},{1,4},{2,7},{3,6},{4,1},{5,0},{6,3},{7,2},{8,13},{9,12},{10,... | collective-permute-start | bytes 49160 | tf_op jit(solution)/shard_map/ppermute | solution.py:277
  19.4 4.0 %collective-permute-start.5 = (f32[1,1,16,128]{3,2,1,0:T(8,128)S(1)}, f32[1,1,16,128]{3,2,1,0:T(8,128)S(1)}, u32[]{:S(2)}, u32[]{:S(2)}) collective-permute-start(f32[1,1,16,128]{3,2,1,0:T(8,128)S(1)} %slice.19), channel_id=1, source_target_pairs={{0,9},{1,8},{2,11},{3,10},{4,13},{5,12},{6,15},{7,14},{8,1},{9,0},... | collective-permute-start | bytes 24584 | tf_op jit(solution)/shard_map/ppermute | solution.py:277
  23.3 3.1 %collective-permute-start.6 = (f32[1,16,128]{2,1,0:T(8,128)S(1)}, f32[1,16,128]{2,1,0:T(8,128)S(1)}, u32[]{:S(2)}, u32[]{:S(2)}) collective-permute-start(f32[1,16,128]{2,1,0:T(8,128)S(1)} %fusion), channel_id=1, source_target_pairs={{0,3},{1,2},{2,1},{3,0},{4,7},{5,6},{6,5},{7,4},{8,11},{9,10},{10,... | collective-permute-start | bytes 24584 | tf_op jit(solution)/shard_map/ppermute | solution.py:277
  26.4 1.2 %collective-permute-start.7 = (f32[1,16,128]{2,1,0:T(8,128)S(1)}, f32[1,16,128]{2,1,0:T(8,128)S(1)}, u32[]{:S(2)}, u32[]{:S(2)}) collective-permute-start(f32[1,16,128]{2,1,0:T(8,128)S(1)} %max.11.mine_ref), channel_id=1, source_target_pairs={{0,1},{1,0},{2,3},{3,2},{4,5},{5,4},{6,7},{7,6},{8,9},{9,8},{10,11... | collective-permute-start | bytes 24584 | tf_op jit(solution)/shard_map/ppermute | solution.py:277
